TPU v7x, 32 devices: a whole 2x2x4 slice. The times are simulated.
32 devices in a mesh: grp: 2 (over x), tok: 16 (over z, y, core).
Axes of the slice: x: 2, y: 2, z: 4, core: 2. Of those that a mesh axis runs over, the one named last changes fastest.
Arguments:
- tokens: bfloat16 [4096, 2048], P(('grp', 'tok')), parts along dimension 0, may hold values from -6 to 6
- norm_gain: float32 [2048], replicated, may hold values from 0.1 to 1.9
- expert_ids: int32 [4096, 8], P(('grp', 'tok')), parts along dimension 0, may hold values from 0 to 15, as said below
- gate_weights: float32 [4096, 8], P(('grp', 'tok')), parts along dimension 0, may hold values from 0.05 to 1
- owner_map: int32 [16], replicated, may hold values from 0 to 15, each once
- in_q: bfloat16 [16, 2, 2048, 768], P('tok'), may hold values from -0.125 to 0.125
- in_scale: bfloat16 [16, 2, 768], P('tok'), may hold values from 0.5 to 2
- down_q: bfloat16 [16, 768, 2048], P('tok'), may hold values from -0.21875 to 0.21875
- down_scale: bfloat16 [16, 2048], P('tok'), may hold values from 0.5 to 2
Outputs:
- moe_out: bfloat16 [4096, 2048], P(('grp', 'tok')), parts along dimension 0
There are 2 independent parts, one for each index of `grp`. A program takes and returns all parts, laid end to end along the dimension named above; an argument that names none is the same for every part. Nothing has to cross between parts.
Inputs may be any that keep to these rules, and one draw needn't show every extreme that they name: `expert_ids`: each row names 8 different experts. One and the same expert is named by exactly 96 of the 128 rows of every device; every other expert is named by between 32 and 80 rows of each device, and 80 is reached on every device. `owner_map`: every slot holds exactly one expert.
All inputs are finite; a program needn't handle non-finite values.
Results may differ from a plain program's by a relative error of at most 0.0071.
Values may be sent and summed in bfloat16 or wider, within the bound.
No kernel may reach another device: no remote copies, remote signals or barrier semaphores. Data moves between devices by JAX's collectives and lax.ppermute only.
A program may use at most 128 MiB of HBM per device.

v0:
```python
import functools

import jax
import jax.numpy as jnp
from jax import lax
from jax.experimental import pallas as pl
from jax.experimental.pallas import tpu as pltpu
from jax.sharding import PartitionSpec as P


LANES = 128
TALL = 16
TILE = 256
SMALL = 8 << 20
LARGE = 20 << 20


def expert_rows(batch_rows, in_blocks, in_scales, down_block, down_scales):
    gate_part = jnp.dot(batch_rows, in_blocks[0], preferred_element_type=jnp.float32) * in_scales[0]
    up_part = jnp.dot(batch_rows, in_blocks[1], preferred_element_type=jnp.float32) * in_scales[1]
    hidden = (jax.nn.silu(gate_part) * up_part).astype(jnp.bfloat16)
    return jnp.dot(hidden, down_block, preferred_element_type=jnp.float32) * down_scales


def normalized(tokens, norm_gain):
    values = tokens.astype(jnp.float32)
    row_scale = lax.rsqrt(jnp.mean(values * values, axis=1, keepdims=True) + 1e-06)
    return (values * row_scale * norm_gain).astype(jnp.bfloat16)


def exchanged(
    tokens, norm_gain, expert_ids, gate_weights, owner_map, in_q, in_scale, down_q, down_scale
):
    tok_rows, model_width = tokens.shape
    top_count = expert_ids.shape[1]
    experts = owner_map.shape[0]
    mean_load = tok_rows * top_count // experts
    capacity = mean_load + mean_load // 2
    normed = normalized(tokens, norm_gain)
    weights = gate_weights / jnp.sum(gate_weights, axis=1, keepdims=True)
    labels = jnp.arange(experts, dtype=jnp.int32)
    slot_table = jnp.sum(jnp.where(expert_ids[:, :, None] == labels, owner_map, 0), axis=2)
    flat_slot = slot_table.reshape(-1)
    onehot = (flat_slot[:, None] == labels).astype(jnp.int32)
    slot_rank = jnp.sum((jnp.cumsum(onehot, axis=0) - onehot) * onehot, axis=1)
    repeated = jnp.repeat(normed, top_count, axis=0)
    outgoing = (
        jnp.zeros((experts, capacity, model_width), jnp.bfloat16)
        .at[flat_slot, slot_rank]
        .set(repeated)
    )
    received = lax.all_to_all(outgoing, "tok", split_axis=0, concat_axis=0, tiled=True)
    source_count, slot_count, _ = received.shape
    flat_rows = received.reshape(source_count * slot_count, model_width)
    served = expert_rows(flat_rows, in_q[0], in_scale[0], down_q[0], down_scale[0])
    served = served.astype(jnp.bfloat16).reshape(source_count, slot_count, model_width)
    returned_rows = lax.all_to_all(served, "tok", split_axis=0, concat_axis=0, tiled=True)
    picked = returned_rows[flat_slot, slot_rank].reshape(tok_rows, top_count, model_width)
    mixed = jnp.sum(weights[:, :, None] * picked.astype(jnp.float32), axis=1)
    return mixed.astype(jnp.bfloat16)


def ring_pairs(devices):
    chips = devices // 2
    loop = list(range(0, chips, 2)) + list(range(chips - 1, 0, -2))
    pairs = []
    for place, chip in enumerate(loop):
        after = loop[(place + 1) % chips]
        pairs.append((2 * chip, 2 * after))
        pairs.append((2 * after + 1, 2 * chip + 1))
    return pairs, chips


def in_hbm(array):
    return pltpu.with_memory_space_constraint(array, pltpu.HBM)


def packed_kernel(tokens_hbm, gain_hbm, ids_hbm, gates_hbm, *refs):
    *part_refs, tokens, gain, ids, gates, sems = refs
    moves = [
        pltpu.make_async_copy(source, target, sems.at[i])
        for i, (source, target) in enumerate(
            ((ids_hbm, ids), (gates_hbm, gates), (tokens_hbm, tokens), (gain_hbm, gain))
        )
    ]
    for move in moves:
        move.start()
    tok_rows, model_width = tokens.shape
    moves[0].wait()
    moves[1].wait()
    weights = gates[...] / jnp.sum(gates[...], axis=0, keepdims=True)
    experts = (sum(ref.shape[0] for ref in part_refs) - tok_rows * model_width // LANES) // 2
    label = lax.broadcasted_iota(jnp.int32, (experts, tok_rows), 0)
    table = jnp.zeros((experts, tok_rows), jnp.float32)
    for k in range(ids.shape[0]):
        table += jnp.where(label == ids[k : k + 1, :], weights[k : k + 1, :], 0.0)
    high = table.astype(jnp.bfloat16)
    low = (table - high.astype(jnp.float32)).astype(jnp.bfloat16)
    last = part_refs[-1]
    last[-2 * experts : -experts, :] = high
    last[-experts:, :] = low
    moves[2].wait()
    moves[3].wait()
    places = tiles_of(part_refs, tok_rows, model_width)
    for top in range(0, tok_rows, TALL):
        values = tokens[top : top + TALL, :].astype(jnp.float32)
        row_scale = lax.rsqrt(jnp.mean(values * values, axis=1, keepdims=True) + 1e-06)
        normed = (values * row_scale * gain[...]).astype(jnp.bfloat16)
        for side in range(0, model_width, LANES):
            ref, row = places[top, side]
            ref[row : row + TALL, :] = normed[:, side : side + LANES]


def tiles_of(part_refs, tok_rows, model_width):
    tiles = [(top, side) for top in range(0, tok_rows, TALL) for side in range(0, model_width, LANES)]
    places, part, row = {}, 0, 0
    for tile in tiles:
        if row == part_refs[part].shape[0]:
            part, row = part + 1, 0
        places[tile] = part_refs[part], row
        row += TALL
    return places


def packed(tokens, norm_gain, expert_ids, gate_weights, experts):
    tok_rows, model_width = tokens.shape
    top_count = expert_ids.shape[1]
    size = tok_rows * model_width // LANES + 2 * experts
    return pl.pallas_call(
        packed_kernel,
        out_shape=(jax.ShapeDtypeStruct((size, LANES), jnp.bfloat16),),
        in_specs=[pl.BlockSpec(memory_space=pltpu.HBM)] * 4,
        out_specs=(pl.BlockSpec(memory_space=pltpu.VMEM),),
        scratch_shapes=[
            pltpu.VMEM((tok_rows, model_width), jnp.bfloat16),
            pltpu.VMEM((1, model_width), jnp.float32),
            pltpu.VMEM((top_count, tok_rows), jnp.int32),
            pltpu.VMEM((top_count, tok_rows), jnp.float32),
            pltpu.SemaphoreType.DMA((4,)),
        ],
        compiler_params=pltpu.CompilerParams(vmem_limit_bytes=SMALL),
        name="packed",
    )(*map(in_hbm, (tokens, norm_gain[None, :], expert_ids.T, gate_weights.T)))


def loaded_kernel(count, *refs):
    sources, targets, sems = refs[:count], refs[count : 2 * count], refs[-1]
    moves = [
        pltpu.make_async_copy(source, target, sems.at[i])
        for i, (source, target) in enumerate(zip(sources, targets))
    ]
    for move in moves:
        move.start()
    for move in moves:
        move.wait()


def loaded(*arrays):
    count = len(arrays)
    return pl.pallas_call(
        functools.partial(loaded_kernel, count),
        out_shape=tuple(jax.ShapeDtypeStruct(x.shape, x.dtype) for x in arrays),
        in_specs=[pl.BlockSpec(memory_space=pltpu.HBM)] * count,
        out_specs=(pl.BlockSpec(memory_space=pltpu.VMEM),) * count,
        scratch_shapes=[pltpu.SemaphoreType.DMA((count,))],
        compiler_params=pltpu.CompilerParams(vmem_limit_bytes=SMALL),
        cost_estimate=pl.CostEstimate(
            flops=0, bytes_accessed=2 * sum(x.size for x in arrays), transcendentals=0
        ),
        name="loaded",
    )(*map(in_hbm, arrays))


def visit_kernel(counts, owners_ref, *refs):
    near_refs, refs = refs[: counts[0]], refs[counts[0] :]
    far_refs, refs = refs[: counts[1]], refs[counts[1] :]
    in_ref, in_scale_ref, down_ref, down_scale_ref, part_ref, lent_ref, rows_ref, hidden_ref = refs
    tok_rows, model_width = part_ref.shape
    hidden_width = hidden_ref.shape[1]
    for base, block_refs in ((0, near_refs), (tok_rows, far_refs)):
        for (top, side), (ref, row) in tiles_of(block_refs, tok_rows, model_width).items():
            tile = ref[row : row + TALL, :]
            rows_ref[base + top : base + top + TALL, side : side + LANES] = tile
    rows = rows_ref[...]
    for start in range(0, hidden_width, TILE):
        cols = slice(start, start + TILE)
        gate = jnp.dot(rows, in_ref[0, 0, :, cols], preferred_element_type=jnp.float32)
        up = jnp.dot(rows, in_ref[0, 1, :, cols], preferred_element_type=jnp.float32)
        gate = gate * in_scale_ref[0, 0:1, cols].astype(jnp.float32)
        up = up * in_scale_ref[0, 1:2, cols].astype(jnp.float32)
        hidden_ref[:, cols] = (gate / (1.0 + jnp.exp(-gate)) * up).astype(jnp.bfloat16)
    experts = owners_ref.shape[1]
    lane = lax.broadcasted_iota(jnp.int32, owners_ref.shape, 1)
    here = owners_ref[...] == lax.axis_index("tok")
    mine = jnp.sum(jnp.where(here, lane, 0), axis=1, keepdims=True)
    label = lax.broadcasted_iota(jnp.int32, (2 * experts, tok_rows), 0)
    chosen = (label == mine) | (label == mine + experts)
    square = (tok_rows, tok_rows)
    same = lax.broadcasted_iota(jnp.int32, square, 0) == lax.broadcasted_iota(jnp.int32, square, 1)

    def share_of(block_refs):
        table = block_refs[-1][-2 * experts :, :].astype(jnp.float32)
        along = jnp.sum(jnp.where(chosen, table, 0.0), axis=0, keepdims=True)
        return jnp.sum(jnp.where(same, along, 0.0), axis=1, keepdims=True)

    near_share, far_share = share_of(near_refs), share_of(far_refs)
    hidden = hidden_ref[...]
    for start in range(0, model_width, TILE):
        cols = slice(start, start + TILE)
        out = jnp.dot(hidden, down_ref[0, :, cols], preferred_element_type=jnp.float32)
        out = out * down_scale_ref[:, cols].astype(jnp.float32)
        part_ref[:, cols] = out[:tok_rows] * near_share
        lent_ref[:, cols] = (out[tok_rows:] * far_share).astype(jnp.bfloat16)


def visit(near, far, owners, in_q, in_scale, down_q, down_scale):
    hidden_width, model_width = down_q.shape[1:]
    tok_rows = (sum(x.shape[0] for x in near) - 2 * owners.shape[1]) * LANES // model_width
    flops = 2 * 2 * tok_rows * 3 * hidden_width * model_width
    operands = (owners, *near, *far, in_q, in_scale, down_q, down_scale)
    return pl.pallas_call(
        functools.partial(visit_kernel, (len(near), len(far))),
        out_shape=(
            jax.ShapeDtypeStruct((tok_rows, model_width), jnp.float32),
            jax.ShapeDtypeStruct((tok_rows, model_width), jnp.bfloat16),
        ),
        in_specs=[pl.BlockSpec(memory_space=pltpu.VMEM)] * len(operands),
        out_specs=(pl.BlockSpec(memory_space=pltpu.VMEM),) * 2,
        scratch_shapes=[
            pltpu.VMEM((2 * tok_rows, model_width), jnp.bfloat16),
            pltpu.VMEM((2 * tok_rows, hidden_width), jnp.bfloat16),
        ],
        compiler_params=pltpu.CompilerParams(vmem_limit_bytes=LARGE),
        cost_estimate=pl.CostEstimate(
            flops=flops, bytes_accessed=6 * tok_rows * model_width, transcendentals=0
        ),
        name="visit",
    )(*operands)


def circulated(
    tokens, norm_gain, expert_ids, gate_weights, owner_map, in_q, in_scale, down_q, down_scale
):
    experts = owner_map.shape[0]
    devices = lax.axis_size("tok")
    ring, chips = ring_pairs(devices)
    swap = [(i, i ^ 1) for i in range(devices)]

    def moved(value, pairs):
        return lax.ppermute(value, "tok", pairs)

    (block,) = packed(tokens, norm_gain, expert_ids, gate_weights, experts)
    blocks = loaded(owner_map[None, :], in_q, in_scale, down_q, down_scale)
    back = moved(block, [(target, source) for source, target in ring])
    parts = []
    for step in range(chips):
        here = block if step < chips - 1 else back
        other = moved(here, swap)
        if step < chips - 2:
            block = moved(block, ring)
        part, lent = visit((here,), (other,), *blocks)
        parts.append((part, moved(lent, swap)))

    def summed(step, rows, arrived):
        part, lent = (x[rows].astype(jnp.float32) for x in parts[step])
        return (part + lent + arrived.astype(jnp.float32)).astype(jnp.bfloat16)

    total = jnp.zeros((), jnp.bfloat16)
    for step in range(1, chips - 2):
        total = lax.ppermute(summed(step, slice(None), total), "tok", ring)
    shares = shares_of(tokens.shape[0])
    totals = {name: total[rows] for name, rows in shares.items()}
    for step in range(chips - 2, chips):
        for name, rows in shares.items():
            totals[name] = lax.ppermute(summed(step, rows, totals[name]), "tok", ring)
    out = []
    for name, rows in shares.items():
        out.append(summed(0, rows, totals[name]))
    return jnp.concatenate(out)


def shares_of(tok_rows):
    one, two = tok_rows // 16 * 6, tok_rows // 16 * 9
    return {"a": slice(0, one), "b": slice(one, two), "c": slice(two, tok_rows)}


def solution(mesh):
    devices = mesh.shape["tok"]
    row = P(("grp", "tok"), None)
    slot = [P("tok", *(None,) * extra) for extra in (3, 2, 2, 1)]

    def placed(body):
        return jax.shard_map(
            body,
            mesh=mesh,
            in_specs=(row, P(), row, row, P(), *slot),
            out_specs=row,
            check_vma=False,
        )

    def step(tokens, norm_gain, expert_ids, gate_weights, owner_map, *blocks):
        tok_rows = tokens.shape[0] // mesh.size
        experts = owner_map.shape[0]
        mean_load = tok_rows * expert_ids.shape[1] // experts
        routed = experts * (mean_load + mean_load // 2)
        arguments = (tokens, norm_gain, expert_ids, gate_weights, owner_map, *blocks)
        if tok_rows * devices > 2 * routed or devices < 16 or devices % 4 or tok_rows != LANES:
            return placed(exchanged)(*arguments)
        return placed(circulated)(*arguments)

    return step
```

profile of v0, /device:TPU:0, one launch (start us, length us, event | category | flops | bytes accessed | tf_op | source)
XLA Modules:
  0.0 109.2 jit_solution(1413150911609435648)
XLA Ops:
  0.0 1.3 %packed.1.refs_0_ = bf16[2080,128]{1,0:T(8,128)(2,1)S(1)} custom-call(bf16[128,2048]{1,0:T(8,128)(2,1)} %tokens_hbm.1, f32[1,2048]{1,0:T(1,128)} %bitcast.4, s32[8,128]{1,0:T(8,128)} %bitcast.5, f32[8,128]{1,0:T(8,128)} %bitcast.6), custom_call_target="tpu_custom_call" | custom-call | tf_op jit(solution)/shard_map/packed/pallas_call | solution.py:129
  1.3 3.1 %collective-permute-start.5 = (bf16[2080,128]{1,0:T(8,128)(2,1)S(1)}, bf16[2080,128]{1,0:T(8,128)(2,1)S(1)}, u32[]{:S(2)}, u32[]{:S(2)}) collective-permute-start(bf16[2080,128]{1,0:T(8,128)(2,1)S(1)} %packed.1.refs_0_), channel_id=1, source_target_pairs={{0,4},{5,1},{4,8},{9,5},{8,12},{13,9},{12,14},{15,13},{14,10},{11,... | collective-permute-start | bytes 1597448 | tf_op jit(solution)/shard_map/ppermute | solution.py:250
  4.4 7.2 %collective-permute-done.5.refs_0_ = bf16[2080,128]{1,0:T(8,128)(2,1)S(1)} collective-permute-done((bf16[2080,128]{1,0:T(8,128)(2,1)S(1)}, bf16[2080,128]{1,0:T(8,128)(2,1)S(1)}, u32[]{:S(2)}, u32[]{:S(2)}) %collective-permute-start.5) | collective-permute-done | bytes 532512 | tf_op jit(solution)/shard_map/ppermute | solution.py:250
  11.6 3.8 %loaded.1 = (s32[1,16]{1,0:T(1,128)S(1)}, bf16[1,2,2048,768]{3,2,1,0:T(8,128)(2,1)S(1)}, bf16[1,2,768]{2,1,0:T(2,128)(2,1)S(1)}, bf16[1,768,2048]{2,1,0:T(8,128)(2,1)S(1)}, bf16[1,2048]{1,0:T(2,128)(2,1)S(1)}) custom-call(s32[1,16]{1,0:T(1,128)} %bitcast.7, bf16[1,2,2048,768]{3,2,1,0:T(8,128)(2,1)} %refs_1_.1, bf16[1,2,768]{2,1,0:T(2,128)(2,1)} %refs_2_.1, ...), custom_call_target="tpu_custom_call" | custom-call | bytes 9444384 | tf_op jit(solution)/shard_map/loaded/pallas_call | solution.py:160
  15.4 2.1 %collective-permute-start.6 = (bf16[2080,128]{1,0:T(8,128)(2,1)S(1)}, bf16[2080,128]{1,0:T(8,128)(2,1)S(1)}, u32[]{:S(2)}, u32[]{:S(2)}) collective-permute-start(bf16[2080,128]{1,0:T(8,128)(2,1)S(1)} %collective-permute-done.5.refs_0_), channel_id=1, source_target_pairs={{0,4},{5,1},{4,8},{9,5},{8,12},{13,9},{12,14},{15,13},{14,10},{11,... | collective-permute-start | bytes 1597448 | tf_op jit(solution)/shard_map/ppermute | solution.py:250
  17.6 2.7 %visit.15 = (f32[128,2048]{1,0:T(8,128)S(1)}, bf16[128,2048]{1,0:T(8,128)(2,1)S(1)}) custom-call(s32[1,16]{1,0:T(1,128)S(1)} %get-tuple-element.26.owners_ref, bf16[2080,128]{1,0:T(8,128)(2,1)S(1)} %collective-permute-done.5.refs_0_, bf16[2080,128]{1,0:T(8,128)(2,1)S(1)} %collective-permute-done.21.refs_1_, ...), custom_call_target="tpu_custom_call" | custom-call | flops 2415919104 | bytes 1572864 | tf_op jit(solution)/shard_map/visit/pallas_call | solution.py:221
  20.2 0.2 collective-permute-start.22
  20.5 4.3 %collective-permute-done.6.refs_0_ = bf16[2080,128]{1,0:T(8,128)(2,1)S(1)} collective-permute-done((bf16[2080,128]{1,0:T(8,128)(2,1)S(1)}, bf16[2080,128]{1,0:T(8,128)(2,1)S(1)}, u32[]{:S(2)}, u32[]{:S(2)}) %collective-permute-start.6) | collective-permute-done | bytes 532512 | tf_op jit(solution)/shard_map/ppermute | solution.py:250
  24.7 2.1 %collective-permute-start.7 = (bf16[2080,128]{1,0:T(8,128)(2,1)S(1)}, bf16[2080,128]{1,0:T(8,128)(2,1)S(1)}, u32[]{:S(2)}, u32[]{:S(2)}) collective-permute-start(bf16[2080,128]{1,0:T(8,128)(2,1)S(1)} %collective-permute-done.6.refs_0_), channel_id=1, source_target_pairs={{0,4},{5,1},{4,8},{9,5},{8,12},{13,9},{12,14},{15,13},{14,10},{11,... | collective-permute-start | bytes 1597448 | tf_op jit(solution)/shard_map/ppermute | solution.py:250
  26.8 0.1 add_convert_fusion.4
  27.0 1.6 %collective-permute-start.23 = (bf16[128,2048]{1,0:T(8,128)(2,1)S(1)}, bf16[128,2048]{1,0:T(8,128)(2,1)S(1)}, u32[]{:S(2)}, u32[]{:S(2)}) collective-permute-start(bf16[128,2048]{1,0:T(8,128)(2,1)S(1)} %add_convert_fusion.4), channel_id=1, source_target_pairs={{0,4},{5,1},{4,8},{9,5},{8,12},{13,9},{12,14},{15,13},{14,10},{11,... | collective-permute-start | bytes 1572872 | tf_op jit(solution)/shard_map/ppermute | solution.py:270
  28.6 2.7 %visit.14 = (f32[128,2048]{1,0:T(8,128)S(1)}, bf16[128,2048]{1,0:T(8,128)(2,1)S(1)}) custom-call(s32[1,16]{1,0:T(1,128)S(1)} %get-tuple-element.26.owners_ref, bf16[2080,128]{1,0:T(8,128)(2,1)S(1)} %collective-permute-done.6.refs_0_, bf16[2080,128]{1,0:T(8,128)(2,1)S(1)} %collective-permute-done.19.refs_1_, ...), custom_call_target="tpu_custom_call" | custom-call | flops 2415919104 | bytes 1572864 | tf_op jit(solution)/shard_map/visit/pallas_call | solution.py:221
  31.3 0.1 collective-permute-start.20
  31.4 2.7 %collective-permute-done.7.refs_0_ = bf16[2080,128]{1,0:T(8,128)(2,1)S(1)} collective-permute-done((bf16[2080,128]{1,0:T(8,128)(2,1)S(1)}, bf16[2080,128]{1,0:T(8,128)(2,1)S(1)}, u32[]{:S(2)}, u32[]{:S(2)}) %collective-permute-start.7) | collective-permute-done | bytes 532512 | tf_op jit(solution)/shard_map/ppermute | solution.py:250
  34.0 2.1 %collective-permute-start.8 = (bf16[2080,128]{1,0:T(8,128)(2,1)S(1)}, bf16[2080,128]{1,0:T(8,128)(2,1)S(1)}, u32[]{:S(2)}, u32[]{:S(2)}) collective-permute-start(bf16[2080,128]{1,0:T(8,128)(2,1)S(1)} %collective-permute-done.7.refs_0_), channel_id=1, source_target_pairs={{0,4},{5,1},{4,8},{9,5},{8,12},{13,9},{12,14},{15,13},{14,10},{11,... | collective-permute-start | bytes 1597448 | tf_op jit(solution)/shard_map/ppermute | solution.py:250
  36.1 3.5 %collective-permute-done.23 = bf16[128,2048]{1,0:T(8,128)(2,1)S(1)} collective-permute-done((bf16[128,2048]{1,0:T(8,128)(2,1)S(1)}, bf16[128,2048]{1,0:T(8,128)(2,1)S(1)}, u32[]{:S(2)}, u32[]{:S(2)}) %collective-permute-start.23) | collective-permute-done | bytes 524320 | tf_op jit(solution)/shard_map/ppermute | solution.py:270
  39.6 0.2 add_convert_fusion.3
  39.9 2.1 %collective-permute-start.24 = (bf16[128,2048]{1,0:T(8,128)(2,1)S(1)}, bf16[128,2048]{1,0:T(8,128)(2,1)S(1)}, u32[]{:S(2)}, u32[]{:S(2)}) collective-permute-start(bf16[128,2048]{1,0:T(8,128)(2,1)S(1)} %add_convert_fusion.3), channel_id=1, source_target_pairs={{0,4},{5,1},{4,8},{9,5},{8,12},{13,9},{12,14},{15,13},{14,10},{11,... | collective-permute-start | bytes 1572872 | tf_op jit(solution)/shard_map/ppermute | solution.py:270
  42.0 2.7 %visit.13 = (f32[128,2048]{1,0:T(8,128)S(1)}, bf16[128,2048]{1,0:T(8,128)(2,1)S(1)}) custom-call(s32[1,16]{1,0:T(1,128)S(1)} %get-tuple-element.26.owners_ref, bf16[2080,128]{1,0:T(8,128)(2,1)S(1)} %collective-permute-done.7.refs_0_, bf16[2080,128]{1,0:T(8,128)(2,1)S(1)} %collective-permute-done.17.refs_1_, ...), custom_call_target="tpu_custom_call" | custom-call | flops 2415919104 | bytes 1572864 | tf_op jit(solution)/shard_map/visit/pallas_call | solution.py:221
  44.7 0.1 collective-permute-start.18
  44.7 0.6 collective-permute-done.8.refs_0_
  45.3 2.1 %collective-permute-start.9 = (bf16[2080,128]{1,0:T(8,128)(2,1)S(1)}, bf16[2080,128]{1,0:T(8,128)(2,1)S(1)}, u32[]{:S(2)}, u32[]{:S(2)}) collective-permute-start(bf16[2080,128]{1,0:T(8,128)(2,1)S(1)} %collective-permute-done.8.refs_0_), channel_id=1, source_target_pairs={{0,4},{5,1},{4,8},{9,5},{8,12},{13,9},{12,14},{15,13},{14,10},{11,... | collective-permute-start | bytes 1597448 | tf_op jit(solution)/shard_map/ppermute | solution.py:250
  47.4 3.5 %collective-permute-done.24 = bf16[128,2048]{1,0:T(8,128)(2,1)S(1)} collective-permute-done((bf16[128,2048]{1,0:T(8,128)(2,1)S(1)}, bf16[128,2048]{1,0:T(8,128)(2,1)S(1)}, u32[]{:S(2)}, u32[]{:S(2)}) %collective-permute-start.24) | collective-permute-done | bytes 524320 | tf_op jit(solution)/shard_map/ppermute | solution.py:270
  51.0 0.2 add_convert_fusion.2
  51.2 2.1 %collective-permute-start.25 = (bf16[128,2048]{1,0:T(8,128)(2,1)S(1)}, bf16[128,2048]{1,0:T(8,128)(2,1)S(1)}, u32[]{:S(2)}, u32[]{:S(2)}) collective-permute-start(bf16[128,2048]{1,0:T(8,128)(2,1)S(1)} %add_convert_fusion.2), channel_id=1, source_target_pairs={{0,4},{5,1},{4,8},{9,5},{8,12},{13,9},{12,14},{15,13},{14,10},{11,... | collective-permute-start | bytes 1572872 | tf_op jit(solution)/shard_map/ppermute | solution.py:270
  53.3 2.7 %visit.12 = (f32[128,2048]{1,0:T(8,128)S(1)}, bf16[128,2048]{1,0:T(8,128)(2,1)S(1)}) custom-call(s32[1,16]{1,0:T(1,128)S(1)} %get-tuple-element.26.owners_ref, bf16[2080,128]{1,0:T(8,128)(2,1)S(1)} %collective-permute-done.8.refs_0_, bf16[2080,128]{1,0:T(8,128)(2,1)S(1)} %collective-permute-done.15.refs_1_, ...), custom_call_target="tpu_custom_call" | custom-call | flops 2415919104 | bytes 1572864 | tf_op jit(solution)/shard_map/visit/pallas_call | solution.py:221
  56.0 0.1 collective-permute-start.16
  56.1 0.6 collective-permute-done.9.refs_0_
  56.7 2.0 %collective-permute-start.2 = (bf16[2080,128]{1,0:T(8,128)(2,1)S(1)}, bf16[2080,128]{1,0:T(8,128)(2,1)S(1)}, u32[]{:S(2)}, u32[]{:S(2)}) collective-permute-start(bf16[2080,128]{1,0:T(8,128)(2,1)S(1)} %packed.1.refs_0_), channel_id=1, source_target_pairs={{4,0},{1,5},{8,4},{5,9},{12,8},{9,13},{14,12},{13,15},{10,14},{15,... | collective-permute-start | bytes 1597448 | tf_op jit(solution)/shard_map/ppermute | solution.py:250
  58.7 0.1 collective-permute-start.10
  58.7 5.8 %collective-permute-done.25 = bf16[128,2048]{1,0:T(8,128)(2,1)S(1)} collective-permute-done((bf16[128,2048]{1,0:T(8,128)(2,1)S(1)}, bf16[128,2048]{1,0:T(8,128)(2,1)S(1)}, u32[]{:S(2)}, u32[]{:S(2)}) %collective-permute-start.25) | collective-permute-done | bytes 524320 | tf_op jit(solution)/shard_map/ppermute | solution.py:270
  64.5 0.2 add_convert_fusion.1
  64.7 2.6 %collective-permute-start.26 = (bf16[128,2048]{1,0:T(8,128)(2,1)S(1)}, bf16[128,2048]{1,0:T(8,128)(2,1)S(1)}, u32[]{:S(2)}, u32[]{:S(2)}) collective-permute-start(bf16[128,2048]{1,0:T(8,128)(2,1)S(1)} %add_convert_fusion.1), channel_id=1, source_target_pairs={{0,4},{5,1},{4,8},{9,5},{8,12},{13,9},{12,14},{15,13},{14,10},{11,... | collective-permute-start | bytes 1572872 | tf_op jit(solution)/shard_map/ppermute | solution.py:270
  67.3 2.7 %visit.11 = (f32[128,2048]{1,0:T(8,128)S(1)}, bf16[128,2048]{1,0:T(8,128)(2,1)S(1)}) custom-call(s32[1,16]{1,0:T(1,128)S(1)} %get-tuple-element.26.owners_ref, bf16[2080,128]{1,0:T(8,128)(2,1)S(1)} %collective-permute-done.9.refs_0_, bf16[2080,128]{1,0:T(8,128)(2,1)S(1)} %collective-permute-done.13.refs_1_, ...), custom_call_target="tpu_custom_call" | custom-call | flops 2415919104 | bytes 1572864 | tf_op jit(solution)/shard_map/visit/pallas_call | solution.py:221
  70.0 0.1 collective-permute-start.14
  70.1 3.6 %collective-permute-done.10.refs_0_ = bf16[2080,128]{1,0:T(8,128)(2,1)S(1)} collective-permute-done((bf16[2080,128]{1,0:T(8,128)(2,1)S(1)}, bf16[2080,128]{1,0:T(8,128)(2,1)S(1)}, u32[]{:S(2)}, u32[]{:S(2)}) %collective-permute-start.10) | collective-permute-done | bytes 532512 | tf_op jit(solution)/shard_map/ppermute | solution.py:250
  73.7 0.5 collective-permute-start
  74.2 0.0 collective-permute-start.3
  74.2 5.1 %collective-permute-done.26 = bf16[128,2048]{1,0:T(8,128)(2,1)S(1)} collective-permute-done((bf16[128,2048]{1,0:T(8,128)(2,1)S(1)}, bf16[128,2048]{1,0:T(8,128)(2,1)S(1)}, u32[]{:S(2)}, u32[]{:S(2)}) %collective-permute-start.26) | collective-permute-done | bytes 524320 | tf_op jit(solution)/shard_map/ppermute | solution.py:270
  79.3 0.2 add_convert_fusion
  79.5 2.1 %collective-permute-start.27 = (bf16[128,2048]{1,0:T(8,128)(2,1)S(1)}, bf16[128,2048]{1,0:T(8,128)(2,1)S(1)}, u32[]{:S(2)}, u32[]{:S(2)}) collective-permute-start(bf16[128,2048]{1,0:T(8,128)(2,1)S(1)} %add_convert_fusion), channel_id=1, source_target_pairs={{0,4},{5,1},{4,8},{9,5},{8,12},{13,9},{12,14},{15,13},{14,10},{11,... | collective-permute-start | bytes 1572872 | tf_op jit(solution)/shard_map/ppermute | solution.py:270
  81.6 2.7 %visit.10 = (f32[128,2048]{1,0:T(8,128)S(1)}, bf16[128,2048]{1,0:T(8,128)(2,1)S(1)}) custom-call(s32[1,16]{1,0:T(1,128)S(1)} %get-tuple-element.26.owners_ref, bf16[2080,128]{1,0:T(8,128)(2,1)S(1)} %collective-permute-done.10.refs_0_, bf16[2080,128]{1,0:T(8,128)(2,1)S(1)} %collective-permute-done.11.refs_1_, ...), custom_call_target="tpu_custom_call" | custom-call | flops 2415919104 | bytes 1572864 | tf_op jit(solution)/shard_map/visit/pallas_call | solution.py:221
  84.3 0.1 collective-permute-start.12
  84.4 2.7 %visit.8 = (f32[128,2048]{1,0:T(8,128)S(1)}, bf16[128,2048]{1,0:T(8,128)(2,1)S(1)}) custom-call(s32[1,16]{1,0:T(1,128)S(1)} %get-tuple-element.26.owners_ref, bf16[2080,128]{1,0:T(8,128)(2,1)S(1)} %packed.1.refs_0_, bf16[2080,128]{1,0:T(8,128)(2,1)S(1)} %collective-permute-done.refs_1_, bf16[1,2,2048,768]{3,2,1,0:T(8,128)(2,1)S(1)} %get-tuple-element.27.refs_2_, ...), custom_call_target="tpu_custom_call" | custom-call | flops 2415919104 | bytes 1572864 | tf_op jit(solution)/shard_map/visit/pallas_call | solution.py:221
  87.1 0.6 collective-permute-start.1
  87.7 2.7 %visit.9 = (f32[128,2048]{1,0:T(8,128)S(1)}, bf16[128,2048]{1,0:T(8,128)(2,1)S(1)}) custom-call(s32[1,16]{1,0:T(1,128)S(1)} %get-tuple-element.26.owners_ref, bf16[2080,128]{1,0:T(8,128)(2,1)S(1)} %collective-permute-done.2.refs_0_, bf16[2080,128]{1,0:T(8,128)(2,1)S(1)} %collective-permute-done.3.refs_1_, ...), custom_call_target="tpu_custom_call" | custom-call | flops 2415919104 | bytes 1572864 | tf_op jit(solution)/shard_map/visit/pallas_call | solution.py:221
  90.3 0.1 collective-permute-start.4
  90.4 0.1 add_convert_fusion.10
  90.5 1.6 %collective-permute-start.28 = (bf16[48,2048]{1,0:T(8,128)(2,1)S(1)}, bf16[48,2048]{1,0:T(8,128)(2,1)S(1)}, u32[]{:S(2)}, u32[]{:S(2)}) collective-permute-start(bf16[48,2048]{1,0:T(8,128)(2,1)S(1)} %add_convert_fusion.10), channel_id=1, source_target_pairs={{0,4},{5,1},{4,8},{9,5},{8,12},{13,9},{12,14},{15,13},{14,10},{11,... | collective-permute-start | bytes 589832 | tf_op jit(solution)/shard_map/ppermute | solution.py:275
  92.2 1.6 %collective-permute-start.30 = (bf16[24,2048]{1,0:T(8,128)(2,1)S(1)}, bf16[24,2048]{1,0:T(8,128)(2,1)S(1)}, u32[]{:S(2)}, u32[]{:S(2)}) collective-permute-start(bf16[24,2048]{1,0:T(8,128)(2,1)S(1)} %add_convert_fusion.13), channel_id=1, source_target_pairs={{0,4},{5,1},{4,8},{9,5},{8,12},{13,9},{12,14},{15,13},{14,10},{11,... | collective-permute-start | bytes 294920 | tf_op jit(solution)/shard_map/ppermute | solution.py:275
  93.8 0.1 add_convert_fusion.7
  93.9 1.6 %collective-permute-start.32 = (bf16[56,2048]{1,0:T(8,128)(2,1)S(1)}, bf16[56,2048]{1,0:T(8,128)(2,1)S(1)}, u32[]{:S(2)}, u32[]{:S(2)}) collective-permute-start(bf16[56,2048]{1,0:T(8,128)(2,1)S(1)} %add_convert_fusion.7), channel_id=1, source_target_pairs={{0,4},{5,1},{4,8},{9,5},{8,12},{13,9},{12,14},{15,13},{14,10},{11,... | collective-permute-start | bytes 688136 | tf_op jit(solution)/shard_map/ppermute | solution.py:275
  95.5 1.8 %collective-permute-done.30 = bf16[24,2048]{1,0:T(8,128)(2,1)S(1)} collective-permute-done((bf16[24,2048]{1,0:T(8,128)(2,1)S(1)}, bf16[24,2048]{1,0:T(8,128)(2,1)S(1)}, u32[]{:S(2)}, u32[]{:S(2)}) %collective-permute-start.30) | collective-permute-done | bytes 98336 | tf_op jit(solution)/shard_map/ppermute | solution.py:275
  97.3 1.6 %collective-permute-start.31 = (bf16[24,2048]{1,0:T(8,128)(2,1)S(1)}, bf16[24,2048]{1,0:T(8,128)(2,1)S(1)}, u32[]{:S(2)}, u32[]{:S(2)}) collective-permute-start(bf16[24,2048]{1,0:T(8,128)(2,1)S(1)} %add_convert_fusion.12), channel_id=1, source_target_pairs={{0,4},{5,1},{4,8},{9,5},{8,12},{13,9},{12,14},{15,13},{14,10},{11,... | collective-permute-start | bytes 294920 | tf_op jit(solution)/shard_map/ppermute | solution.py:275
  99.0 0.1 add_convert_fusion.9
  99.0 1.6 %collective-permute-start.29 = (bf16[48,2048]{1,0:T(8,128)(2,1)S(1)}, bf16[48,2048]{1,0:T(8,128)(2,1)S(1)}, u32[]{:S(2)}, u32[]{:S(2)}) collective-permute-start(bf16[48,2048]{1,0:T(8,128)(2,1)S(1)} %add_convert_fusion.9), channel_id=1, source_target_pairs={{0,4},{5,1},{4,8},{9,5},{8,12},{13,9},{12,14},{15,13},{14,10},{11,... | collective-permute-start | bytes 589832 | tf_op jit(solution)/shard_map/ppermute | solution.py:275
  100.7 1.3 %collective-permute-done.31 = bf16[24,2048]{1,0:T(8,128)(2,1)S(1)} collective-permute-done((bf16[24,2048]{1,0:T(8,128)(2,1)S(1)}, bf16[24,2048]{1,0:T(8,128)(2,1)S(1)}, u32[]{:S(2)}, u32[]{:S(2)}) %collective-permute-start.31) | collective-permute-done | bytes 98336 | tf_op jit(solution)/shard_map/ppermute | solution.py:275
  102.1 0.1 add_convert_fusion.6
  102.1 1.6 %collective-permute-start.33 = (bf16[56,2048]{1,0:T(8,128)(2,1)S(1)}, bf16[56,2048]{1,0:T(8,128)(2,1)S(1)}, u32[]{:S(2)}, u32[]{:S(2)}) collective-permute-start(bf16[56,2048]{1,0:T(8,128)(2,1)S(1)} %add_convert_fusion.6), channel_id=1, source_target_pairs={{0,4},{5,1},{4,8},{9,5},{8,12},{13,9},{12,14},{15,13},{14,10},{11,... | collective-permute-start | bytes 688136 | tf_op jit(solution)/shard_map/ppermute | solution.py:275
  103.8 1.0 collective-permute-done.29
  104.8 0.1 add_convert_fusion.8
  104.8 3.4 %collective-permute-done.33 = bf16[56,2048]{1,0:T(8,128)(2,1)S(1)} collective-permute-done((bf16[56,2048]{1,0:T(8,128)(2,1)S(1)}, bf16[56,2048]{1,0:T(8,128)(2,1)S(1)}, u32[]{:S(2)}, u32[]{:S(2)}) %collective-permute-start.33) | collective-permute-done | bytes 229408 | tf_op jit(solution)/shard_map/ppermute | solution.py:275
  108.2 0.1 add_convert_fusion.5
  108.3 0.8 pad_maximum_fusion
  (29 shorter events, 0.2 us)
Async XLA Ops:
  1.3 10.3 %collective-permute-start.5 = (bf16[2080,128]{1,0:T(8,128)(2,1)S(1)}, bf16[2080,128]{1,0:T(8,128)(2,1)S(1)}, u32[]{:S(2)}, u32[]{:S(2)}) collective-permute-start(bf16[2080,128]{1,0:T(8,128)(2,1)S(1)} %packed.1.refs_0_), channel_id=1, source_target_pairs={{0,4},{5,1},{4,8},{9,5},{8,12},{13,9},{12,14},{15,13},{14,10},{11,... | collective-permute-start | bytes 1597448 | tf_op jit(solution)/shard_map/ppermute | solution.py:250
  11.6 5.9 %collective-permute-start.21 = (bf16[2080,128]{1,0:T(8,128)(2,1)S(1)}, bf16[2080,128]{1,0:T(8,128)(2,1)S(1)}, u32[]{:S(2)}, u32[]{:S(2)}) collective-permute-start(bf16[2080,128]{1,0:T(8,128)(2,1)S(1)} %collective-permute-done.5.refs_0_), channel_id=1, source_target_pairs={{0,1},{1,0},{2,3},{3,2},{4,5},{5,4},{6,7},{7,6},{8,9},{9,8},{10,11... | collective-permute-start | bytes 1597448 | tf_op jit(solution)/shard_map/ppermute | solution.py:250
  15.4 9.3 %collective-permute-start.6 = (bf16[2080,128]{1,0:T(8,128)(2,1)S(1)}, bf16[2080,128]{1,0:T(8,128)(2,1)S(1)}, u32[]{:S(2)}, u32[]{:S(2)}) collective-permute-start(bf16[2080,128]{1,0:T(8,128)(2,1)S(1)} %collective-permute-done.5.refs_0_), channel_id=1, source_target_pairs={{0,4},{5,1},{4,8},{9,5},{8,12},{13,9},{12,14},{15,13},{14,10},{11,... | collective-permute-start | bytes 1597448 | tf_op jit(solution)/shard_map/ppermute | solution.py:250
  20.2 6.6 %collective-permute-start.22 = (bf16[128,2048]{1,0:T(8,128)(2,1)S(1)}, bf16[128,2048]{1,0:T(8,128)(2,1)S(1)}, u32[]{:S(2)}, u32[]{:S(2)}) collective-permute-start(bf16[128,2048]{1,0:T(8,128)(2,1)S(1)} %get-tuple-element.46), channel_id=1, source_target_pairs={{0,1},{1,0},{2,3},{3,2},{4,5},{5,4},{6,7},{7,6},{8,9},{9,8},{10,11... | collective-permute-start | bytes 1572872 | tf_op jit(solution)/shard_map/ppermute | solution.py:250
  24.7 3.9 %collective-permute-start.19 = (bf16[2080,128]{1,0:T(8,128)(2,1)S(1)}, bf16[2080,128]{1,0:T(8,128)(2,1)S(1)}, u32[]{:S(2)}, u32[]{:S(2)}) collective-permute-start(bf16[2080,128]{1,0:T(8,128)(2,1)S(1)} %collective-permute-done.6.refs_0_), channel_id=1, source_target_pairs={{0,1},{1,0},{2,3},{3,2},{4,5},{5,4},{6,7},{7,6},{8,9},{9,8},{10,11... | collective-permute-start | bytes 1597448 | tf_op jit(solution)/shard_map/ppermute | solution.py:250
  24.7 9.3 %collective-permute-start.7 = (bf16[2080,128]{1,0:T(8,128)(2,1)S(1)}, bf16[2080,128]{1,0:T(8,128)(2,1)S(1)}, u32[]{:S(2)}, u32[]{:S(2)}) collective-permute-start(bf16[2080,128]{1,0:T(8,128)(2,1)S(1)} %collective-permute-done.6.refs_0_), channel_id=1, source_target_pairs={{0,4},{5,1},{4,8},{9,5},{8,12},{13,9},{12,14},{15,13},{14,10},{11,... | collective-permute-start | bytes 1597448 | tf_op jit(solution)/shard_map/ppermute | solution.py:250
  27.0 12.7 %collective-permute-start.23 = (bf16[128,2048]{1,0:T(8,128)(2,1)S(1)}, bf16[128,2048]{1,0:T(8,128)(2,1)S(1)}, u32[]{:S(2)}, u32[]{:S(2)}) collective-permute-start(bf16[128,2048]{1,0:T(8,128)(2,1)S(1)} %add_convert_fusion.4), channel_id=1, source_target_pairs={{0,4},{5,1},{4,8},{9,5},{8,12},{13,9},{12,14},{15,13},{14,10},{11,... | collective-permute-start | bytes 1572872 | tf_op jit(solution)/shard_map/ppermute | solution.py:270
  31.3 8.4 %collective-permute-start.20 = (bf16[128,2048]{1,0:T(8,128)(2,1)S(1)}, bf16[128,2048]{1,0:T(8,128)(2,1)S(1)}, u32[]{:S(2)}, u32[]{:S(2)}) collective-permute-start(bf16[128,2048]{1,0:T(8,128)(2,1)S(1)} %get-tuple-element.44), channel_id=1, source_target_pairs={{0,1},{1,0},{2,3},{3,2},{4,5},{5,4},{6,7},{7,6},{8,9},{9,8},{10,11... | collective-permute-start | bytes 1572872 | tf_op jit(solution)/shard_map/ppermute | solution.py:250
  34.0 8.0 %collective-permute-start.17 = (bf16[2080,128]{1,0:T(8,128)(2,1)S(1)}, bf16[2080,128]{1,0:T(8,128)(2,1)S(1)}, u32[]{:S(2)}, u32[]{:S(2)}) collective-permute-start(bf16[2080,128]{1,0:T(8,128)(2,1)S(1)} %collective-permute-done.7.refs_0_), channel_id=1, source_target_pairs={{0,1},{1,0},{2,3},{3,2},{4,5},{5,4},{6,7},{7,6},{8,9},{9,8},{10,11... | collective-permute-start | bytes 1597448 | tf_op jit(solution)/shard_map/ppermute | solution.py:250
  34.0 11.3 %collective-permute-start.8 = (bf16[2080,128]{1,0:T(8,128)(2,1)S(1)}, bf16[2080,128]{1,0:T(8,128)(2,1)S(1)}, u32[]{:S(2)}, u32[]{:S(2)}) collective-permute-start(bf16[2080,128]{1,0:T(8,128)(2,1)S(1)} %collective-permute-done.7.refs_0_), channel_id=1, source_target_pairs={{0,4},{5,1},{4,8},{9,5},{8,12},{13,9},{12,14},{15,13},{14,10},{11,... | collective-permute-start | bytes 1597448 | tf_op jit(solution)/shard_map/ppermute | solution.py:250
  39.9 11.1 %collective-permute-start.24 = (bf16[128,2048]{1,0:T(8,128)(2,1)S(1)}, bf16[128,2048]{1,0:T(8,128)(2,1)S(1)}, u32[]{:S(2)}, u32[]{:S(2)}) collective-permute-start(bf16[128,2048]{1,0:T(8,128)(2,1)S(1)} %add_convert_fusion.3), channel_id=1, source_target_pairs={{0,4},{5,1},{4,8},{9,5},{8,12},{13,9},{12,14},{15,13},{14,10},{11,... | collective-permute-start | bytes 1572872 | tf_op jit(solution)/shard_map/ppermute | solution.py:270
  44.7 6.3 %collective-permute-start.18 = (bf16[128,2048]{1,0:T(8,128)(2,1)S(1)}, bf16[128,2048]{1,0:T(8,128)(2,1)S(1)}, u32[]{:S(2)}, u32[]{:S(2)}) collective-permute-start(bf16[128,2048]{1,0:T(8,128)(2,1)S(1)} %get-tuple-element.42), channel_id=1, source_target_pairs={{0,1},{1,0},{2,3},{3,2},{4,5},{5,4},{6,7},{7,6},{8,9},{9,8},{10,11... | collective-permute-start | bytes 1572872 | tf_op jit(solution)/shard_map/ppermute | solution.py:250
  45.3 8.0 %collective-permute-start.15 = (bf16[2080,128]{1,0:T(8,128)(2,1)S(1)}, bf16[2080,128]{1,0:T(8,128)(2,1)S(1)}, u32[]{:S(2)}, u32[]{:S(2)}) collective-permute-start(bf16[2080,128]{1,0:T(8,128)(2,1)S(1)} %collective-permute-done.8.refs_0_), channel_id=1, source_target_pairs={{0,1},{1,0},{2,3},{3,2},{4,5},{5,4},{6,7},{7,6},{8,9},{9,8},{10,11... | collective-permute-start | bytes 1597448 | tf_op jit(solution)/shard_map/ppermute | solution.py:250
  45.3 11.3 %collective-permute-start.9 = (bf16[2080,128]{1,0:T(8,128)(2,1)S(1)}, bf16[2080,128]{1,0:T(8,128)(2,1)S(1)}, u32[]{:S(2)}, u32[]{:S(2)}) collective-permute-start(bf16[2080,128]{1,0:T(8,128)(2,1)S(1)} %collective-permute-done.8.refs_0_), channel_id=1, source_target_pairs={{0,4},{5,1},{4,8},{9,5},{8,12},{13,9},{12,14},{15,13},{14,10},{11,... | collective-permute-start | bytes 1597448 | tf_op jit(solution)/shard_map/ppermute | solution.py:250
  51.2 13.3 %collective-permute-start.25 = (bf16[128,2048]{1,0:T(8,128)(2,1)S(1)}, bf16[128,2048]{1,0:T(8,128)(2,1)S(1)}, u32[]{:S(2)}, u32[]{:S(2)}) collective-permute-start(bf16[128,2048]{1,0:T(8,128)(2,1)S(1)} %add_convert_fusion.2), channel_id=1, source_target_pairs={{0,4},{5,1},{4,8},{9,5},{8,12},{13,9},{12,14},{15,13},{14,10},{11,... | collective-permute-start | bytes 1572872 | tf_op jit(solution)/shard_map/ppermute | solution.py:270
  56.0 8.5 %collective-permute-start.16 = (bf16[128,2048]{1,0:T(8,128)(2,1)S(1)}, bf16[128,2048]{1,0:T(8,128)(2,1)S(1)}, u32[]{:S(2)}, u32[]{:S(2)}) collective-permute-start(bf16[128,2048]{1,0:T(8,128)(2,1)S(1)} %get-tuple-element.40), channel_id=1, source_target_pairs={{0,1},{1,0},{2,3},{3,2},{4,5},{5,4},{6,7},{7,6},{8,9},{9,8},{10,11... | collective-permute-start | bytes 1572872 | tf_op jit(solution)/shard_map/ppermute | solution.py:250
  56.7 10.7 %collective-permute-start.13 = (bf16[2080,128]{1,0:T(8,128)(2,1)S(1)}, bf16[2080,128]{1,0:T(8,128)(2,1)S(1)}, u32[]{:S(2)}, u32[]{:S(2)}) collective-permute-start(bf16[2080,128]{1,0:T(8,128)(2,1)S(1)} %collective-permute-done.9.refs_0_), channel_id=1, source_target_pairs={{0,1},{1,0},{2,3},{3,2},{4,5},{5,4},{6,7},{7,6},{8,9},{9,8},{10,11... | collective-permute-start | bytes 1597448 | tf_op jit(solution)/shard_map/ppermute | solution.py:250
  56.7 17.5 %collective-permute-start.2 = (bf16[2080,128]{1,0:T(8,128)(2,1)S(1)}, bf16[2080,128]{1,0:T(8,128)(2,1)S(1)}, u32[]{:S(2)}, u32[]{:S(2)}) collective-permute-start(bf16[2080,128]{1,0:T(8,128)(2,1)S(1)} %packed.1.refs_0_), channel_id=1, source_target_pairs={{4,0},{1,5},{8,4},{5,9},{12,8},{9,13},{14,12},{13,15},{10,14},{15,... | collective-permute-start | bytes 1597448 | tf_op jit(solution)/shard_map/ppermute | solution.py:250
  58.7 15.0 %collective-permute-start.10 = (bf16[2080,128]{1,0:T(8,128)(2,1)S(1)}, bf16[2080,128]{1,0:T(8,128)(2,1)S(1)}, u32[]{:S(2)}, u32[]{:S(2)}) collective-permute-start(bf16[2080,128]{1,0:T(8,128)(2,1)S(1)} %collective-permute-done.9.refs_0_), channel_id=1, source_target_pairs={{0,4},{5,1},{4,8},{9,5},{8,12},{13,9},{12,14},{15,13},{14,10},{11,... | collective-permute-start | bytes 1597448 | tf_op jit(solution)/shard_map/ppermute | solution.py:250
  64.7 14.6 %collective-permute-start.26 = (bf16[128,2048]{1,0:T(8,128)(2,1)S(1)}, bf16[128,2048]{1,0:T(8,128)(2,1)S(1)}, u32[]{:S(2)}, u32[]{:S(2)}) collective-permute-start(bf16[128,2048]{1,0:T(8,128)(2,1)S(1)} %add_convert_fusion.1), channel_id=1, source_target_pairs={{0,4},{5,1},{4,8},{9,5},{8,12},{13,9},{12,14},{15,13},{14,10},{11,... | collective-permute-start | bytes 1572872 | tf_op jit(solution)/shard_map/ppermute | solution.py:270
  70.0 9.3 %collective-permute-start.14 = (bf16[128,2048]{1,0:T(8,128)(2,1)S(1)}, bf16[128,2048]{1,0:T(8,128)(2,1)S(1)}, u32[]{:S(2)}, u32[]{:S(2)}) collective-permute-start(bf16[128,2048]{1,0:T(8,128)(2,1)S(1)} %get-tuple-element.38), channel_id=1, source_target_pairs={{0,1},{1,0},{2,3},{3,2},{4,5},{5,4},{6,7},{7,6},{8,9},{9,8},{10,11... | collective-permute-start | bytes 1572872 | tf_op jit(solution)/shard_map/ppermute | solution.py:250
  73.7 8.0 %collective-permute-start.11 = (bf16[2080,128]{1,0:T(8,128)(2,1)S(1)}, bf16[2080,128]{1,0:T(8,128)(2,1)S(1)}, u32[]{:S(2)}, u32[]{:S(2)}) collective-permute-start(bf16[2080,128]{1,0:T(8,128)(2,1)S(1)} %collective-permute-done.10.refs_0_), channel_id=1, source_target_pairs={{0,1},{1,0},{2,3},{3,2},{4,5},{5,4},{6,7},{7,6},{8,9},{9,8},{10,11... | collective-permute-start | bytes 1597448 | tf_op jit(solution)/shard_map/ppermute | solution.py:250
  73.7 10.7 %collective-permute-start = (bf16[2080,128]{1,0:T(8,128)(2,1)S(1)}, bf16[2080,128]{1,0:T(8,128)(2,1)S(1)}, u32[]{:S(2)}, u32[]{:S(2)}) collective-permute-start(bf16[2080,128]{1,0:T(8,128)(2,1)S(1)} %packed.1.refs_0_), channel_id=1, source_target_pairs={{0,1},{1,0},{2,3},{3,2},{4,5},{5,4},{6,7},{7,6},{8,9},{9,8},{10,11... | collective-permute-start | bytes 1597448 | tf_op jit(solution)/shard_map/ppermute | solution.py:250
  74.2 13.5 %collective-permute-start.3 = (bf16[2080,128]{1,0:T(8,128)(2,1)S(1)}, bf16[2080,128]{1,0:T(8,128)(2,1)S(1)}, u32[]{:S(2)}, u32[]{:S(2)}) collective-permute-start(bf16[2080,128]{1,0:T(8,128)(2,1)S(1)} %collective-permute-done.2.refs_0_), channel_id=1, source_target_pairs={{0,1},{1,0},{2,3},{3,2},{4,5},{5,4},{6,7},{7,6},{8,9},{9,8},{10,11... | collective-permute-start | bytes 1597448 | tf_op jit(solution)/shard_map/ppermute | solution.py:250
  79.5 10.9 %collective-permute-start.27 = (bf16[128,2048]{1,0:T(8,128)(2,1)S(1)}, bf16[128,2048]{1,0:T(8,128)(2,1)S(1)}, u32[]{:S(2)}, u32[]{:S(2)}) collective-permute-start(bf16[128,2048]{1,0:T(8,128)(2,1)S(1)} %add_convert_fusion), channel_id=1, source_target_pairs={{0,4},{5,1},{4,8},{9,5},{8,12},{13,9},{12,14},{15,13},{14,10},{11,... | collective-permute-start | bytes 1572872 | tf_op jit(solution)/shard_map/ppermute | solution.py:270
  84.3 6.1 %collective-permute-start.12 = (bf16[128,2048]{1,0:T(8,128)(2,1)S(1)}, bf16[128,2048]{1,0:T(8,128)(2,1)S(1)}, u32[]{:S(2)}, u32[]{:S(2)}) collective-permute-start(bf16[128,2048]{1,0:T(8,128)(2,1)S(1)} %get-tuple-element.36), channel_id=1, source_target_pairs={{0,1},{1,0},{2,3},{3,2},{4,5},{5,4},{6,7},{7,6},{8,9},{9,8},{10,11... | collective-permute-start | bytes 1572872 | tf_op jit(solution)/shard_map/ppermute | solution.py:250
  87.1 13.6 %collective-permute-start.1 = (bf16[128,2048]{1,0:T(8,128)(2,1)S(1)}, bf16[128,2048]{1,0:T(8,128)(2,1)S(1)}, u32[]{:S(2)}, u32[]{:S(2)}) collective-permute-start(bf16[128,2048]{1,0:T(8,128)(2,1)S(1)} %get-tuple-element.32), channel_id=1, source_target_pairs={{0,1},{1,0},{2,3},{3,2},{4,5},{5,4},{6,7},{7,6},{8,9},{9,8},{10,11... | collective-permute-start | bytes 1572872 | tf_op jit(solution)/shard_map/ppermute | solution.py:250
  90.3 5.1 %collective-permute-start.4 = (bf16[128,2048]{1,0:T(8,128)(2,1)S(1)}, bf16[128,2048]{1,0:T(8,128)(2,1)S(1)}, u32[]{:S(2)}, u32[]{:S(2)}) collective-permute-start(bf16[128,2048]{1,0:T(8,128)(2,1)S(1)} %get-tuple-element.34), channel_id=1, source_target_pairs={{0,1},{1,0},{2,3},{3,2},{4,5},{5,4},{6,7},{7,6},{8,9},{9,8},{10,11... | collective-permute-start | bytes 1572872 | tf_op jit(solution)/shard_map/ppermute | solution.py:250
  90.5 8.4 %collective-permute-start.28 = (bf16[48,2048]{1,0:T(8,128)(2,1)S(1)}, bf16[48,2048]{1,0:T(8,128)(2,1)S(1)}, u32[]{:S(2)}, u32[]{:S(2)}) collective-permute-start(bf16[48,2048]{1,0:T(8,128)(2,1)S(1)} %add_convert_fusion.10), channel_id=1, source_target_pairs={{0,4},{5,1},{4,8},{9,5},{8,12},{13,9},{12,14},{15,13},{14,10},{11,... | collective-permute-start | bytes 589832 | tf_op jit(solution)/shard_map/ppermute | solution.py:275
  92.2 5.1 %collective-permute-start.30 = (bf16[24,2048]{1,0:T(8,128)(2,1)S(1)}, bf16[24,2048]{1,0:T(8,128)(2,1)S(1)}, u32[]{:S(2)}, u32[]{:S(2)}) collective-permute-start(bf16[24,2048]{1,0:T(8,128)(2,1)S(1)} %add_convert_fusion.13), channel_id=1, source_target_pairs={{0,4},{5,1},{4,8},{9,5},{8,12},{13,9},{12,14},{15,13},{14,10},{11,... | collective-permute-start | bytes 294920 | tf_op jit(solution)/shard_map/ppermute | solution.py:275
  93.9 8.1 %collective-permute-start.32 = (bf16[56,2048]{1,0:T(8,128)(2,1)S(1)}, bf16[56,2048]{1,0:T(8,128)(2,1)S(1)}, u32[]{:S(2)}, u32[]{:S(2)}) collective-permute-start(bf16[56,2048]{1,0:T(8,128)(2,1)S(1)} %add_convert_fusion.7), channel_id=1, source_target_pairs={{0,4},{5,1},{4,8},{9,5},{8,12},{13,9},{12,14},{15,13},{14,10},{11,... | collective-permute-start | bytes 688136 | tf_op jit(solution)/shard_map/ppermute | solution.py:275
  97.3 4.7 %collective-permute-start.31 = (bf16[24,2048]{1,0:T(8,128)(2,1)S(1)}, bf16[24,2048]{1,0:T(8,128)(2,1)S(1)}, u32[]{:S(2)}, u32[]{:S(2)}) collective-permute-start(bf16[24,2048]{1,0:T(8,128)(2,1)S(1)} %add_convert_fusion.12), channel_id=1, source_target_pairs={{0,4},{5,1},{4,8},{9,5},{8,12},{13,9},{12,14},{15,13},{14,10},{11,... | collective-permute-start | bytes 294920 | tf_op jit(solution)/shard_map/ppermute | solution.py:275
  99.0 5.7 %collective-permute-start.29 = (bf16[48,2048]{1,0:T(8,128)(2,1)S(1)}, bf16[48,2048]{1,0:T(8,128)(2,1)S(1)}, u32[]{:S(2)}, u32[]{:S(2)}) collective-permute-start(bf16[48,2048]{1,0:T(8,128)(2,1)S(1)} %add_convert_fusion.9), channel_id=1, source_target_pairs={{0,4},{5,1},{4,8},{9,5},{8,12},{13,9},{12,14},{15,13},{14,10},{11,... | collective-permute-start | bytes 589832 | tf_op jit(solution)/shard_map/ppermute | solution.py:275
  102.1 6.1 %collective-permute-start.33 = (bf16[56,2048]{1,0:T(8,128)(2,1)S(1)}, bf16[56,2048]{1,0:T(8,128)(2,1)S(1)}, u32[]{:S(2)}, u32[]{:S(2)}) collective-permute-start(bf16[56,2048]{1,0:T(8,128)(2,1)S(1)} %add_convert_fusion.6), channel_id=1, source_target_pairs={{0,4},{5,1},{4,8},{9,5},{8,12},{13,9},{12,14},{15,13},{14,10},{11,... | collective-permute-start | bytes 688136 | tf_op jit(solution)/shard_map/ppermute | solution.py:275
where the time goes:
time: 109 us
  waiting for transfers between devices  44.4 us (41%)
  starting transfers between devices  35.6 us (33%)
  Pallas kernels  26.5 us (24%)
  other arithmetic  2.42 us (2%)
    pallas_call x8, Pallas kernels, visit(): pl.pallas_call(functools.partial(visit_kernel, (len(near), len(far))), ou...  21.3 us
    ppermute x23, waiting for transfers between devices, moved(): return lax.ppermute(value, 'tok', pairs)  19 us
    ppermute x5, waiting for transfers between devices, circulated(): total = lax.ppermute(summed(step, slice(None), total), 'tok', ring)  17.9 us
    ppermute x23, starting transfers between devices, moved(): return lax.ppermute(value, 'tok', pairs)  15.3 us
    ppermute x5, starting transfers between devices, circulated(): total = lax.ppermute(summed(step, slice(None), total), 'tok', ring)  10.6 us
    ppermute x6, starting transfers between devices, circulated(): totals[name] = lax.ppermute(summed(step, rows, totals[name]), 'tok', ring)  9.72 us
    ppermute x6, waiting for transfers between devices, circulated(): totals[name] = lax.ppermute(summed(step, rows, totals[name]), 'tok', ring)  7.51 us
    pallas_call x1, Pallas kernels, loaded(): pl.pallas_call(functools.partial(loaded_kernel, count), out_shape=tuple((...  3.78 us
  transfers between devices with their start and end apart: 34, of which 14 were waited for; matrix products, arithmetic and copies ran while one was open for 1% of the time, Pallas kernels for 23%

commit v1 on v0

--- a/solution.py
+++ b/solution.py
@@ -76,7 +76,7 @@
 
 
 def packed_kernel(tokens_hbm, gain_hbm, ids_hbm, gates_hbm, *refs):
-    *part_refs, tokens, gain, ids, gates, sems = refs
+    out_ref, tokens, gain, ids, gates, sems = refs
     moves = [
         pltpu.make_async_copy(source, target, sems.at[i])
         for i, (source, target) in enumerate(
@@ -89,37 +89,24 @@
     moves[0].wait()
     moves[1].wait()
     weights = gates[...] / jnp.sum(gates[...], axis=0, keepdims=True)
-    experts = (sum(ref.shape[0] for ref in part_refs) - tok_rows * model_width // LANES) // 2
+    experts = (out_ref.shape[0] - tok_rows * model_width // LANES) // 2
     label = lax.broadcasted_iota(jnp.int32, (experts, tok_rows), 0)
     table = jnp.zeros((experts, tok_rows), jnp.float32)
     for k in range(ids.shape[0]):
         table += jnp.where(label == ids[k : k + 1, :], weights[k : k + 1, :], 0.0)
     high = table.astype(jnp.bfloat16)
     low = (table - high.astype(jnp.float32)).astype(jnp.bfloat16)
-    last = part_refs[-1]
-    last[-2 * experts : -experts, :] = high
-    last[-experts:, :] = low
+    out_ref[-2 * experts : -experts, :] = high
+    out_ref[-experts:, :] = low
     moves[2].wait()
     moves[3].wait()
-    places = tiles_of(part_refs, tok_rows, model_width)
     for top in range(0, tok_rows, TALL):
         values = tokens[top : top + TALL, :].astype(jnp.float32)
         row_scale = lax.rsqrt(jnp.mean(values * values, axis=1, keepdims=True) + 1e-06)
         normed = (values * row_scale * gain[...]).astype(jnp.bfloat16)
         for side in range(0, model_width, LANES):
-            ref, row = places[top, side]
-            ref[row : row + TALL, :] = normed[:, side : side + LANES]
-
-
-def tiles_of(part_refs, tok_rows, model_width):
-    tiles = [(top, side) for top in range(0, tok_rows, TALL) for side in range(0, model_width, LANES)]
-    places, part, row = {}, 0, 0
-    for tile in tiles:
-        if row == part_refs[part].shape[0]:
-            part, row = part + 1, 0
-        places[tile] = part_refs[part], row
-        row += TALL
-    return places
+            row = top * model_width // LANES + side // LANES * TALL
+            out_ref[row : row + TALL, :] = normed[:, side : side + LANES]
 
 
 def packed(tokens, norm_gain, expert_ids, gate_weights, experts):
@@ -128,9 +115,9 @@
     size = tok_rows * model_width // LANES + 2 * experts
     return pl.pallas_call(
         packed_kernel,
-        out_shape=(jax.ShapeDtypeStruct((size, LANES), jnp.bfloat16),),
+        out_shape=jax.ShapeDtypeStruct((size, LANES), jnp.bfloat16),
         in_specs=[pl.BlockSpec(memory_space=pltpu.HBM)] * 4,
-        out_specs=(pl.BlockSpec(memory_space=pltpu.VMEM),),
+        out_specs=pl.BlockSpec(memory_space=pltpu.VMEM),
         scratch_shapes=[
             pltpu.VMEM((tok_rows, model_width), jnp.bfloat16),
             pltpu.VMEM((1, model_width), jnp.float32),
@@ -171,16 +158,18 @@
     )(*map(in_hbm, arrays))
 
 
-def visit_kernel(counts, owners_ref, *refs):
-    near_refs, refs = refs[: counts[0]], refs[counts[0] :]
-    far_refs, refs = refs[: counts[1]], refs[counts[1] :]
-    in_ref, in_scale_ref, down_ref, down_scale_ref, part_ref, lent_ref, rows_ref, hidden_ref = refs
-    tok_rows, model_width = part_ref.shape
+def visit_kernel(count, owners_ref, *refs):
+    block_refs, refs = refs[:count], refs[count:]
+    in_ref, in_scale_ref, down_ref, down_scale_ref = refs[:4]
+    out_refs, (rows_ref, hidden_ref) = refs[4 : 4 + count], refs[4 + count :]
+    tok_rows, model_width = out_refs[0].shape
     hidden_width = hidden_ref.shape[1]
-    for base, block_refs in ((0, near_refs), (tok_rows, far_refs)):
-        for (top, side), (ref, row) in tiles_of(block_refs, tok_rows, model_width).items():
-            tile = ref[row : row + TALL, :]
-            rows_ref[base + top : base + top + TALL, side : side + LANES] = tile
+    tall = [(top, side) for top in range(0, tok_rows, TALL) for side in range(0, model_width, LANES)]
+    for i, block_ref in enumerate(block_refs):
+        for place, (top, side) in enumerate(tall):
+            tile = block_ref[place * TALL : (place + 1) * TALL, :]
+            base = i * tok_rows + top
+            rows_ref[base : base + TALL, side : side + LANES] = tile
     rows = rows_ref[...]
     for start in range(0, hidden_width, TILE):
         cols = slice(start, start + TILE)
@@ -197,42 +186,40 @@
     chosen = (label == mine) | (label == mine + experts)
     square = (tok_rows, tok_rows)
     same = lax.broadcasted_iota(jnp.int32, square, 0) == lax.broadcasted_iota(jnp.int32, square, 1)
-
-    def share_of(block_refs):
-        table = block_refs[-1][-2 * experts :, :].astype(jnp.float32)
+    shares = []
+    for block_ref in block_refs:
+        table = block_ref[-2 * experts :, :].astype(jnp.float32)
         along = jnp.sum(jnp.where(chosen, table, 0.0), axis=0, keepdims=True)
-        return jnp.sum(jnp.where(same, along, 0.0), axis=1, keepdims=True)
-
-    near_share, far_share = share_of(near_refs), share_of(far_refs)
+        shares.append(jnp.sum(jnp.where(same, along, 0.0), axis=1, keepdims=True))
     hidden = hidden_ref[...]
     for start in range(0, model_width, TILE):
         cols = slice(start, start + TILE)
         out = jnp.dot(hidden, down_ref[0, :, cols], preferred_element_type=jnp.float32)
         out = out * down_scale_ref[:, cols].astype(jnp.float32)
-        part_ref[:, cols] = out[:tok_rows] * near_share
-        lent_ref[:, cols] = (out[tok_rows:] * far_share).astype(jnp.bfloat16)
-
-
-def visit(near, far, owners, in_q, in_scale, down_q, down_scale):
+        for i, (out_ref, share) in enumerate(zip(out_refs, shares)):
+            weighted = out[i * tok_rows : (i + 1) * tok_rows] * share
+            out_ref[:, cols] = weighted.astype(out_ref.dtype)
+
+
+def visit(visitors, kinds, owners, in_q, in_scale, down_q, down_scale):
     hidden_width, model_width = down_q.shape[1:]
-    tok_rows = (sum(x.shape[0] for x in near) - 2 * owners.shape[1]) * LANES // model_width
-    flops = 2 * 2 * tok_rows * 3 * hidden_width * model_width
-    operands = (owners, *near, *far, in_q, in_scale, down_q, down_scale)
+    tok_rows = (visitors[0].shape[0] - 2 * owners.shape[1]) * LANES // model_width
+    count = len(visitors)
+    operands = (owners, *visitors, in_q, in_scale, down_q, down_scale)
     return pl.pallas_call(
-        functools.partial(visit_kernel, (len(near), len(far))),
-        out_shape=(
-            jax.ShapeDtypeStruct((tok_rows, model_width), jnp.float32),
-            jax.ShapeDtypeStruct((tok_rows, model_width), jnp.bfloat16),
-        ),
+        functools.partial(visit_kernel, count),
+        out_shape=tuple(jax.ShapeDtypeStruct((tok_rows, model_width), kind) for kind in kinds),
         in_specs=[pl.BlockSpec(memory_space=pltpu.VMEM)] * len(operands),
-        out_specs=(pl.BlockSpec(memory_space=pltpu.VMEM),) * 2,
+        out_specs=(pl.BlockSpec(memory_space=pltpu.VMEM),) * count,
         scratch_shapes=[
-            pltpu.VMEM((2 * tok_rows, model_width), jnp.bfloat16),
-            pltpu.VMEM((2 * tok_rows, hidden_width), jnp.bfloat16),
+            pltpu.VMEM((count * tok_rows, model_width), jnp.bfloat16),
+            pltpu.VMEM((count * tok_rows, hidden_width), jnp.bfloat16),
         ],
         compiler_params=pltpu.CompilerParams(vmem_limit_bytes=LARGE),
         cost_estimate=pl.CostEstimate(
-            flops=flops, bytes_accessed=6 * tok_rows * model_width, transcendentals=0
+            flops=2 * count * tok_rows * 3 * hidden_width * model_width,
+            bytes_accessed=3 * count * tok_rows * model_width,
+            transcendentals=0,
         ),
         name="visit",
     )(*operands)
@@ -249,7 +236,7 @@
     def moved(value, pairs):
         return lax.ppermute(value, "tok", pairs)
 
-    (block,) = packed(tokens, norm_gain, expert_ids, gate_weights, experts)
+    block = packed(tokens, norm_gain, expert_ids, gate_weights, experts)
     blocks = loaded(owner_map[None, :], in_q, in_scale, down_q, down_scale)
     back = moved(block, [(target, source) for source, target in ring])
     parts = []
@@ -258,7 +245,11 @@
         other = moved(here, swap)
         if step < chips - 2:
             block = moved(block, ring)
-        part, lent = visit((here,), (other,), *blocks)
+        if step == chips - 2:
+            (part,) = visit((here,), (jnp.float32,), *blocks)
+            (lent,) = visit((other,), (jnp.bfloat16,), *blocks)
+        else:
+            part, lent = visit((here, other), (jnp.float32, jnp.bfloat16), *blocks)
         parts.append((part, moved(lent, swap)))
 
     def summed(step, rows, arrived):
@@ -280,7 +271,7 @@
 
 
 def shares_of(tok_rows):
-    one, two = tok_rows // 16 * 6, tok_rows // 16 * 9
+    one, two = tok_rows // 16 * 7, tok_rows // 16 * 12
     return {"a": slice(0, one), "b": slice(one, two), "c": slice(two, tok_rows)}
 
 

time: 109 us -> 109 us (level)
    pallas_call x9 -> x10, Pallas kernels: 22.7 us -> 23.1 us  [the longest x9 21.8 us: visit(): pl.pallas_call(functools.partial(visit_kernel, count), out_shape=tuple((j...]
where the time goes in v1:
time: 109 us
  waiting for transfers between devices  43.8 us (40%)
  starting transfers between devices  35.6 us (33%)
  Pallas kernels  26.9 us (25%)
  other arithmetic  2.35 us (2%)
    pallas_call x9, Pallas kernels, visit(): pl.pallas_call(functools.partial(visit_kernel, count), out_shape=tuple((j...  21.8 us
    ppermute x23, waiting for transfers between devices, moved(): return lax.ppermute(value, 'tok', pairs)  18.9 us
    ppermute x5, waiting for transfers between devices, circulated(): total = lax.ppermute(summed(step, slice(None), total), 'tok', ring)  17.9 us
    ppermute x23, starting transfers between devices, moved(): return lax.ppermute(value, 'tok', pairs)  15.3 us
    ppermute x5, starting transfers between devices, circulated(): total = lax.ppermute(summed(step, slice(None), total), 'tok', ring)  10.6 us
    ppermute x6, starting transfers between devices, circulated(): totals[name] = lax.ppermute(summed(step, rows, totals[name]), 'tok', ring)  9.73 us
    ppermute x6, waiting for transfers between devices, circulated(): totals[name] = lax.ppermute(summed(step, rows, totals[name]), 'tok', ring)  6.94 us
    pallas_call x1, Pallas kernels, loaded(): pl.pallas_call(functools.partial(loaded_kernel, count), out_shape=tuple((...  3.78 us
  transfers between devices with their start and end apart: 34, of which 14 were waited for; matrix products, arithmetic and copies ran while one was open for 1% of the time, Pallas kernels for 23%

profile of v1, /device:TPU:0, one launch (start us, length us, event | category | flops | bytes accessed | tf_op | source)
XLA Modules:
  0.0 108.9 jit_solution(366119512013885513)
XLA Ops:
  0.0 1.3 %packed.1.refs_0_ = bf16[2080,128]{1,0:T(8,128)(2,1)S(1)} custom-call(bf16[128,2048]{1,0:T(8,128)(2,1)} %tokens_hbm.1, f32[1,2048]{1,0:T(1,128)} %bitcast.4, s32[8,128]{1,0:T(8,128)} %bitcast.5, f32[8,128]{1,0:T(8,128)} %bitcast.6), custom_call_target="tpu_custom_call" | custom-call | tf_op jit(solution)/shard_map/packed/pallas_call | solution.py:116
  1.3 3.1 %collective-permute-start.5 = (bf16[2080,128]{1,0:T(8,128)(2,1)S(1)}, bf16[2080,128]{1,0:T(8,128)(2,1)S(1)}, u32[]{:S(2)}, u32[]{:S(2)}) collective-permute-start(bf16[2080,128]{1,0:T(8,128)(2,1)S(1)} %packed.1.refs_0_), channel_id=1, source_target_pairs={{0,4},{5,1},{4,8},{9,5},{8,12},{13,9},{12,14},{15,13},{14,10},{11,... | collective-permute-start | bytes 1597448 | tf_op jit(solution)/shard_map/ppermute | solution.py:237
  4.4 7.2 %collective-permute-done.5.refs_0_ = bf16[2080,128]{1,0:T(8,128)(2,1)S(1)} collective-permute-done((bf16[2080,128]{1,0:T(8,128)(2,1)S(1)}, bf16[2080,128]{1,0:T(8,128)(2,1)S(1)}, u32[]{:S(2)}, u32[]{:S(2)}) %collective-permute-start.5) | collective-permute-done | bytes 532512 | tf_op jit(solution)/shard_map/ppermute | solution.py:237
  11.6 3.8 %loaded.1 = (s32[1,16]{1,0:T(1,128)S(1)}, bf16[1,2,2048,768]{3,2,1,0:T(8,128)(2,1)S(1)}, bf16[1,2,768]{2,1,0:T(2,128)(2,1)S(1)}, bf16[1,768,2048]{2,1,0:T(8,128)(2,1)S(1)}, bf16[1,2048]{1,0:T(2,128)(2,1)S(1)}) custom-call(s32[1,16]{1,0:T(1,128)} %bitcast.7, bf16[1,2,2048,768]{3,2,1,0:T(8,128)(2,1)} %refs_1_.1, bf16[1,2,768]{2,1,0:T(2,128)(2,1)} %refs_2_.1, ...), custom_call_target="tpu_custom_call" | custom-call | bytes 9444384 | tf_op jit(solution)/shard_map/loaded/pallas_call | solution.py:147
  15.4 2.1 %collective-permute-start.6 = (bf16[2080,128]{1,0:T(8,128)(2,1)S(1)}, bf16[2080,128]{1,0:T(8,128)(2,1)S(1)}, u32[]{:S(2)}, u32[]{:S(2)}) collective-permute-start(bf16[2080,128]{1,0:T(8,128)(2,1)S(1)} %collective-permute-done.5.refs_0_), channel_id=1, source_target_pairs={{0,4},{5,1},{4,8},{9,5},{8,12},{13,9},{12,14},{15,13},{14,10},{11,... | collective-permute-start | bytes 1597448 | tf_op jit(solution)/shard_map/ppermute | solution.py:237
  17.6 2.7 %visit.17 = (f32[128,2048]{1,0:T(8,128)S(1)}, bf16[128,2048]{1,0:T(8,128)(2,1)S(1)}) custom-call(s32[1,16]{1,0:T(1,128)S(1)} %get-tuple-element.24.owners_ref, bf16[2080,128]{1,0:T(8,128)(2,1)S(1)} %collective-permute-done.5.refs_0_, bf16[2080,128]{1,0:T(8,128)(2,1)S(1)} %collective-permute-done.21.refs_1_, ...), custom_call_target="tpu_custom_call" | custom-call | flops 2415919104 | bytes 1572864 | tf_op jit(solution)/shard_map/visit/pallas_call | solution.py:209
  20.2 0.2 collective-permute-start.22
  20.5 4.3 %collective-permute-done.6.refs_0_ = bf16[2080,128]{1,0:T(8,128)(2,1)S(1)} collective-permute-done((bf16[2080,128]{1,0:T(8,128)(2,1)S(1)}, bf16[2080,128]{1,0:T(8,128)(2,1)S(1)}, u32[]{:S(2)}, u32[]{:S(2)}) %collective-permute-start.6) | collective-permute-done | bytes 532512 | tf_op jit(solution)/shard_map/ppermute | solution.py:237
  24.7 2.1 %collective-permute-start.7 = (bf16[2080,128]{1,0:T(8,128)(2,1)S(1)}, bf16[2080,128]{1,0:T(8,128)(2,1)S(1)}, u32[]{:S(2)}, u32[]{:S(2)}) collective-permute-start(bf16[2080,128]{1,0:T(8,128)(2,1)S(1)} %collective-permute-done.6.refs_0_), channel_id=1, source_target_pairs={{0,4},{5,1},{4,8},{9,5},{8,12},{13,9},{12,14},{15,13},{14,10},{11,... | collective-permute-start | bytes 1597448 | tf_op jit(solution)/shard_map/ppermute | solution.py:237
  26.8 0.1 add_convert_fusion.4
  27.0 1.6 %collective-permute-start.23 = (bf16[128,2048]{1,0:T(8,128)(2,1)S(1)}, bf16[128,2048]{1,0:T(8,128)(2,1)S(1)}, u32[]{:S(2)}, u32[]{:S(2)}) collective-permute-start(bf16[128,2048]{1,0:T(8,128)(2,1)S(1)} %add_convert_fusion.4), channel_id=1, source_target_pairs={{0,4},{5,1},{4,8},{9,5},{8,12},{13,9},{12,14},{15,13},{14,10},{11,... | collective-permute-start | bytes 1572872 | tf_op jit(solution)/shard_map/ppermute | solution.py:261
  28.6 2.7 %visit.16 = (f32[128,2048]{1,0:T(8,128)S(1)}, bf16[128,2048]{1,0:T(8,128)(2,1)S(1)}) custom-call(s32[1,16]{1,0:T(1,128)S(1)} %get-tuple-element.24.owners_ref, bf16[2080,128]{1,0:T(8,128)(2,1)S(1)} %collective-permute-done.6.refs_0_, bf16[2080,128]{1,0:T(8,128)(2,1)S(1)} %collective-permute-done.19.refs_1_, ...), custom_call_target="tpu_custom_call" | custom-call | flops 2415919104 | bytes 1572864 | tf_op jit(solution)/shard_map/visit/pallas_call | solution.py:209
  31.3 0.1 collective-permute-start.20
  31.3 2.7 %collective-permute-done.7.refs_0_ = bf16[2080,128]{1,0:T(8,128)(2,1)S(1)} collective-permute-done((bf16[2080,128]{1,0:T(8,128)(2,1)S(1)}, bf16[2080,128]{1,0:T(8,128)(2,1)S(1)}, u32[]{:S(2)}, u32[]{:S(2)}) %collective-permute-start.7) | collective-permute-done | bytes 532512 | tf_op jit(solution)/shard_map/ppermute | solution.py:237
  34.0 2.1 %collective-permute-start.8 = (bf16[2080,128]{1,0:T(8,128)(2,1)S(1)}, bf16[2080,128]{1,0:T(8,128)(2,1)S(1)}, u32[]{:S(2)}, u32[]{:S(2)}) collective-permute-start(bf16[2080,128]{1,0:T(8,128)(2,1)S(1)} %collective-permute-done.7.refs_0_), channel_id=1, source_target_pairs={{0,4},{5,1},{4,8},{9,5},{8,12},{13,9},{12,14},{15,13},{14,10},{11,... | collective-permute-start | bytes 1597448 | tf_op jit(solution)/shard_map/ppermute | solution.py:237
  36.1 3.5 %collective-permute-done.23 = bf16[128,2048]{1,0:T(8,128)(2,1)S(1)} collective-permute-done((bf16[128,2048]{1,0:T(8,128)(2,1)S(1)}, bf16[128,2048]{1,0:T(8,128)(2,1)S(1)}, u32[]{:S(2)}, u32[]{:S(2)}) %collective-permute-start.23) | collective-permute-done | bytes 524320 | tf_op jit(solution)/shard_map/ppermute | solution.py:261
  39.6 0.2 add_convert_fusion.3
  39.8 2.1 %collective-permute-start.24 = (bf16[128,2048]{1,0:T(8,128)(2,1)S(1)}, bf16[128,2048]{1,0:T(8,128)(2,1)S(1)}, u32[]{:S(2)}, u32[]{:S(2)}) collective-permute-start(bf16[128,2048]{1,0:T(8,128)(2,1)S(1)} %add_convert_fusion.3), channel_id=1, source_target_pairs={{0,4},{5,1},{4,8},{9,5},{8,12},{13,9},{12,14},{15,13},{14,10},{11,... | collective-permute-start | bytes 1572872 | tf_op jit(solution)/shard_map/ppermute | solution.py:261
  42.0 2.7 %visit.15 = (f32[128,2048]{1,0:T(8,128)S(1)}, bf16[128,2048]{1,0:T(8,128)(2,1)S(1)}) custom-call(s32[1,16]{1,0:T(1,128)S(1)} %get-tuple-element.24.owners_ref, bf16[2080,128]{1,0:T(8,128)(2,1)S(1)} %collective-permute-done.7.refs_0_, bf16[2080,128]{1,0:T(8,128)(2,1)S(1)} %collective-permute-done.17.refs_1_, ...), custom_call_target="tpu_custom_call" | custom-call | flops 2415919104 | bytes 1572864 | tf_op jit(solution)/shard_map/visit/pallas_call | solution.py:209
  44.6 0.1 collective-permute-start.18
  44.7 0.6 collective-permute-done.8.refs_0_
  45.3 2.1 %collective-permute-start.9 = (bf16[2080,128]{1,0:T(8,128)(2,1)S(1)}, bf16[2080,128]{1,0:T(8,128)(2,1)S(1)}, u32[]{:S(2)}, u32[]{:S(2)}) collective-permute-start(bf16[2080,128]{1,0:T(8,128)(2,1)S(1)} %collective-permute-done.8.refs_0_), channel_id=1, source_target_pairs={{0,4},{5,1},{4,8},{9,5},{8,12},{13,9},{12,14},{15,13},{14,10},{11,... | collective-permute-start | bytes 1597448 | tf_op jit(solution)/shard_map/ppermute | solution.py:237
  47.4 3.5 %collective-permute-done.24 = bf16[128,2048]{1,0:T(8,128)(2,1)S(1)} collective-permute-done((bf16[128,2048]{1,0:T(8,128)(2,1)S(1)}, bf16[128,2048]{1,0:T(8,128)(2,1)S(1)}, u32[]{:S(2)}, u32[]{:S(2)}) %collective-permute-start.24) | collective-permute-done | bytes 524320 | tf_op jit(solution)/shard_map/ppermute | solution.py:261
  51.0 0.2 add_convert_fusion.2
  51.2 2.1 %collective-permute-start.25 = (bf16[128,2048]{1,0:T(8,128)(2,1)S(1)}, bf16[128,2048]{1,0:T(8,128)(2,1)S(1)}, u32[]{:S(2)}, u32[]{:S(2)}) collective-permute-start(bf16[128,2048]{1,0:T(8,128)(2,1)S(1)} %add_convert_fusion.2), channel_id=1, source_target_pairs={{0,4},{5,1},{4,8},{9,5},{8,12},{13,9},{12,14},{15,13},{14,10},{11,... | collective-permute-start | bytes 1572872 | tf_op jit(solution)/shard_map/ppermute | solution.py:261
  53.3 2.7 %visit.14 = (f32[128,2048]{1,0:T(8,128)S(1)}, bf16[128,2048]{1,0:T(8,128)(2,1)S(1)}) custom-call(s32[1,16]{1,0:T(1,128)S(1)} %get-tuple-element.24.owners_ref, bf16[2080,128]{1,0:T(8,128)(2,1)S(1)} %collective-permute-done.8.refs_0_, bf16[2080,128]{1,0:T(8,128)(2,1)S(1)} %collective-permute-done.15.refs_1_, ...), custom_call_target="tpu_custom_call" | custom-call | flops 2415919104 | bytes 1572864 | tf_op jit(solution)/shard_map/visit/pallas_call | solution.py:209
  56.0 0.1 collective-permute-start.16
  56.1 0.6 collective-permute-done.9.refs_0_
  56.7 2.0 %collective-permute-start.2 = (bf16[2080,128]{1,0:T(8,128)(2,1)S(1)}, bf16[2080,128]{1,0:T(8,128)(2,1)S(1)}, u32[]{:S(2)}, u32[]{:S(2)}) collective-permute-start(bf16[2080,128]{1,0:T(8,128)(2,1)S(1)} %packed.1.refs_0_), channel_id=1, source_target_pairs={{4,0},{1,5},{8,4},{5,9},{12,8},{9,13},{14,12},{13,15},{10,14},{15,... | collective-permute-start | bytes 1597448 | tf_op jit(solution)/shard_map/ppermute | solution.py:237
  58.7 0.1 collective-permute-start.10
  58.7 5.8 %collective-permute-done.25 = bf16[128,2048]{1,0:T(8,128)(2,1)S(1)} collective-permute-done((bf16[128,2048]{1,0:T(8,128)(2,1)S(1)}, bf16[128,2048]{1,0:T(8,128)(2,1)S(1)}, u32[]{:S(2)}, u32[]{:S(2)}) %collective-permute-start.25) | collective-permute-done | bytes 524320 | tf_op jit(solution)/shard_map/ppermute | solution.py:261
  64.5 0.2 add_convert_fusion.1
  64.7 2.6 %collective-permute-start.26 = (bf16[128,2048]{1,0:T(8,128)(2,1)S(1)}, bf16[128,2048]{1,0:T(8,128)(2,1)S(1)}, u32[]{:S(2)}, u32[]{:S(2)}) collective-permute-start(bf16[128,2048]{1,0:T(8,128)(2,1)S(1)} %add_convert_fusion.1), channel_id=1, source_target_pairs={{0,4},{5,1},{4,8},{9,5},{8,12},{13,9},{12,14},{15,13},{14,10},{11,... | collective-permute-start | bytes 1572872 | tf_op jit(solution)/shard_map/ppermute | solution.py:261
  67.3 2.7 %visit.13 = (f32[128,2048]{1,0:T(8,128)S(1)}, bf16[128,2048]{1,0:T(8,128)(2,1)S(1)}) custom-call(s32[1,16]{1,0:T(1,128)S(1)} %get-tuple-element.24.owners_ref, bf16[2080,128]{1,0:T(8,128)(2,1)S(1)} %collective-permute-done.9.refs_0_, bf16[2080,128]{1,0:T(8,128)(2,1)S(1)} %collective-permute-done.13.refs_1_, ...), custom_call_target="tpu_custom_call" | custom-call | flops 2415919104 | bytes 1572864 | tf_op jit(solution)/shard_map/visit/pallas_call | solution.py:209
  70.0 0.1 collective-permute-start.14
  70.1 3.6 %collective-permute-done.10.refs_0_ = bf16[2080,128]{1,0:T(8,128)(2,1)S(1)} collective-permute-done((bf16[2080,128]{1,0:T(8,128)(2,1)S(1)}, bf16[2080,128]{1,0:T(8,128)(2,1)S(1)}, u32[]{:S(2)}, u32[]{:S(2)}) %collective-permute-start.10) | collective-permute-done | bytes 532512 | tf_op jit(solution)/shard_map/ppermute | solution.py:237
  73.7 0.5 collective-permute-start
  74.2 5.1 %collective-permute-done.26 = bf16[128,2048]{1,0:T(8,128)(2,1)S(1)} collective-permute-done((bf16[128,2048]{1,0:T(8,128)(2,1)S(1)}, bf16[128,2048]{1,0:T(8,128)(2,1)S(1)}, u32[]{:S(2)}, u32[]{:S(2)}) %collective-permute-start.26) | collective-permute-done | bytes 524320 | tf_op jit(solution)/shard_map/ppermute | solution.py:261
  79.3 0.2 add_convert_fusion
  79.5 2.1 %collective-permute-start.27 = (bf16[128,2048]{1,0:T(8,128)(2,1)S(1)}, bf16[128,2048]{1,0:T(8,128)(2,1)S(1)}, u32[]{:S(2)}, u32[]{:S(2)}) collective-permute-start(bf16[128,2048]{1,0:T(8,128)(2,1)S(1)} %add_convert_fusion), channel_id=1, source_target_pairs={{0,4},{5,1},{4,8},{9,5},{8,12},{13,9},{12,14},{15,13},{14,10},{11,... | collective-permute-start | bytes 1572872 | tf_op jit(solution)/shard_map/ppermute | solution.py:261
  81.6 1.5 %visit.12 = bf16[128,2048]{1,0:T(8,128)(2,1)S(1)} custom-call(s32[1,16]{1,0:T(1,128)S(1)} %get-tuple-element.24.owners_ref, bf16[2080,128]{1,0:T(8,128)(2,1)S(1)} %collective-permute-done.11.refs_0_, bf16[1,2,2048,768]{3,2,1,0:T(8,128)(2,1)S(1)} %get-tuple-element.25.refs_2_.refs_1_, bf16[1,2,768]{2,1,0:T(2,128)(2,1)S(1)} %get-tuple-element.26.refs_3_.refs_2_, ...), custom_call_target="tpu_custom_call" | custom-call | flops 1207959552 | bytes 786432 | tf_op jit(solution)/shard_map/visit/pallas_call | solution.py:209
  83.2 0.1 collective-permute-start.12
  83.3 2.7 %visit.9 = (f32[128,2048]{1,0:T(8,128)S(1)}, bf16[128,2048]{1,0:T(8,128)(2,1)S(1)}) custom-call(s32[1,16]{1,0:T(1,128)S(1)} %get-tuple-element.24.owners_ref, bf16[2080,128]{1,0:T(8,128)(2,1)S(1)} %packed.1.refs_0_, bf16[2080,128]{1,0:T(8,128)(2,1)S(1)} %collective-permute-done.refs_1_, bf16[1,2,2048,768]{3,2,1,0:T(8,128)(2,1)S(1)} %get-tuple-element.25.refs_2_.refs_1_, ...), custom_call_target="tpu_custom_call" | custom-call | flops 2415919104 | bytes 1572864 | tf_op jit(solution)/shard_map/visit/pallas_call | solution.py:209
  85.9 0.6 collective-permute-start.1
  86.5 2.7 %visit.10 = (f32[128,2048]{1,0:T(8,128)S(1)}, bf16[128,2048]{1,0:T(8,128)(2,1)S(1)}) custom-call(s32[1,16]{1,0:T(1,128)S(1)} %get-tuple-element.24.owners_ref, bf16[2080,128]{1,0:T(8,128)(2,1)S(1)} %collective-permute-done.2.refs_0_, bf16[2080,128]{1,0:T(8,128)(2,1)S(1)} %collective-permute-done.3.refs_1_, ...), custom_call_target="tpu_custom_call" | custom-call | flops 2415919104 | bytes 1572864 | tf_op jit(solution)/shard_map/visit/pallas_call | solution.py:209
  89.2 0.1 collective-permute-start.4
  89.3 1.5 %visit.11 = f32[128,2048]{1,0:T(8,128)S(1)} custom-call(s32[1,16]{1,0:T(1,128)S(1)} %get-tuple-element.24.owners_ref, bf16[2080,128]{1,0:T(8,128)(2,1)S(1)} %collective-permute-done.10.refs_0_, bf16[1,2,2048,768]{3,2,1,0:T(8,128)(2,1)S(1)} %get-tuple-element.25.refs_2_.refs_1_, bf16[1,2,768]{2,1,0:T(2,128)(2,1)S(1)} %get-tuple-element.26.refs_3_.refs_2_, ...), custom_call_target="tpu_custom_call" | custom-call | flops 1207959552 | bytes 786432 | tf_op jit(solution)/shard_map/visit/pallas_call | solution.py:209
  90.8 0.1 fusion.1
  90.9 1.6 %collective-permute-start.28 = (bf16[56,2048]{1,0:T(8,128)(2,1)S(1)}, bf16[56,2048]{1,0:T(8,128)(2,1)S(1)}, u32[]{:S(2)}, u32[]{:S(2)}) collective-permute-start(bf16[56,2048]{1,0:T(8,128)(2,1)S(1)} %fusion.1), channel_id=1, source_target_pairs={{0,4},{5,1},{4,8},{9,5},{8,12},{13,9},{12,14},{15,13},{14,10},{11,... | collective-permute-start | bytes 688136 | tf_op jit(solution)/shard_map/ppermute | solution.py:266
  92.6 1.6 %collective-permute-start.32 = (bf16[32,2048]{1,0:T(8,128)(2,1)S(1)}, bf16[32,2048]{1,0:T(8,128)(2,1)S(1)}, u32[]{:S(2)}, u32[]{:S(2)}) collective-permute-start(bf16[32,2048]{1,0:T(8,128)(2,1)S(1)} %fusion.5), channel_id=1, source_target_pairs={{0,4},{5,1},{4,8},{9,5},{8,12},{13,9},{12,14},{15,13},{14,10},{11,... | collective-permute-start | bytes 393224 | tf_op jit(solution)/shard_map/ppermute | solution.py:266
  94.2 0.1 fusion.3
  94.3 1.6 %collective-permute-start.30 = (bf16[40,2048]{1,0:T(8,128)(2,1)S(1)}, bf16[40,2048]{1,0:T(8,128)(2,1)S(1)}, u32[]{:S(2)}, u32[]{:S(2)}) collective-permute-start(bf16[40,2048]{1,0:T(8,128)(2,1)S(1)} %fusion.3), channel_id=1, source_target_pairs={{0,4},{5,1},{4,8},{9,5},{8,12},{13,9},{12,14},{15,13},{14,10},{11,... | collective-permute-start | bytes 491528 | tf_op jit(solution)/shard_map/ppermute | solution.py:266
  95.9 2.5 %collective-permute-done.32 = bf16[32,2048]{1,0:T(8,128)(2,1)S(1)} collective-permute-done((bf16[32,2048]{1,0:T(8,128)(2,1)S(1)}, bf16[32,2048]{1,0:T(8,128)(2,1)S(1)}, u32[]{:S(2)}, u32[]{:S(2)}) %collective-permute-start.32) | collective-permute-done | bytes 131104 | tf_op jit(solution)/shard_map/ppermute | solution.py:266
  98.4 1.6 %collective-permute-start.33 = (bf16[32,2048]{1,0:T(8,128)(2,1)S(1)}, bf16[32,2048]{1,0:T(8,128)(2,1)S(1)}, u32[]{:S(2)}, u32[]{:S(2)}) collective-permute-start(bf16[32,2048]{1,0:T(8,128)(2,1)S(1)} %add_convert_fusion.10), channel_id=1, source_target_pairs={{0,4},{5,1},{4,8},{9,5},{8,12},{13,9},{12,14},{15,13},{14,10},{11,... | collective-permute-start | bytes 393224 | tf_op jit(solution)/shard_map/ppermute | solution.py:266
  100.1 0.1 collective-permute-done.30
  100.1 0.1 add_convert_fusion.8
  100.2 1.6 %collective-permute-start.31 = (bf16[40,2048]{1,0:T(8,128)(2,1)S(1)}, bf16[40,2048]{1,0:T(8,128)(2,1)S(1)}, u32[]{:S(2)}, u32[]{:S(2)}) collective-permute-start(bf16[40,2048]{1,0:T(8,128)(2,1)S(1)} %add_convert_fusion.8), channel_id=1, source_target_pairs={{0,4},{5,1},{4,8},{9,5},{8,12},{13,9},{12,14},{15,13},{14,10},{11,... | collective-permute-start | bytes 491528 | tf_op jit(solution)/shard_map/ppermute | solution.py:266
  101.8 0.1 add_convert_fusion.6
  101.9 1.6 %collective-permute-start.29 = (bf16[56,2048]{1,0:T(8,128)(2,1)S(1)}, bf16[56,2048]{1,0:T(8,128)(2,1)S(1)}, u32[]{:S(2)}, u32[]{:S(2)}) collective-permute-start(bf16[56,2048]{1,0:T(8,128)(2,1)S(1)} %add_convert_fusion.6), channel_id=1, source_target_pairs={{0,4},{5,1},{4,8},{9,5},{8,12},{13,9},{12,14},{15,13},{14,10},{11,... | collective-permute-start | bytes 688136 | tf_op jit(solution)/shard_map/ppermute | solution.py:266
  103.6 2.0 %collective-permute-done.31 = bf16[40,2048]{1,0:T(8,128)(2,1)S(1)} collective-permute-done((bf16[40,2048]{1,0:T(8,128)(2,1)S(1)}, bf16[40,2048]{1,0:T(8,128)(2,1)S(1)}, u32[]{:S(2)}, u32[]{:S(2)}) %collective-permute-start.31) | collective-permute-done | bytes 163872 | tf_op jit(solution)/shard_map/ppermute | solution.py:266
  105.6 0.1 add_convert_fusion.7
  105.6 2.4 %collective-permute-done.29 = bf16[56,2048]{1,0:T(8,128)(2,1)S(1)} collective-permute-done((bf16[56,2048]{1,0:T(8,128)(2,1)S(1)}, bf16[56,2048]{1,0:T(8,128)(2,1)S(1)}, u32[]{:S(2)}, u32[]{:S(2)}) %collective-permute-start.29) | collective-permute-done | bytes 229408 | tf_op jit(solution)/shard_map/ppermute | solution.py:266
  108.0 0.1 add_convert_fusion.5
  108.1 0.8 pad_maximum_fusion
  (30 shorter events, 0.2 us)
Async XLA Ops:
  1.3 10.3 %collective-permute-start.5 = (bf16[2080,128]{1,0:T(8,128)(2,1)S(1)}, bf16[2080,128]{1,0:T(8,128)(2,1)S(1)}, u32[]{:S(2)}, u32[]{:S(2)}) collective-permute-start(bf16[2080,128]{1,0:T(8,128)(2,1)S(1)} %packed.1.refs_0_), channel_id=1, source_target_pairs={{0,4},{5,1},{4,8},{9,5},{8,12},{13,9},{12,14},{15,13},{14,10},{11,... | collective-permute-start | bytes 1597448 | tf_op jit(solution)/shard_map/ppermute | solution.py:237
  11.6 5.9 %collective-permute-start.21 = (bf16[2080,128]{1,0:T(8,128)(2,1)S(1)}, bf16[2080,128]{1,0:T(8,128)(2,1)S(1)}, u32[]{:S(2)}, u32[]{:S(2)}) collective-permute-start(bf16[2080,128]{1,0:T(8,128)(2,1)S(1)} %collective-permute-done.5.refs_0_), channel_id=1, source_target_pairs={{0,1},{1,0},{2,3},{3,2},{4,5},{5,4},{6,7},{7,6},{8,9},{9,8},{10,11... | collective-permute-start | bytes 1597448 | tf_op jit(solution)/shard_map/ppermute | solution.py:237
  15.4 9.3 %collective-permute-start.6 = (bf16[2080,128]{1,0:T(8,128)(2,1)S(1)}, bf16[2080,128]{1,0:T(8,128)(2,1)S(1)}, u32[]{:S(2)}, u32[]{:S(2)}) collective-permute-start(bf16[2080,128]{1,0:T(8,128)(2,1)S(1)} %collective-permute-done.5.refs_0_), channel_id=1, source_target_pairs={{0,4},{5,1},{4,8},{9,5},{8,12},{13,9},{12,14},{15,13},{14,10},{11,... | collective-permute-start | bytes 1597448 | tf_op jit(solution)/shard_map/ppermute | solution.py:237
  20.2 6.6 %collective-permute-start.22 = (bf16[128,2048]{1,0:T(8,128)(2,1)S(1)}, bf16[128,2048]{1,0:T(8,128)(2,1)S(1)}, u32[]{:S(2)}, u32[]{:S(2)}) collective-permute-start(bf16[128,2048]{1,0:T(8,128)(2,1)S(1)} %get-tuple-element.42), channel_id=1, source_target_pairs={{0,1},{1,0},{2,3},{3,2},{4,5},{5,4},{6,7},{7,6},{8,9},{9,8},{10,11... | collective-permute-start | bytes 1572872 | tf_op jit(solution)/shard_map/ppermute | solution.py:237
  24.7 3.8 %collective-permute-start.19 = (bf16[2080,128]{1,0:T(8,128)(2,1)S(1)}, bf16[2080,128]{1,0:T(8,128)(2,1)S(1)}, u32[]{:S(2)}, u32[]{:S(2)}) collective-permute-start(bf16[2080,128]{1,0:T(8,128)(2,1)S(1)} %collective-permute-done.6.refs_0_), channel_id=1, source_target_pairs={{0,1},{1,0},{2,3},{3,2},{4,5},{5,4},{6,7},{7,6},{8,9},{9,8},{10,11... | collective-permute-start | bytes 1597448 | tf_op jit(solution)/shard_map/ppermute | solution.py:237
  24.7 9.3 %collective-permute-start.7 = (bf16[2080,128]{1,0:T(8,128)(2,1)S(1)}, bf16[2080,128]{1,0:T(8,128)(2,1)S(1)}, u32[]{:S(2)}, u32[]{:S(2)}) collective-permute-start(bf16[2080,128]{1,0:T(8,128)(2,1)S(1)} %collective-permute-done.6.refs_0_), channel_id=1, source_target_pairs={{0,4},{5,1},{4,8},{9,5},{8,12},{13,9},{12,14},{15,13},{14,10},{11,... | collective-permute-start | bytes 1597448 | tf_op jit(solution)/shard_map/ppermute | solution.py:237
  27.0 12.7 %collective-permute-start.23 = (bf16[128,2048]{1,0:T(8,128)(2,1)S(1)}, bf16[128,2048]{1,0:T(8,128)(2,1)S(1)}, u32[]{:S(2)}, u32[]{:S(2)}) collective-permute-start(bf16[128,2048]{1,0:T(8,128)(2,1)S(1)} %add_convert_fusion.4), channel_id=1, source_target_pairs={{0,4},{5,1},{4,8},{9,5},{8,12},{13,9},{12,14},{15,13},{14,10},{11,... | collective-permute-start | bytes 1572872 | tf_op jit(solution)/shard_map/ppermute | solution.py:261
  31.3 8.4 %collective-permute-start.20 = (bf16[128,2048]{1,0:T(8,128)(2,1)S(1)}, bf16[128,2048]{1,0:T(8,128)(2,1)S(1)}, u32[]{:S(2)}, u32[]{:S(2)}) collective-permute-start(bf16[128,2048]{1,0:T(8,128)(2,1)S(1)} %get-tuple-element.40), channel_id=1, source_target_pairs={{0,1},{1,0},{2,3},{3,2},{4,5},{5,4},{6,7},{7,6},{8,9},{9,8},{10,11... | collective-permute-start | bytes 1572872 | tf_op jit(solution)/shard_map/ppermute | solution.py:237
  34.0 7.9 %collective-permute-start.17 = (bf16[2080,128]{1,0:T(8,128)(2,1)S(1)}, bf16[2080,128]{1,0:T(8,128)(2,1)S(1)}, u32[]{:S(2)}, u32[]{:S(2)}) collective-permute-start(bf16[2080,128]{1,0:T(8,128)(2,1)S(1)} %collective-permute-done.7.refs_0_), channel_id=1, source_target_pairs={{0,1},{1,0},{2,3},{3,2},{4,5},{5,4},{6,7},{7,6},{8,9},{9,8},{10,11... | collective-permute-start | bytes 1597448 | tf_op jit(solution)/shard_map/ppermute | solution.py:237
  34.0 11.3 %collective-permute-start.8 = (bf16[2080,128]{1,0:T(8,128)(2,1)S(1)}, bf16[2080,128]{1,0:T(8,128)(2,1)S(1)}, u32[]{:S(2)}, u32[]{:S(2)}) collective-permute-start(bf16[2080,128]{1,0:T(8,128)(2,1)S(1)} %collective-permute-done.7.refs_0_), channel_id=1, source_target_pairs={{0,4},{5,1},{4,8},{9,5},{8,12},{13,9},{12,14},{15,13},{14,10},{11,... | collective-permute-start | bytes 1597448 | tf_op jit(solution)/shard_map/ppermute | solution.py:237
  39.8 11.1 %collective-permute-start.24 = (bf16[128,2048]{1,0:T(8,128)(2,1)S(1)}, bf16[128,2048]{1,0:T(8,128)(2,1)S(1)}, u32[]{:S(2)}, u32[]{:S(2)}) collective-permute-start(bf16[128,2048]{1,0:T(8,128)(2,1)S(1)} %add_convert_fusion.3), channel_id=1, source_target_pairs={{0,4},{5,1},{4,8},{9,5},{8,12},{13,9},{12,14},{15,13},{14,10},{11,... | collective-permute-start | bytes 1572872 | tf_op jit(solution)/shard_map/ppermute | solution.py:261
  44.6 6.3 %collective-permute-start.18 = (bf16[128,2048]{1,0:T(8,128)(2,1)S(1)}, bf16[128,2048]{1,0:T(8,128)(2,1)S(1)}, u32[]{:S(2)}, u32[]{:S(2)}) collective-permute-start(bf16[128,2048]{1,0:T(8,128)(2,1)S(1)} %get-tuple-element.38), channel_id=1, source_target_pairs={{0,1},{1,0},{2,3},{3,2},{4,5},{5,4},{6,7},{7,6},{8,9},{9,8},{10,11... | collective-permute-start | bytes 1572872 | tf_op jit(solution)/shard_map/ppermute | solution.py:237
  45.3 8.0 %collective-permute-start.15 = (bf16[2080,128]{1,0:T(8,128)(2,1)S(1)}, bf16[2080,128]{1,0:T(8,128)(2,1)S(1)}, u32[]{:S(2)}, u32[]{:S(2)}) collective-permute-start(bf16[2080,128]{1,0:T(8,128)(2,1)S(1)} %collective-permute-done.8.refs_0_), channel_id=1, source_target_pairs={{0,1},{1,0},{2,3},{3,2},{4,5},{5,4},{6,7},{7,6},{8,9},{9,8},{10,11... | collective-permute-start | bytes 1597448 | tf_op jit(solution)/shard_map/ppermute | solution.py:237
  45.3 11.3 %collective-permute-start.9 = (bf16[2080,128]{1,0:T(8,128)(2,1)S(1)}, bf16[2080,128]{1,0:T(8,128)(2,1)S(1)}, u32[]{:S(2)}, u32[]{:S(2)}) collective-permute-start(bf16[2080,128]{1,0:T(8,128)(2,1)S(1)} %collective-permute-done.8.refs_0_), channel_id=1, source_target_pairs={{0,4},{5,1},{4,8},{9,5},{8,12},{13,9},{12,14},{15,13},{14,10},{11,... | collective-permute-start | bytes 1597448 | tf_op jit(solution)/shard_map/ppermute | solution.py:237
  51.2 13.3 %collective-permute-start.25 = (bf16[128,2048]{1,0:T(8,128)(2,1)S(1)}, bf16[128,2048]{1,0:T(8,128)(2,1)S(1)}, u32[]{:S(2)}, u32[]{:S(2)}) collective-permute-start(bf16[128,2048]{1,0:T(8,128)(2,1)S(1)} %add_convert_fusion.2), channel_id=1, source_target_pairs={{0,4},{5,1},{4,8},{9,5},{8,12},{13,9},{12,14},{15,13},{14,10},{11,... | collective-permute-start | bytes 1572872 | tf_op jit(solution)/shard_map/ppermute | solution.py:261
  56.0 8.5 %collective-permute-start.16 = (bf16[128,2048]{1,0:T(8,128)(2,1)S(1)}, bf16[128,2048]{1,0:T(8,128)(2,1)S(1)}, u32[]{:S(2)}, u32[]{:S(2)}) collective-permute-start(bf16[128,2048]{1,0:T(8,128)(2,1)S(1)} %get-tuple-element.36), channel_id=1, source_target_pairs={{0,1},{1,0},{2,3},{3,2},{4,5},{5,4},{6,7},{7,6},{8,9},{9,8},{10,11... | collective-permute-start | bytes 1572872 | tf_op jit(solution)/shard_map/ppermute | solution.py:237
  56.7 10.7 %collective-permute-start.13 = (bf16[2080,128]{1,0:T(8,128)(2,1)S(1)}, bf16[2080,128]{1,0:T(8,128)(2,1)S(1)}, u32[]{:S(2)}, u32[]{:S(2)}) collective-permute-start(bf16[2080,128]{1,0:T(8,128)(2,1)S(1)} %collective-permute-done.9.refs_0_), channel_id=1, source_target_pairs={{0,1},{1,0},{2,3},{3,2},{4,5},{5,4},{6,7},{7,6},{8,9},{9,8},{10,11... | collective-permute-start | bytes 1597448 | tf_op jit(solution)/shard_map/ppermute | solution.py:237
  56.7 17.5 %collective-permute-start.2 = (bf16[2080,128]{1,0:T(8,128)(2,1)S(1)}, bf16[2080,128]{1,0:T(8,128)(2,1)S(1)}, u32[]{:S(2)}, u32[]{:S(2)}) collective-permute-start(bf16[2080,128]{1,0:T(8,128)(2,1)S(1)} %packed.1.refs_0_), channel_id=1, source_target_pairs={{4,0},{1,5},{8,4},{5,9},{12,8},{9,13},{14,12},{13,15},{10,14},{15,... | collective-permute-start | bytes 1597448 | tf_op jit(solution)/shard_map/ppermute | solution.py:237
  58.7 15.0 %collective-permute-start.10 = (bf16[2080,128]{1,0:T(8,128)(2,1)S(1)}, bf16[2080,128]{1,0:T(8,128)(2,1)S(1)}, u32[]{:S(2)}, u32[]{:S(2)}) collective-permute-start(bf16[2080,128]{1,0:T(8,128)(2,1)S(1)} %collective-permute-done.9.refs_0_), channel_id=1, source_target_pairs={{0,4},{5,1},{4,8},{9,5},{8,12},{13,9},{12,14},{15,13},{14,10},{11,... | collective-permute-start | bytes 1597448 | tf_op jit(solution)/shard_map/ppermute | solution.py:237
  64.7 14.6 %collective-permute-start.26 = (bf16[128,2048]{1,0:T(8,128)(2,1)S(1)}, bf16[128,2048]{1,0:T(8,128)(2,1)S(1)}, u32[]{:S(2)}, u32[]{:S(2)}) collective-permute-start(bf16[128,2048]{1,0:T(8,128)(2,1)S(1)} %add_convert_fusion.1), channel_id=1, source_target_pairs={{0,4},{5,1},{4,8},{9,5},{8,12},{13,9},{12,14},{15,13},{14,10},{11,... | collective-permute-start | bytes 1572872 | tf_op jit(solution)/shard_map/ppermute | solution.py:261
  70.0 9.3 %collective-permute-start.14 = (bf16[128,2048]{1,0:T(8,128)(2,1)S(1)}, bf16[128,2048]{1,0:T(8,128)(2,1)S(1)}, u32[]{:S(2)}, u32[]{:S(2)}) collective-permute-start(bf16[128,2048]{1,0:T(8,128)(2,1)S(1)} %get-tuple-element.34), channel_id=1, source_target_pairs={{0,1},{1,0},{2,3},{3,2},{4,5},{5,4},{6,7},{7,6},{8,9},{9,8},{10,11... | collective-permute-start | bytes 1572872 | tf_op jit(solution)/shard_map/ppermute | solution.py:237
  73.7 8.0 %collective-permute-start.11 = (bf16[2080,128]{1,0:T(8,128)(2,1)S(1)}, bf16[2080,128]{1,0:T(8,128)(2,1)S(1)}, u32[]{:S(2)}, u32[]{:S(2)}) collective-permute-start(bf16[2080,128]{1,0:T(8,128)(2,1)S(1)} %collective-permute-done.10.refs_0_), channel_id=1, source_target_pairs={{0,1},{1,0},{2,3},{3,2},{4,5},{5,4},{6,7},{7,6},{8,9},{9,8},{10,11... | collective-permute-start | bytes 1597448 | tf_op jit(solution)/shard_map/ppermute | solution.py:237
  73.7 9.6 %collective-permute-start = (bf16[2080,128]{1,0:T(8,128)(2,1)S(1)}, bf16[2080,128]{1,0:T(8,128)(2,1)S(1)}, u32[]{:S(2)}, u32[]{:S(2)}) collective-permute-start(bf16[2080,128]{1,0:T(8,128)(2,1)S(1)} %packed.1.refs_0_), channel_id=1, source_target_pairs={{0,1},{1,0},{2,3},{3,2},{4,5},{5,4},{6,7},{7,6},{8,9},{9,8},{10,11... | collective-permute-start | bytes 1597448 | tf_op jit(solution)/shard_map/ppermute | solution.py:237
  74.2 12.3 %collective-permute-start.3 = (bf16[2080,128]{1,0:T(8,128)(2,1)S(1)}, bf16[2080,128]{1,0:T(8,128)(2,1)S(1)}, u32[]{:S(2)}, u32[]{:S(2)}) collective-permute-start(bf16[2080,128]{1,0:T(8,128)(2,1)S(1)} %collective-permute-done.2.refs_0_), channel_id=1, source_target_pairs={{0,1},{1,0},{2,3},{3,2},{4,5},{5,4},{6,7},{7,6},{8,9},{9,8},{10,11... | collective-permute-start | bytes 1597448 | tf_op jit(solution)/shard_map/ppermute | solution.py:237
  79.5 11.3 %collective-permute-start.27 = (bf16[128,2048]{1,0:T(8,128)(2,1)S(1)}, bf16[128,2048]{1,0:T(8,128)(2,1)S(1)}, u32[]{:S(2)}, u32[]{:S(2)}) collective-permute-start(bf16[128,2048]{1,0:T(8,128)(2,1)S(1)} %add_convert_fusion), channel_id=1, source_target_pairs={{0,4},{5,1},{4,8},{9,5},{8,12},{13,9},{12,14},{15,13},{14,10},{11,... | collective-permute-start | bytes 1572872 | tf_op jit(solution)/shard_map/ppermute | solution.py:261
  83.2 7.6 %collective-permute-start.12 = (bf16[128,2048]{1,0:T(8,128)(2,1)S(1)}, bf16[128,2048]{1,0:T(8,128)(2,1)S(1)}, u32[]{:S(2)}, u32[]{:S(2)}) collective-permute-start(bf16[128,2048]{1,0:T(8,128)(2,1)S(1)} %visit.12), channel_id=1, source_target_pairs={{0,1},{1,0},{2,3},{3,2},{4,5},{5,4},{6,7},{7,6},{8,9},{9,8},{10,11... | collective-permute-start | bytes 1572872 | tf_op jit(solution)/shard_map/ppermute | solution.py:237
  85.9 17.6 %collective-permute-start.1 = (bf16[128,2048]{1,0:T(8,128)(2,1)S(1)}, bf16[128,2048]{1,0:T(8,128)(2,1)S(1)}, u32[]{:S(2)}, u32[]{:S(2)}) collective-permute-start(bf16[128,2048]{1,0:T(8,128)(2,1)S(1)} %get-tuple-element.30), channel_id=1, source_target_pairs={{0,1},{1,0},{2,3},{3,2},{4,5},{5,4},{6,7},{7,6},{8,9},{9,8},{10,11... | collective-permute-start | bytes 1572872 | tf_op jit(solution)/shard_map/ppermute | solution.py:237
  89.2 6.7 %collective-permute-start.4 = (bf16[128,2048]{1,0:T(8,128)(2,1)S(1)}, bf16[128,2048]{1,0:T(8,128)(2,1)S(1)}, u32[]{:S(2)}, u32[]{:S(2)}) collective-permute-start(bf16[128,2048]{1,0:T(8,128)(2,1)S(1)} %get-tuple-element.32), channel_id=1, source_target_pairs={{0,1},{1,0},{2,3},{3,2},{4,5},{5,4},{6,7},{7,6},{8,9},{9,8},{10,11... | collective-permute-start | bytes 1572872 | tf_op jit(solution)/shard_map/ppermute | solution.py:237
  90.9 10.9 %collective-permute-start.28 = (bf16[56,2048]{1,0:T(8,128)(2,1)S(1)}, bf16[56,2048]{1,0:T(8,128)(2,1)S(1)}, u32[]{:S(2)}, u32[]{:S(2)}) collective-permute-start(bf16[56,2048]{1,0:T(8,128)(2,1)S(1)} %fusion.1), channel_id=1, source_target_pairs={{0,4},{5,1},{4,8},{9,5},{8,12},{13,9},{12,14},{15,13},{14,10},{11,... | collective-permute-start | bytes 688136 | tf_op jit(solution)/shard_map/ppermute | solution.py:266
  92.6 5.8 %collective-permute-start.32 = (bf16[32,2048]{1,0:T(8,128)(2,1)S(1)}, bf16[32,2048]{1,0:T(8,128)(2,1)S(1)}, u32[]{:S(2)}, u32[]{:S(2)}) collective-permute-start(bf16[32,2048]{1,0:T(8,128)(2,1)S(1)} %fusion.5), channel_id=1, source_target_pairs={{0,4},{5,1},{4,8},{9,5},{8,12},{13,9},{12,14},{15,13},{14,10},{11,... | collective-permute-start | bytes 393224 | tf_op jit(solution)/shard_map/ppermute | solution.py:266
  94.3 5.8 %collective-permute-start.30 = (bf16[40,2048]{1,0:T(8,128)(2,1)S(1)}, bf16[40,2048]{1,0:T(8,128)(2,1)S(1)}, u32[]{:S(2)}, u32[]{:S(2)}) collective-permute-start(bf16[40,2048]{1,0:T(8,128)(2,1)S(1)} %fusion.3), channel_id=1, source_target_pairs={{0,4},{5,1},{4,8},{9,5},{8,12},{13,9},{12,14},{15,13},{14,10},{11,... | collective-permute-start | bytes 491528 | tf_op jit(solution)/shard_map/ppermute | solution.py:266
  98.4 5.1 %collective-permute-start.33 = (bf16[32,2048]{1,0:T(8,128)(2,1)S(1)}, bf16[32,2048]{1,0:T(8,128)(2,1)S(1)}, u32[]{:S(2)}, u32[]{:S(2)}) collective-permute-start(bf16[32,2048]{1,0:T(8,128)(2,1)S(1)} %add_convert_fusion.10), channel_id=1, source_target_pairs={{0,4},{5,1},{4,8},{9,5},{8,12},{13,9},{12,14},{15,13},{14,10},{11,... | collective-permute-start | bytes 393224 | tf_op jit(solution)/shard_map/ppermute | solution.py:266
  100.2 5.4 %collective-permute-start.31 = (bf16[40,2048]{1,0:T(8,128)(2,1)S(1)}, bf16[40,2048]{1,0:T(8,128)(2,1)S(1)}, u32[]{:S(2)}, u32[]{:S(2)}) collective-permute-start(bf16[40,2048]{1,0:T(8,128)(2,1)S(1)} %add_convert_fusion.8), channel_id=1, source_target_pairs={{0,4},{5,1},{4,8},{9,5},{8,12},{13,9},{12,14},{15,13},{14,10},{11,... | collective-permute-start | bytes 491528 | tf_op jit(solution)/shard_map/ppermute | solution.py:266
  101.9 6.1 %collective-permute-start.29 = (bf16[56,2048]{1,0:T(8,128)(2,1)S(1)}, bf16[56,2048]{1,0:T(8,128)(2,1)S(1)}, u32[]{:S(2)}, u32[]{:S(2)}) collective-permute-start(bf16[56,2048]{1,0:T(8,128)(2,1)S(1)} %add_convert_fusion.6), channel_id=1, source_target_pairs={{0,4},{5,1},{4,8},{9,5},{8,12},{13,9},{12,14},{15,13},{14,10},{11,... | collective-permute-start | bytes 688136 | tf_op jit(solution)/shard_map/ppermute | solution.py:266

commit v2 on v1

--- a/solution.py
+++ b/solution.py
@@ -75,8 +75,20 @@
     return pltpu.with_memory_space_constraint(array, pltpu.HBM)
 
 
-def packed_kernel(tokens_hbm, gain_hbm, ids_hbm, gates_hbm, *refs):
-    out_ref, tokens, gain, ids, gates, sems = refs
+def write_rows(tokens, gain, out_ref):
+    tok_rows, model_width = tokens.shape
+    for top in range(0, tok_rows, TALL):
+        values = tokens[top : top + TALL, :].astype(jnp.float32)
+        row_scale = lax.rsqrt(jnp.mean(values * values, axis=1, keepdims=True) + 1e-06)
+        normed = (values * row_scale * gain[...]).astype(jnp.bfloat16)
+        for side in range(0, model_width, LANES):
+            row = top * model_width // LANES + side // LANES * TALL
+            out_ref[row : row + TALL, :] = normed[:, side : side + LANES]
+
+
+def packed_kernel(
+    tokens_hbm, gain_hbm, ids_hbm, gates_hbm, out_ref, table_ref, tokens, gain, ids, gates, sems
+):
     moves = [
         pltpu.make_async_copy(source, target, sems.at[i])
         for i, (source, target) in enumerate(
@@ -85,28 +97,21 @@
     ]
     for move in moves:
         move.start()
-    tok_rows, model_width = tokens.shape
     moves[0].wait()
     moves[1].wait()
     weights = gates[...] / jnp.sum(gates[...], axis=0, keepdims=True)
-    experts = (out_ref.shape[0] - tok_rows * model_width // LANES) // 2
-    label = lax.broadcasted_iota(jnp.int32, (experts, tok_rows), 0)
-    table = jnp.zeros((experts, tok_rows), jnp.float32)
+    experts = table_ref.shape[0] // 2
+    label = lax.broadcasted_iota(jnp.int32, (experts, tokens.shape[0]), 0)
+    table = jnp.zeros(label.shape, jnp.float32)
     for k in range(ids.shape[0]):
         table += jnp.where(label == ids[k : k + 1, :], weights[k : k + 1, :], 0.0)
     high = table.astype(jnp.bfloat16)
-    low = (table - high.astype(jnp.float32)).astype(jnp.bfloat16)
-    out_ref[-2 * experts : -experts, :] = high
-    out_ref[-experts:, :] = low
+    table_ref[:experts, :] = high
+    table_ref[experts:, :] = (table - high.astype(jnp.float32)).astype(jnp.bfloat16)
+    out_ref[-2 * experts :, :] = table_ref[...]
     moves[2].wait()
     moves[3].wait()
-    for top in range(0, tok_rows, TALL):
-        values = tokens[top : top + TALL, :].astype(jnp.float32)
-        row_scale = lax.rsqrt(jnp.mean(values * values, axis=1, keepdims=True) + 1e-06)
-        normed = (values * row_scale * gain[...]).astype(jnp.bfloat16)
-        for side in range(0, model_width, LANES):
-            row = top * model_width // LANES + side // LANES * TALL
-            out_ref[row : row + TALL, :] = normed[:, side : side + LANES]
+    write_rows(tokens, gain, out_ref)
 
 
 def packed(tokens, norm_gain, expert_ids, gate_weights, experts):
@@ -115,9 +120,11 @@
     size = tok_rows * model_width // LANES + 2 * experts
     return pl.pallas_call(
         packed_kernel,
-        out_shape=jax.ShapeDtypeStruct((size, LANES), jnp.bfloat16),
+        out_shape=tuple(
+            jax.ShapeDtypeStruct((rows, LANES), jnp.bfloat16) for rows in (size, 2 * experts)
+        ),
         in_specs=[pl.BlockSpec(memory_space=pltpu.HBM)] * 4,
-        out_specs=pl.BlockSpec(memory_space=pltpu.VMEM),
+        out_specs=(pl.BlockSpec(memory_space=pltpu.VMEM),) * 2,
         scratch_shapes=[
             pltpu.VMEM((tok_rows, model_width), jnp.bfloat16),
             pltpu.VMEM((1, model_width), jnp.float32),
@@ -128,6 +135,23 @@
         compiler_params=pltpu.CompilerParams(vmem_limit_bytes=SMALL),
         name="packed",
     )(*map(in_hbm, (tokens, norm_gain[None, :], expert_ids.T, gate_weights.T)))
+
+
+def mended_kernel(tokens_ref, table_ref, gain_ref, out_ref):
+    out_ref[-table_ref.shape[0] :, :] = table_ref[...]
+    write_rows(tokens_ref, gain_ref, out_ref)
+
+
+def mended(tokens, table, gain):
+    size = tokens.size // LANES + table.shape[0]
+    return pl.pallas_call(
+        mended_kernel,
+        out_shape=jax.ShapeDtypeStruct((size, LANES), jnp.bfloat16),
+        in_specs=[pl.BlockSpec(memory_space=pltpu.VMEM)] * 3,
+        out_specs=pl.BlockSpec(memory_space=pltpu.VMEM),
+        compiler_params=pltpu.CompilerParams(vmem_limit_bytes=SMALL),
+        name="mended",
+    )(tokens, table, gain)
 
 
 def loaded_kernel(count, *refs):
@@ -236,15 +260,20 @@
     def moved(value, pairs):
         return lax.ppermute(value, "tok", pairs)
 
-    block = packed(tokens, norm_gain, expert_ids, gate_weights, experts)
-    blocks = loaded(owner_map[None, :], in_q, in_scale, down_q, down_scale)
+    raw = moved(tokens, ring)
+    block, table = packed(tokens, norm_gain, expert_ids, gate_weights, experts)
+    table = moved(table, ring)
+    gain, *blocks = loaded(
+        norm_gain[None, :], owner_map[None, :], in_q, in_scale, down_q, down_scale
+    )
     back = moved(block, [(target, source) for source, target in ring])
+    near = mended(raw, table, gain)
     parts = []
     for step in range(chips):
-        here = block if step < chips - 1 else back
+        here = {0: block, chips - 1: back}.get(step, near)
         other = moved(here, swap)
-        if step < chips - 2:
-            block = moved(block, ring)
+        if 0 < step < chips - 2:
+            near = moved(near, ring)
         if step == chips - 2:
             (part,) = visit((here,), (jnp.float32,), *blocks)
             (lent,) = visit((other,), (jnp.bfloat16,), *blocks)

time: 109 us -> 105 us (0.963)
  waiting for transfers between devices: 43.8 us -> 37.4 us
  starting transfers between devices: 35.6 us -> 37.2 us
    ppermute x23 -> x24, waiting for transfers between devices: 18.9 us -> 12.5 us  [moved(): return lax.ppermute(value, 'tok', pairs)]
    ppermute x23 -> x24, starting transfers between devices: 15.3 us -> 16.9 us  [moved(): return lax.ppermute(value, 'tok', pairs)]
  transfers between devices with their start and end apart: 34 -> 35, of which waited for: 14 -> 14; matrix products, arithmetic and copies ran while one was open for 1% -> 1% of each run, Pallas kernels for 23% -> 26%
where the time goes in v2:
time: 105 us; the launch traced here: 104 us
  waiting for transfers between devices  37.4 us (36%)
  starting transfers between devices  37.2 us (35%)
  Pallas kernels  27.1 us (26%)
  other arithmetic  2.31 us (2%)
    pallas_call x9, Pallas kernels, visit(): pl.pallas_call(functools.partial(visit_kernel, count), out_shape=tuple((j...  21.8 us
    ppermute x5, waiting for transfers between devices, circulated(): total = lax.ppermute(summed(step, slice(None), total), 'tok', ring)  17.9 us
    ppermute x24, starting transfers between devices, moved(): return lax.ppermute(value, 'tok', pairs)  16.9 us
    ppermute x24, waiting for transfers between devices, moved(): return lax.ppermute(value, 'tok', pairs)  12.5 us
    ppermute x5, starting transfers between devices, circulated(): total = lax.ppermute(summed(step, slice(None), total), 'tok', ring)  10.6 us
    ppermute x6, starting transfers between devices, circulated(): totals[name] = lax.ppermute(summed(step, rows, totals[name]), 'tok', ring)  9.73 us
    ppermute x6, waiting for transfers between devices, circulated(): totals[name] = lax.ppermute(summed(step, rows, totals[name]), 'tok', ring)  6.94 us
    pallas_call x1, Pallas kernels, loaded(): pl.pallas_call(functools.partial(loaded_kernel, count), out_shape=tuple((...  3.81 us
  transfers between devices with their start and end apart: 35, of which 14 were waited for; matrix products, arithmetic and copies ran while one was open for 1% of the time, Pallas kernels for 26%

profile of v2, /device:TPU:0, one launch (start us, length us, event | category | flops | bytes accessed | tf_op | source)
XLA Modules:
  0.0 104.3 jit_solution(15202119676651014465)
XLA Ops:
  0.0 3.1 %collective-permute-start.5 = (bf16[128,2048]{1,0:T(8,128)(2,1)}, bf16[128,2048]{1,0:T(8,128)(2,1)S(1)}, u32[]{:S(2)}, u32[]{:S(2)}) collective-permute-start(bf16[128,2048]{1,0:T(8,128)(2,1)} %tokens_hbm.1), channel_id=1, source_target_pairs={{0,4},{5,1},{4,8},{9,5},{8,12},{13,9},{12,14},{15,13},{14,10},{11,... | collective-permute-start | bytes 1572872 | tf_op jit(solution)/shard_map/ppermute | solution.py:261
  3.1 1.3 %packed.1 = (bf16[2080,128]{1,0:T(8,128)(2,1)S(1)}, bf16[32,128]{1,0:T(8,128)(2,1)S(1)}) custom-call(bf16[128,2048]{1,0:T(8,128)(2,1)} %tokens_hbm.1, f32[1,2048]{1,0:T(1,128)} %bitcast.4, s32[8,128]{1,0:T(8,128)} %bitcast.6, f32[8,128]{1,0:T(8,128)} %bitcast.7), custom_call_target="tpu_custom_call" | custom-call | tf_op jit(solution)/shard_map/packed/pallas_call | solution.py:121
  4.4 1.6 %collective-permute-start.6 = (bf16[32,128]{1,0:T(8,128)(2,1)S(1)}, bf16[32,128]{1,0:T(8,128)(2,1)S(1)}, u32[]{:S(2)}, u32[]{:S(2)}) collective-permute-start(bf16[32,128]{1,0:T(8,128)(2,1)S(1)} %get-tuple-element.37), channel_id=1, source_target_pairs={{0,4},{5,1},{4,8},{9,5},{8,12},{13,9},{12,14},{15,13},{14,10},{11,... | collective-permute-start | bytes 24584 | tf_op jit(solution)/shard_map/ppermute | solution.py:261
  6.0 3.8 %loaded.1 = (f32[1,2048]{1,0:T(1,128)S(1)}, s32[1,16]{1,0:T(1,128)S(1)}, bf16[1,2,2048,768]{3,2,1,0:T(8,128)(2,1)S(1)}, bf16[1,2,768]{2,1,0:T(2,128)(2,1)S(1)}, ...) custom-call(f32[1,2048]{1,0:T(1,128)} %bitcast.5, s32[1,16]{1,0:T(1,128)} %bitcast.8, ...), custom_call_target="tpu_custom_call" | custom-call | bytes 9448480 | tf_op jit(solution)/shard_map/loaded/pallas_call | solution.py:171
  9.8 0.6 collective-permute-done.6.table_ref
  10.5 0.2 mended.1.refs_0_
  10.7 0.1 collective-permute-start.22
  10.7 2.1 %collective-permute-start.7 = (bf16[2080,128]{1,0:T(8,128)(2,1)S(1)}, bf16[2080,128]{1,0:T(8,128)(2,1)S(1)}, u32[]{:S(2)}, u32[]{:S(2)}) collective-permute-start(bf16[2080,128]{1,0:T(8,128)(2,1)S(1)} %mended.1.refs_0_), channel_id=1, source_target_pairs={{0,4},{5,1},{4,8},{9,5},{8,12},{13,9},{12,14},{15,13},{14,10},{11,... | collective-permute-start | bytes 1597448 | tf_op jit(solution)/shard_map/ppermute | solution.py:261
  12.9 2.7 %visit.17 = (f32[128,2048]{1,0:T(8,128)S(1)}, bf16[128,2048]{1,0:T(8,128)(2,1)S(1)}) custom-call(s32[1,16]{1,0:T(1,128)S(1)} %get-tuple-element.27.owners_ref, bf16[2080,128]{1,0:T(8,128)(2,1)S(1)} %mended.1.refs_0_, bf16[2080,128]{1,0:T(8,128)(2,1)S(1)} %collective-permute-done.22.refs_1_, bf16[1,2,2048,768]{3,2,1,0:T(8,128)(2,1)S(1)} %get-tuple-element.29.refs_2_.refs_1_, ...), custom_call_target="tpu_custom_call" | custom-call | flops 2415919104 | bytes 1572864 | tf_op jit(solution)/shard_map/visit/pallas_call | solution.py:233
  15.6 0.2 collective-permute-start.23
  15.7 4.3 %collective-permute-done.7.refs_0_ = bf16[2080,128]{1,0:T(8,128)(2,1)S(1)} collective-permute-done((bf16[2080,128]{1,0:T(8,128)(2,1)S(1)}, bf16[2080,128]{1,0:T(8,128)(2,1)S(1)}, u32[]{:S(2)}, u32[]{:S(2)}) %collective-permute-start.7) | collective-permute-done | bytes 532512 | tf_op jit(solution)/shard_map/ppermute | solution.py:261
  20.1 2.1 %collective-permute-start.8 = (bf16[2080,128]{1,0:T(8,128)(2,1)S(1)}, bf16[2080,128]{1,0:T(8,128)(2,1)S(1)}, u32[]{:S(2)}, u32[]{:S(2)}) collective-permute-start(bf16[2080,128]{1,0:T(8,128)(2,1)S(1)} %collective-permute-done.7.refs_0_), channel_id=1, source_target_pairs={{0,4},{5,1},{4,8},{9,5},{8,12},{13,9},{12,14},{15,13},{14,10},{11,... | collective-permute-start | bytes 1597448 | tf_op jit(solution)/shard_map/ppermute | solution.py:261
  22.2 0.1 add_convert_fusion.4
  22.3 1.6 %collective-permute-start.24 = (bf16[128,2048]{1,0:T(8,128)(2,1)S(1)}, bf16[128,2048]{1,0:T(8,128)(2,1)S(1)}, u32[]{:S(2)}, u32[]{:S(2)}) collective-permute-start(bf16[128,2048]{1,0:T(8,128)(2,1)S(1)} %add_convert_fusion.4), channel_id=1, source_target_pairs={{0,4},{5,1},{4,8},{9,5},{8,12},{13,9},{12,14},{15,13},{14,10},{11,... | collective-permute-start | bytes 1572872 | tf_op jit(solution)/shard_map/ppermute | solution.py:290
  23.9 2.7 %visit.16 = (f32[128,2048]{1,0:T(8,128)S(1)}, bf16[128,2048]{1,0:T(8,128)(2,1)S(1)}) custom-call(s32[1,16]{1,0:T(1,128)S(1)} %get-tuple-element.27.owners_ref, bf16[2080,128]{1,0:T(8,128)(2,1)S(1)} %collective-permute-done.7.refs_0_, bf16[2080,128]{1,0:T(8,128)(2,1)S(1)} %collective-permute-done.20.refs_1_, ...), custom_call_target="tpu_custom_call" | custom-call | flops 2415919104 | bytes 1572864 | tf_op jit(solution)/shard_map/visit/pallas_call | solution.py:233
  26.6 0.1 collective-permute-start.21
  26.7 2.7 %collective-permute-done.8.refs_0_ = bf16[2080,128]{1,0:T(8,128)(2,1)S(1)} collective-permute-done((bf16[2080,128]{1,0:T(8,128)(2,1)S(1)}, bf16[2080,128]{1,0:T(8,128)(2,1)S(1)}, u32[]{:S(2)}, u32[]{:S(2)}) %collective-permute-start.8) | collective-permute-done | bytes 532512 | tf_op jit(solution)/shard_map/ppermute | solution.py:261
  29.3 2.1 %collective-permute-start.9 = (bf16[2080,128]{1,0:T(8,128)(2,1)S(1)}, bf16[2080,128]{1,0:T(8,128)(2,1)S(1)}, u32[]{:S(2)}, u32[]{:S(2)}) collective-permute-start(bf16[2080,128]{1,0:T(8,128)(2,1)S(1)} %collective-permute-done.8.refs_0_), channel_id=1, source_target_pairs={{0,4},{5,1},{4,8},{9,5},{8,12},{13,9},{12,14},{15,13},{14,10},{11,... | collective-permute-start | bytes 1597448 | tf_op jit(solution)/shard_map/ppermute | solution.py:261
  31.4 3.5 %collective-permute-done.24 = bf16[128,2048]{1,0:T(8,128)(2,1)S(1)} collective-permute-done((bf16[128,2048]{1,0:T(8,128)(2,1)S(1)}, bf16[128,2048]{1,0:T(8,128)(2,1)S(1)}, u32[]{:S(2)}, u32[]{:S(2)}) %collective-permute-start.24) | collective-permute-done | bytes 524320 | tf_op jit(solution)/shard_map/ppermute | solution.py:290
  35.0 0.2 add_convert_fusion.3
  35.2 2.1 %collective-permute-start.25 = (bf16[128,2048]{1,0:T(8,128)(2,1)S(1)}, bf16[128,2048]{1,0:T(8,128)(2,1)S(1)}, u32[]{:S(2)}, u32[]{:S(2)}) collective-permute-start(bf16[128,2048]{1,0:T(8,128)(2,1)S(1)} %add_convert_fusion.3), channel_id=1, source_target_pairs={{0,4},{5,1},{4,8},{9,5},{8,12},{13,9},{12,14},{15,13},{14,10},{11,... | collective-permute-start | bytes 1572872 | tf_op jit(solution)/shard_map/ppermute | solution.py:290
  37.3 2.7 %visit.15 = (f32[128,2048]{1,0:T(8,128)S(1)}, bf16[128,2048]{1,0:T(8,128)(2,1)S(1)}) custom-call(s32[1,16]{1,0:T(1,128)S(1)} %get-tuple-element.27.owners_ref, bf16[2080,128]{1,0:T(8,128)(2,1)S(1)} %collective-permute-done.8.refs_0_, bf16[2080,128]{1,0:T(8,128)(2,1)S(1)} %collective-permute-done.18.refs_1_, ...), custom_call_target="tpu_custom_call" | custom-call | flops 2415919104 | bytes 1572864 | tf_op jit(solution)/shard_map/visit/pallas_call | solution.py:233
  40.0 0.1 collective-permute-start.19
  40.1 0.6 collective-permute-done.9.refs_0_
  40.7 2.1 %collective-permute-start.10 = (bf16[2080,128]{1,0:T(8,128)(2,1)S(1)}, bf16[2080,128]{1,0:T(8,128)(2,1)S(1)}, u32[]{:S(2)}, u32[]{:S(2)}) collective-permute-start(bf16[2080,128]{1,0:T(8,128)(2,1)S(1)} %collective-permute-done.9.refs_0_), channel_id=1, source_target_pairs={{0,4},{5,1},{4,8},{9,5},{8,12},{13,9},{12,14},{15,13},{14,10},{11,... | collective-permute-start | bytes 1597448 | tf_op jit(solution)/shard_map/ppermute | solution.py:261
  42.8 3.5 %collective-permute-done.25 = bf16[128,2048]{1,0:T(8,128)(2,1)S(1)} collective-permute-done((bf16[128,2048]{1,0:T(8,128)(2,1)S(1)}, bf16[128,2048]{1,0:T(8,128)(2,1)S(1)}, u32[]{:S(2)}, u32[]{:S(2)}) %collective-permute-start.25) | collective-permute-done | bytes 524320 | tf_op jit(solution)/shard_map/ppermute | solution.py:290
  46.3 0.2 add_convert_fusion.2
  46.5 2.1 %collective-permute-start.26 = (bf16[128,2048]{1,0:T(8,128)(2,1)S(1)}, bf16[128,2048]{1,0:T(8,128)(2,1)S(1)}, u32[]{:S(2)}, u32[]{:S(2)}) collective-permute-start(bf16[128,2048]{1,0:T(8,128)(2,1)S(1)} %add_convert_fusion.2), channel_id=1, source_target_pairs={{0,4},{5,1},{4,8},{9,5},{8,12},{13,9},{12,14},{15,13},{14,10},{11,... | collective-permute-start | bytes 1572872 | tf_op jit(solution)/shard_map/ppermute | solution.py:290
  48.6 2.7 %visit.14 = (f32[128,2048]{1,0:T(8,128)S(1)}, bf16[128,2048]{1,0:T(8,128)(2,1)S(1)}) custom-call(s32[1,16]{1,0:T(1,128)S(1)} %get-tuple-element.27.owners_ref, bf16[2080,128]{1,0:T(8,128)(2,1)S(1)} %collective-permute-done.9.refs_0_, bf16[2080,128]{1,0:T(8,128)(2,1)S(1)} %collective-permute-done.16.refs_1_, ...), custom_call_target="tpu_custom_call" | custom-call | flops 2415919104 | bytes 1572864 | tf_op jit(solution)/shard_map/visit/pallas_call | solution.py:233
  51.3 0.1 collective-permute-start.17
  51.4 0.6 collective-permute-done.10.refs_0_
  52.0 2.0 %collective-permute-start.2 = (bf16[2080,128]{1,0:T(8,128)(2,1)S(1)}, bf16[2080,128]{1,0:T(8,128)(2,1)S(1)}, u32[]{:S(2)}, u32[]{:S(2)}) collective-permute-start(bf16[2080,128]{1,0:T(8,128)(2,1)S(1)} %get-tuple-element.28.refs_0_), channel_id=1, source_target_pairs={{4,0},{1,5},{8,4},{5,9},{12,8},{9,13},{14,12},{13,15},{10,14},{15,... | collective-permute-start | bytes 1597448 | tf_op jit(solution)/shard_map/ppermute | solution.py:261
  54.1 5.8 %collective-permute-done.26 = bf16[128,2048]{1,0:T(8,128)(2,1)S(1)} collective-permute-done((bf16[128,2048]{1,0:T(8,128)(2,1)S(1)}, bf16[128,2048]{1,0:T(8,128)(2,1)S(1)}, u32[]{:S(2)}, u32[]{:S(2)}) %collective-permute-start.26) | collective-permute-done | bytes 524320 | tf_op jit(solution)/shard_map/ppermute | solution.py:290
  59.8 0.2 add_convert_fusion.1
  60.1 2.6 %collective-permute-start.27 = (bf16[128,2048]{1,0:T(8,128)(2,1)S(1)}, bf16[128,2048]{1,0:T(8,128)(2,1)S(1)}, u32[]{:S(2)}, u32[]{:S(2)}) collective-permute-start(bf16[128,2048]{1,0:T(8,128)(2,1)S(1)} %add_convert_fusion.1), channel_id=1, source_target_pairs={{0,4},{5,1},{4,8},{9,5},{8,12},{13,9},{12,14},{15,13},{14,10},{11,... | collective-permute-start | bytes 1572872 | tf_op jit(solution)/shard_map/ppermute | solution.py:290
  62.6 2.7 %visit.13 = (f32[128,2048]{1,0:T(8,128)S(1)}, bf16[128,2048]{1,0:T(8,128)(2,1)S(1)}) custom-call(s32[1,16]{1,0:T(1,128)S(1)} %get-tuple-element.27.owners_ref, bf16[2080,128]{1,0:T(8,128)(2,1)S(1)} %collective-permute-done.10.refs_0_, bf16[2080,128]{1,0:T(8,128)(2,1)S(1)} %collective-permute-done.14.refs_1_, ...), custom_call_target="tpu_custom_call" | custom-call | flops 2415919104 | bytes 1572864 | tf_op jit(solution)/shard_map/visit/pallas_call | solution.py:233
  65.3 0.1 collective-permute-start.15
  65.4 3.6 %collective-permute-done.11.refs_0_ = bf16[2080,128]{1,0:T(8,128)(2,1)S(1)} collective-permute-done((bf16[2080,128]{1,0:T(8,128)(2,1)S(1)}, bf16[2080,128]{1,0:T(8,128)(2,1)S(1)}, u32[]{:S(2)}, u32[]{:S(2)}) %collective-permute-start.11) | collective-permute-done | bytes 532512 | tf_op jit(solution)/shard_map/ppermute | solution.py:261
  69.0 0.5 collective-permute-start
  69.5 5.1 %collective-permute-done.27 = bf16[128,2048]{1,0:T(8,128)(2,1)S(1)} collective-permute-done((bf16[128,2048]{1,0:T(8,128)(2,1)S(1)}, bf16[128,2048]{1,0:T(8,128)(2,1)S(1)}, u32[]{:S(2)}, u32[]{:S(2)}) %collective-permute-start.27) | collective-permute-done | bytes 524320 | tf_op jit(solution)/shard_map/ppermute | solution.py:290
  74.6 0.2 add_convert_fusion
  74.8 2.1 %collective-permute-start.28 = (bf16[128,2048]{1,0:T(8,128)(2,1)S(1)}, bf16[128,2048]{1,0:T(8,128)(2,1)S(1)}, u32[]{:S(2)}, u32[]{:S(2)}) collective-permute-start(bf16[128,2048]{1,0:T(8,128)(2,1)S(1)} %add_convert_fusion), channel_id=1, source_target_pairs={{0,4},{5,1},{4,8},{9,5},{8,12},{13,9},{12,14},{15,13},{14,10},{11,... | collective-permute-start | bytes 1572872 | tf_op jit(solution)/shard_map/ppermute | solution.py:290
  77.0 1.5 %visit.12 = bf16[128,2048]{1,0:T(8,128)(2,1)S(1)} custom-call(s32[1,16]{1,0:T(1,128)S(1)} %get-tuple-element.27.owners_ref, bf16[2080,128]{1,0:T(8,128)(2,1)S(1)} %collective-permute-done.12.refs_0_, bf16[1,2,2048,768]{3,2,1,0:T(8,128)(2,1)S(1)} %get-tuple-element.29.refs_2_.refs_1_, bf16[1,2,768]{2,1,0:T(2,128)(2,1)S(1)} %get-tuple-element.30.refs_3_.refs_2_, ...), custom_call_target="tpu_custom_call" | custom-call | flops 1207959552 | bytes 786432 | tf_op jit(solution)/shard_map/visit/pallas_call | solution.py:233
  78.5 0.1 collective-permute-start.13
  78.6 2.7 %visit.9 = (f32[128,2048]{1,0:T(8,128)S(1)}, bf16[128,2048]{1,0:T(8,128)(2,1)S(1)}) custom-call(s32[1,16]{1,0:T(1,128)S(1)} %get-tuple-element.27.owners_ref, bf16[2080,128]{1,0:T(8,128)(2,1)S(1)} %get-tuple-element.28.refs_0_, bf16[2080,128]{1,0:T(8,128)(2,1)S(1)} %collective-permute-done.refs_1_, ...), custom_call_target="tpu_custom_call" | custom-call | flops 2415919104 | bytes 1572864 | tf_op jit(solution)/shard_map/visit/pallas_call | solution.py:233
  81.3 0.6 collective-permute-start.1
  81.8 2.7 %visit.10 = (f32[128,2048]{1,0:T(8,128)S(1)}, bf16[128,2048]{1,0:T(8,128)(2,1)S(1)}) custom-call(s32[1,16]{1,0:T(1,128)S(1)} %get-tuple-element.27.owners_ref, bf16[2080,128]{1,0:T(8,128)(2,1)S(1)} %collective-permute-done.2.refs_0_, bf16[2080,128]{1,0:T(8,128)(2,1)S(1)} %collective-permute-done.3.refs_1_, ...), custom_call_target="tpu_custom_call" | custom-call | flops 2415919104 | bytes 1572864 | tf_op jit(solution)/shard_map/visit/pallas_call | solution.py:233
  84.5 0.1 collective-permute-start.4
  84.6 1.5 %visit.11 = f32[128,2048]{1,0:T(8,128)S(1)} custom-call(s32[1,16]{1,0:T(1,128)S(1)} %get-tuple-element.27.owners_ref, bf16[2080,128]{1,0:T(8,128)(2,1)S(1)} %collective-permute-done.11.refs_0_, bf16[1,2,2048,768]{3,2,1,0:T(8,128)(2,1)S(1)} %get-tuple-element.29.refs_2_.refs_1_, bf16[1,2,768]{2,1,0:T(2,128)(2,1)S(1)} %get-tuple-element.30.refs_3_.refs_2_, ...), custom_call_target="tpu_custom_call" | custom-call | flops 1207959552 | bytes 786432 | tf_op jit(solution)/shard_map/visit/pallas_call | solution.py:233
  86.1 0.1 fusion.1
  86.2 1.6 %collective-permute-start.29 = (bf16[56,2048]{1,0:T(8,128)(2,1)S(1)}, bf16[56,2048]{1,0:T(8,128)(2,1)S(1)}, u32[]{:S(2)}, u32[]{:S(2)}) collective-permute-start(bf16[56,2048]{1,0:T(8,128)(2,1)S(1)} %fusion.1), channel_id=1, source_target_pairs={{0,4},{5,1},{4,8},{9,5},{8,12},{13,9},{12,14},{15,13},{14,10},{11,... | collective-permute-start | bytes 688136 | tf_op jit(solution)/shard_map/ppermute | solution.py:295
  87.9 1.6 %collective-permute-start.33 = (bf16[32,2048]{1,0:T(8,128)(2,1)S(1)}, bf16[32,2048]{1,0:T(8,128)(2,1)S(1)}, u32[]{:S(2)}, u32[]{:S(2)}) collective-permute-start(bf16[32,2048]{1,0:T(8,128)(2,1)S(1)} %fusion.5), channel_id=1, source_target_pairs={{0,4},{5,1},{4,8},{9,5},{8,12},{13,9},{12,14},{15,13},{14,10},{11,... | collective-permute-start | bytes 393224 | tf_op jit(solution)/shard_map/ppermute | solution.py:295
  89.5 0.1 fusion.3
  89.6 1.6 %collective-permute-start.31 = (bf16[40,2048]{1,0:T(8,128)(2,1)S(1)}, bf16[40,2048]{1,0:T(8,128)(2,1)S(1)}, u32[]{:S(2)}, u32[]{:S(2)}) collective-permute-start(bf16[40,2048]{1,0:T(8,128)(2,1)S(1)} %fusion.3), channel_id=1, source_target_pairs={{0,4},{5,1},{4,8},{9,5},{8,12},{13,9},{12,14},{15,13},{14,10},{11,... | collective-permute-start | bytes 491528 | tf_op jit(solution)/shard_map/ppermute | solution.py:295
  91.2 2.5 %collective-permute-done.33 = bf16[32,2048]{1,0:T(8,128)(2,1)S(1)} collective-permute-done((bf16[32,2048]{1,0:T(8,128)(2,1)S(1)}, bf16[32,2048]{1,0:T(8,128)(2,1)S(1)}, u32[]{:S(2)}, u32[]{:S(2)}) %collective-permute-start.33) | collective-permute-done | bytes 131104 | tf_op jit(solution)/shard_map/ppermute | solution.py:295
  93.8 1.6 %collective-permute-start.34 = (bf16[32,2048]{1,0:T(8,128)(2,1)S(1)}, bf16[32,2048]{1,0:T(8,128)(2,1)S(1)}, u32[]{:S(2)}, u32[]{:S(2)}) collective-permute-start(bf16[32,2048]{1,0:T(8,128)(2,1)S(1)} %add_convert_fusion.10), channel_id=1, source_target_pairs={{0,4},{5,1},{4,8},{9,5},{8,12},{13,9},{12,14},{15,13},{14,10},{11,... | collective-permute-start | bytes 393224 | tf_op jit(solution)/shard_map/ppermute | solution.py:295
  95.4 0.1 collective-permute-done.31
  95.5 1.6 %collective-permute-start.32 = (bf16[40,2048]{1,0:T(8,128)(2,1)S(1)}, bf16[40,2048]{1,0:T(8,128)(2,1)S(1)}, u32[]{:S(2)}, u32[]{:S(2)}) collective-permute-start(bf16[40,2048]{1,0:T(8,128)(2,1)S(1)} %add_convert_fusion.8), channel_id=1, source_target_pairs={{0,4},{5,1},{4,8},{9,5},{8,12},{13,9},{12,14},{15,13},{14,10},{11,... | collective-permute-start | bytes 491528 | tf_op jit(solution)/shard_map/ppermute | solution.py:295
  97.2 0.1 add_convert_fusion.6
  97.2 1.6 %collective-permute-start.30 = (bf16[56,2048]{1,0:T(8,128)(2,1)S(1)}, bf16[56,2048]{1,0:T(8,128)(2,1)S(1)}, u32[]{:S(2)}, u32[]{:S(2)}) collective-permute-start(bf16[56,2048]{1,0:T(8,128)(2,1)S(1)} %add_convert_fusion.6), channel_id=1, source_target_pairs={{0,4},{5,1},{4,8},{9,5},{8,12},{13,9},{12,14},{15,13},{14,10},{11,... | collective-permute-start | bytes 688136 | tf_op jit(solution)/shard_map/ppermute | solution.py:295
  98.9 1.9 %collective-permute-done.32 = bf16[40,2048]{1,0:T(8,128)(2,1)S(1)} collective-permute-done((bf16[40,2048]{1,0:T(8,128)(2,1)S(1)}, bf16[40,2048]{1,0:T(8,128)(2,1)S(1)}, u32[]{:S(2)}, u32[]{:S(2)}) %collective-permute-start.32) | collective-permute-done | bytes 163872 | tf_op jit(solution)/shard_map/ppermute | solution.py:295
  101.0 2.4 %collective-permute-done.30 = bf16[56,2048]{1,0:T(8,128)(2,1)S(1)} collective-permute-done((bf16[56,2048]{1,0:T(8,128)(2,1)S(1)}, bf16[56,2048]{1,0:T(8,128)(2,1)S(1)}, u32[]{:S(2)}, u32[]{:S(2)}) %collective-permute-start.30) | collective-permute-done | bytes 229408 | tf_op jit(solution)/shard_map/ppermute | solution.py:295
  103.4 0.1 add_convert_fusion.5
  103.4 0.8 pad_maximum_fusion
  (33 shorter events, 0.4 us)
Async XLA Ops:
  0.0 10.5 %collective-permute-start.5 = (bf16[128,2048]{1,0:T(8,128)(2,1)}, bf16[128,2048]{1,0:T(8,128)(2,1)S(1)}, u32[]{:S(2)}, u32[]{:S(2)}) collective-permute-start(bf16[128,2048]{1,0:T(8,128)(2,1)} %tokens_hbm.1), channel_id=1, source_target_pairs={{0,4},{5,1},{4,8},{9,5},{8,12},{13,9},{12,14},{15,13},{14,10},{11,... | collective-permute-start | bytes 1572872 | tf_op jit(solution)/shard_map/ppermute | solution.py:261
  4.4 6.1 %collective-permute-start.6 = (bf16[32,128]{1,0:T(8,128)(2,1)S(1)}, bf16[32,128]{1,0:T(8,128)(2,1)S(1)}, u32[]{:S(2)}, u32[]{:S(2)}) collective-permute-start(bf16[32,128]{1,0:T(8,128)(2,1)S(1)} %get-tuple-element.37), channel_id=1, source_target_pairs={{0,4},{5,1},{4,8},{9,5},{8,12},{13,9},{12,14},{15,13},{14,10},{11,... | collective-permute-start | bytes 24584 | tf_op jit(solution)/shard_map/ppermute | solution.py:261
  10.7 2.2 %collective-permute-start.22 = (bf16[2080,128]{1,0:T(8,128)(2,1)S(1)}, bf16[2080,128]{1,0:T(8,128)(2,1)S(1)}, u32[]{:S(2)}, u32[]{:S(2)}) collective-permute-start(bf16[2080,128]{1,0:T(8,128)(2,1)S(1)} %mended.1.refs_0_), channel_id=1, source_target_pairs={{0,1},{1,0},{2,3},{3,2},{4,5},{5,4},{6,7},{7,6},{8,9},{9,8},{10,11... | collective-permute-start | bytes 1597448 | tf_op jit(solution)/shard_map/ppermute | solution.py:261
  10.7 9.3 %collective-permute-start.7 = (bf16[2080,128]{1,0:T(8,128)(2,1)S(1)}, bf16[2080,128]{1,0:T(8,128)(2,1)S(1)}, u32[]{:S(2)}, u32[]{:S(2)}) collective-permute-start(bf16[2080,128]{1,0:T(8,128)(2,1)S(1)} %mended.1.refs_0_), channel_id=1, source_target_pairs={{0,4},{5,1},{4,8},{9,5},{8,12},{13,9},{12,14},{15,13},{14,10},{11,... | collective-permute-start | bytes 1597448 | tf_op jit(solution)/shard_map/ppermute | solution.py:261
  15.6 6.6 %collective-permute-start.23 = (bf16[128,2048]{1,0:T(8,128)(2,1)S(1)}, bf16[128,2048]{1,0:T(8,128)(2,1)S(1)}, u32[]{:S(2)}, u32[]{:S(2)}) collective-permute-start(bf16[128,2048]{1,0:T(8,128)(2,1)S(1)} %get-tuple-element.48), channel_id=1, source_target_pairs={{0,1},{1,0},{2,3},{3,2},{4,5},{5,4},{6,7},{7,6},{8,9},{9,8},{10,11... | collective-permute-start | bytes 1572872 | tf_op jit(solution)/shard_map/ppermute | solution.py:261
  20.1 3.8 %collective-permute-start.20 = (bf16[2080,128]{1,0:T(8,128)(2,1)S(1)}, bf16[2080,128]{1,0:T(8,128)(2,1)S(1)}, u32[]{:S(2)}, u32[]{:S(2)}) collective-permute-start(bf16[2080,128]{1,0:T(8,128)(2,1)S(1)} %collective-permute-done.7.refs_0_), channel_id=1, source_target_pairs={{0,1},{1,0},{2,3},{3,2},{4,5},{5,4},{6,7},{7,6},{8,9},{9,8},{10,11... | collective-permute-start | bytes 1597448 | tf_op jit(solution)/shard_map/ppermute | solution.py:261
  20.1 9.3 %collective-permute-start.8 = (bf16[2080,128]{1,0:T(8,128)(2,1)S(1)}, bf16[2080,128]{1,0:T(8,128)(2,1)S(1)}, u32[]{:S(2)}, u32[]{:S(2)}) collective-permute-start(bf16[2080,128]{1,0:T(8,128)(2,1)S(1)} %collective-permute-done.7.refs_0_), channel_id=1, source_target_pairs={{0,4},{5,1},{4,8},{9,5},{8,12},{13,9},{12,14},{15,13},{14,10},{11,... | collective-permute-start | bytes 1597448 | tf_op jit(solution)/shard_map/ppermute | solution.py:261
  22.3 12.7 %collective-permute-start.24 = (bf16[128,2048]{1,0:T(8,128)(2,1)S(1)}, bf16[128,2048]{1,0:T(8,128)(2,1)S(1)}, u32[]{:S(2)}, u32[]{:S(2)}) collective-permute-start(bf16[128,2048]{1,0:T(8,128)(2,1)S(1)} %add_convert_fusion.4), channel_id=1, source_target_pairs={{0,4},{5,1},{4,8},{9,5},{8,12},{13,9},{12,14},{15,13},{14,10},{11,... | collective-permute-start | bytes 1572872 | tf_op jit(solution)/shard_map/ppermute | solution.py:290
  26.6 8.4 %collective-permute-start.21 = (bf16[128,2048]{1,0:T(8,128)(2,1)S(1)}, bf16[128,2048]{1,0:T(8,128)(2,1)S(1)}, u32[]{:S(2)}, u32[]{:S(2)}) collective-permute-start(bf16[128,2048]{1,0:T(8,128)(2,1)S(1)} %get-tuple-element.46), channel_id=1, source_target_pairs={{0,1},{1,0},{2,3},{3,2},{4,5},{5,4},{6,7},{7,6},{8,9},{9,8},{10,11... | collective-permute-start | bytes 1572872 | tf_op jit(solution)/shard_map/ppermute | solution.py:261
  29.3 7.9 %collective-permute-start.18 = (bf16[2080,128]{1,0:T(8,128)(2,1)S(1)}, bf16[2080,128]{1,0:T(8,128)(2,1)S(1)}, u32[]{:S(2)}, u32[]{:S(2)}) collective-permute-start(bf16[2080,128]{1,0:T(8,128)(2,1)S(1)} %collective-permute-done.8.refs_0_), channel_id=1, source_target_pairs={{0,1},{1,0},{2,3},{3,2},{4,5},{5,4},{6,7},{7,6},{8,9},{9,8},{10,11... | collective-permute-start | bytes 1597448 | tf_op jit(solution)/shard_map/ppermute | solution.py:261
  29.3 11.3 %collective-permute-start.9 = (bf16[2080,128]{1,0:T(8,128)(2,1)S(1)}, bf16[2080,128]{1,0:T(8,128)(2,1)S(1)}, u32[]{:S(2)}, u32[]{:S(2)}) collective-permute-start(bf16[2080,128]{1,0:T(8,128)(2,1)S(1)} %collective-permute-done.8.refs_0_), channel_id=1, source_target_pairs={{0,4},{5,1},{4,8},{9,5},{8,12},{13,9},{12,14},{15,13},{14,10},{11,... | collective-permute-start | bytes 1597448 | tf_op jit(solution)/shard_map/ppermute | solution.py:261
  35.2 11.1 %collective-permute-start.25 = (bf16[128,2048]{1,0:T(8,128)(2,1)S(1)}, bf16[128,2048]{1,0:T(8,128)(2,1)S(1)}, u32[]{:S(2)}, u32[]{:S(2)}) collective-permute-start(bf16[128,2048]{1,0:T(8,128)(2,1)S(1)} %add_convert_fusion.3), channel_id=1, source_target_pairs={{0,4},{5,1},{4,8},{9,5},{8,12},{13,9},{12,14},{15,13},{14,10},{11,... | collective-permute-start | bytes 1572872 | tf_op jit(solution)/shard_map/ppermute | solution.py:290
  40.0 6.3 %collective-permute-start.19 = (bf16[128,2048]{1,0:T(8,128)(2,1)S(1)}, bf16[128,2048]{1,0:T(8,128)(2,1)S(1)}, u32[]{:S(2)}, u32[]{:S(2)}) collective-permute-start(bf16[128,2048]{1,0:T(8,128)(2,1)S(1)} %get-tuple-element.44), channel_id=1, source_target_pairs={{0,1},{1,0},{2,3},{3,2},{4,5},{5,4},{6,7},{7,6},{8,9},{9,8},{10,11... | collective-permute-start | bytes 1572872 | tf_op jit(solution)/shard_map/ppermute | solution.py:261
  40.7 8.0 %collective-permute-start.16 = (bf16[2080,128]{1,0:T(8,128)(2,1)S(1)}, bf16[2080,128]{1,0:T(8,128)(2,1)S(1)}, u32[]{:S(2)}, u32[]{:S(2)}) collective-permute-start(bf16[2080,128]{1,0:T(8,128)(2,1)S(1)} %collective-permute-done.9.refs_0_), channel_id=1, source_target_pairs={{0,1},{1,0},{2,3},{3,2},{4,5},{5,4},{6,7},{7,6},{8,9},{9,8},{10,11... | collective-permute-start | bytes 1597448 | tf_op jit(solution)/shard_map/ppermute | solution.py:261
  40.7 11.3 %collective-permute-start.10 = (bf16[2080,128]{1,0:T(8,128)(2,1)S(1)}, bf16[2080,128]{1,0:T(8,128)(2,1)S(1)}, u32[]{:S(2)}, u32[]{:S(2)}) collective-permute-start(bf16[2080,128]{1,0:T(8,128)(2,1)S(1)} %collective-permute-done.9.refs_0_), channel_id=1, source_target_pairs={{0,4},{5,1},{4,8},{9,5},{8,12},{13,9},{12,14},{15,13},{14,10},{11,... | collective-permute-start | bytes 1597448 | tf_op jit(solution)/shard_map/ppermute | solution.py:261
  46.5 13.3 %collective-permute-start.26 = (bf16[128,2048]{1,0:T(8,128)(2,1)S(1)}, bf16[128,2048]{1,0:T(8,128)(2,1)S(1)}, u32[]{:S(2)}, u32[]{:S(2)}) collective-permute-start(bf16[128,2048]{1,0:T(8,128)(2,1)S(1)} %add_convert_fusion.2), channel_id=1, source_target_pairs={{0,4},{5,1},{4,8},{9,5},{8,12},{13,9},{12,14},{15,13},{14,10},{11,... | collective-permute-start | bytes 1572872 | tf_op jit(solution)/shard_map/ppermute | solution.py:290
  51.3 8.5 %collective-permute-start.17 = (bf16[128,2048]{1,0:T(8,128)(2,1)S(1)}, bf16[128,2048]{1,0:T(8,128)(2,1)S(1)}, u32[]{:S(2)}, u32[]{:S(2)}) collective-permute-start(bf16[128,2048]{1,0:T(8,128)(2,1)S(1)} %get-tuple-element.42), channel_id=1, source_target_pairs={{0,1},{1,0},{2,3},{3,2},{4,5},{5,4},{6,7},{7,6},{8,9},{9,8},{10,11... | collective-permute-start | bytes 1572872 | tf_op jit(solution)/shard_map/ppermute | solution.py:261
  52.0 10.7 %collective-permute-start.14 = (bf16[2080,128]{1,0:T(8,128)(2,1)S(1)}, bf16[2080,128]{1,0:T(8,128)(2,1)S(1)}, u32[]{:S(2)}, u32[]{:S(2)}) collective-permute-start(bf16[2080,128]{1,0:T(8,128)(2,1)S(1)} %collective-permute-done.10.refs_0_), channel_id=1, source_target_pairs={{0,1},{1,0},{2,3},{3,2},{4,5},{5,4},{6,7},{7,6},{8,9},{9,8},{10,11... | collective-permute-start | bytes 1597448 | tf_op jit(solution)/shard_map/ppermute | solution.py:261
  52.0 17.5 %collective-permute-start.2 = (bf16[2080,128]{1,0:T(8,128)(2,1)S(1)}, bf16[2080,128]{1,0:T(8,128)(2,1)S(1)}, u32[]{:S(2)}, u32[]{:S(2)}) collective-permute-start(bf16[2080,128]{1,0:T(8,128)(2,1)S(1)} %get-tuple-element.28.refs_0_), channel_id=1, source_target_pairs={{4,0},{1,5},{8,4},{5,9},{12,8},{9,13},{14,12},{13,15},{10,14},{15,... | collective-permute-start | bytes 1597448 | tf_op jit(solution)/shard_map/ppermute | solution.py:261
  54.0 15.0 %collective-permute-start.11 = (bf16[2080,128]{1,0:T(8,128)(2,1)S(1)}, bf16[2080,128]{1,0:T(8,128)(2,1)S(1)}, u32[]{:S(2)}, u32[]{:S(2)}) collective-permute-start(bf16[2080,128]{1,0:T(8,128)(2,1)S(1)} %collective-permute-done.10.refs_0_), channel_id=1, source_target_pairs={{0,4},{5,1},{4,8},{9,5},{8,12},{13,9},{12,14},{15,13},{14,10},{11,... | collective-permute-start | bytes 1597448 | tf_op jit(solution)/shard_map/ppermute | solution.py:261
  60.1 14.6 %collective-permute-start.27 = (bf16[128,2048]{1,0:T(8,128)(2,1)S(1)}, bf16[128,2048]{1,0:T(8,128)(2,1)S(1)}, u32[]{:S(2)}, u32[]{:S(2)}) collective-permute-start(bf16[128,2048]{1,0:T(8,128)(2,1)S(1)} %add_convert_fusion.1), channel_id=1, source_target_pairs={{0,4},{5,1},{4,8},{9,5},{8,12},{13,9},{12,14},{15,13},{14,10},{11,... | collective-permute-start | bytes 1572872 | tf_op jit(solution)/shard_map/ppermute | solution.py:290
  65.3 9.3 %collective-permute-start.15 = (bf16[128,2048]{1,0:T(8,128)(2,1)S(1)}, bf16[128,2048]{1,0:T(8,128)(2,1)S(1)}, u32[]{:S(2)}, u32[]{:S(2)}) collective-permute-start(bf16[128,2048]{1,0:T(8,128)(2,1)S(1)} %get-tuple-element.40), channel_id=1, source_target_pairs={{0,1},{1,0},{2,3},{3,2},{4,5},{5,4},{6,7},{7,6},{8,9},{9,8},{10,11... | collective-permute-start | bytes 1572872 | tf_op jit(solution)/shard_map/ppermute | solution.py:261
  69.0 7.9 %collective-permute-start.12 = (bf16[2080,128]{1,0:T(8,128)(2,1)S(1)}, bf16[2080,128]{1,0:T(8,128)(2,1)S(1)}, u32[]{:S(2)}, u32[]{:S(2)}) collective-permute-start(bf16[2080,128]{1,0:T(8,128)(2,1)S(1)} %collective-permute-done.11.refs_0_), channel_id=1, source_target_pairs={{0,1},{1,0},{2,3},{3,2},{4,5},{5,4},{6,7},{7,6},{8,9},{9,8},{10,11... | collective-permute-start | bytes 1597448 | tf_op jit(solution)/shard_map/ppermute | solution.py:261
  69.0 9.5 %collective-permute-start = (bf16[2080,128]{1,0:T(8,128)(2,1)S(1)}, bf16[2080,128]{1,0:T(8,128)(2,1)S(1)}, u32[]{:S(2)}, u32[]{:S(2)}) collective-permute-start(bf16[2080,128]{1,0:T(8,128)(2,1)S(1)} %get-tuple-element.28.refs_0_), channel_id=1, source_target_pairs={{0,1},{1,0},{2,3},{3,2},{4,5},{5,4},{6,7},{7,6},{8,9},{9,8},{10,11... | collective-permute-start | bytes 1597448 | tf_op jit(solution)/shard_map/ppermute | solution.py:261
  69.5 12.3 %collective-permute-start.3 = (bf16[2080,128]{1,0:T(8,128)(2,1)S(1)}, bf16[2080,128]{1,0:T(8,128)(2,1)S(1)}, u32[]{:S(2)}, u32[]{:S(2)}) collective-permute-start(bf16[2080,128]{1,0:T(8,128)(2,1)S(1)} %collective-permute-done.2.refs_0_), channel_id=1, source_target_pairs={{0,1},{1,0},{2,3},{3,2},{4,5},{5,4},{6,7},{7,6},{8,9},{9,8},{10,11... | collective-permute-start | bytes 1597448 | tf_op jit(solution)/shard_map/ppermute | solution.py:261
  74.8 11.3 %collective-permute-start.28 = (bf16[128,2048]{1,0:T(8,128)(2,1)S(1)}, bf16[128,2048]{1,0:T(8,128)(2,1)S(1)}, u32[]{:S(2)}, u32[]{:S(2)}) collective-permute-start(bf16[128,2048]{1,0:T(8,128)(2,1)S(1)} %add_convert_fusion), channel_id=1, source_target_pairs={{0,4},{5,1},{4,8},{9,5},{8,12},{13,9},{12,14},{15,13},{14,10},{11,... | collective-permute-start | bytes 1572872 | tf_op jit(solution)/shard_map/ppermute | solution.py:290
  78.5 7.6 %collective-permute-start.13 = (bf16[128,2048]{1,0:T(8,128)(2,1)S(1)}, bf16[128,2048]{1,0:T(8,128)(2,1)S(1)}, u32[]{:S(2)}, u32[]{:S(2)}) collective-permute-start(bf16[128,2048]{1,0:T(8,128)(2,1)S(1)} %visit.12), channel_id=1, source_target_pairs={{0,1},{1,0},{2,3},{3,2},{4,5},{5,4},{6,7},{7,6},{8,9},{9,8},{10,11... | collective-permute-start | bytes 1572872 | tf_op jit(solution)/shard_map/ppermute | solution.py:261
  81.3 17.6 %collective-permute-start.1 = (bf16[128,2048]{1,0:T(8,128)(2,1)S(1)}, bf16[128,2048]{1,0:T(8,128)(2,1)S(1)}, u32[]{:S(2)}, u32[]{:S(2)}) collective-permute-start(bf16[128,2048]{1,0:T(8,128)(2,1)S(1)} %get-tuple-element.34), channel_id=1, source_target_pairs={{0,1},{1,0},{2,3},{3,2},{4,5},{5,4},{6,7},{7,6},{8,9},{9,8},{10,11... | collective-permute-start | bytes 1572872 | tf_op jit(solution)/shard_map/ppermute | solution.py:261
  84.5 6.7 %collective-permute-start.4 = (bf16[128,2048]{1,0:T(8,128)(2,1)S(1)}, bf16[128,2048]{1,0:T(8,128)(2,1)S(1)}, u32[]{:S(2)}, u32[]{:S(2)}) collective-permute-start(bf16[128,2048]{1,0:T(8,128)(2,1)S(1)} %get-tuple-element.36), channel_id=1, source_target_pairs={{0,1},{1,0},{2,3},{3,2},{4,5},{5,4},{6,7},{7,6},{8,9},{9,8},{10,11... | collective-permute-start | bytes 1572872 | tf_op jit(solution)/shard_map/ppermute | solution.py:261
  86.2 10.9 %collective-permute-start.29 = (bf16[56,2048]{1,0:T(8,128)(2,1)S(1)}, bf16[56,2048]{1,0:T(8,128)(2,1)S(1)}, u32[]{:S(2)}, u32[]{:S(2)}) collective-permute-start(bf16[56,2048]{1,0:T(8,128)(2,1)S(1)} %fusion.1), channel_id=1, source_target_pairs={{0,4},{5,1},{4,8},{9,5},{8,12},{13,9},{12,14},{15,13},{14,10},{11,... | collective-permute-start | bytes 688136 | tf_op jit(solution)/shard_map/ppermute | solution.py:295
  87.9 5.8 %collective-permute-start.33 = (bf16[32,2048]{1,0:T(8,128)(2,1)S(1)}, bf16[32,2048]{1,0:T(8,128)(2,1)S(1)}, u32[]{:S(2)}, u32[]{:S(2)}) collective-permute-start(bf16[32,2048]{1,0:T(8,128)(2,1)S(1)} %fusion.5), channel_id=1, source_target_pairs={{0,4},{5,1},{4,8},{9,5},{8,12},{13,9},{12,14},{15,13},{14,10},{11,... | collective-permute-start | bytes 393224 | tf_op jit(solution)/shard_map/ppermute | solution.py:295
  89.6 5.8 %collective-permute-start.31 = (bf16[40,2048]{1,0:T(8,128)(2,1)S(1)}, bf16[40,2048]{1,0:T(8,128)(2,1)S(1)}, u32[]{:S(2)}, u32[]{:S(2)}) collective-permute-start(bf16[40,2048]{1,0:T(8,128)(2,1)S(1)} %fusion.3), channel_id=1, source_target_pairs={{0,4},{5,1},{4,8},{9,5},{8,12},{13,9},{12,14},{15,13},{14,10},{11,... | collective-permute-start | bytes 491528 | tf_op jit(solution)/shard_map/ppermute | solution.py:295
  93.8 5.1 %collective-permute-start.34 = (bf16[32,2048]{1,0:T(8,128)(2,1)S(1)}, bf16[32,2048]{1,0:T(8,128)(2,1)S(1)}, u32[]{:S(2)}, u32[]{:S(2)}) collective-permute-start(bf16[32,2048]{1,0:T(8,128)(2,1)S(1)} %add_convert_fusion.10), channel_id=1, source_target_pairs={{0,4},{5,1},{4,8},{9,5},{8,12},{13,9},{12,14},{15,13},{14,10},{11,... | collective-permute-start | bytes 393224 | tf_op jit(solution)/shard_map/ppermute | solution.py:295
  95.5 5.4 %collective-permute-start.32 = (bf16[40,2048]{1,0:T(8,128)(2,1)S(1)}, bf16[40,2048]{1,0:T(8,128)(2,1)S(1)}, u32[]{:S(2)}, u32[]{:S(2)}) collective-permute-start(bf16[40,2048]{1,0:T(8,128)(2,1)S(1)} %add_convert_fusion.8), channel_id=1, source_target_pairs={{0,4},{5,1},{4,8},{9,5},{8,12},{13,9},{12,14},{15,13},{14,10},{11,... | collective-permute-start | bytes 491528 | tf_op jit(solution)/shard_map/ppermute | solution.py:295
  97.2 6.1 %collective-permute-start.30 = (bf16[56,2048]{1,0:T(8,128)(2,1)S(1)}, bf16[56,2048]{1,0:T(8,128)(2,1)S(1)}, u32[]{:S(2)}, u32[]{:S(2)}) collective-permute-start(bf16[56,2048]{1,0:T(8,128)(2,1)S(1)} %add_convert_fusion.6), channel_id=1, source_target_pairs={{0,4},{5,1},{4,8},{9,5},{8,12},{13,9},{12,14},{15,13},{14,10},{11,... | collective-permute-start | bytes 688136 | tf_op jit(solution)/shard_map/ppermute | solution.py:295

commit v3 on v2

--- a/solution.py
+++ b/solution.py
@@ -263,9 +263,9 @@
     raw = moved(tokens, ring)
     block, table = packed(tokens, norm_gain, expert_ids, gate_weights, experts)
     table = moved(table, ring)
-    gain, *blocks = loaded(
-        norm_gain[None, :], owner_map[None, :], in_q, in_scale, down_q, down_scale
-    )
+    gain, owners, in_q, in_scale = loaded(norm_gain[None, :], owner_map[None, :], in_q, in_scale)
+    down_q, down_scale = loaded(down_q, down_scale)
+    blocks = (owners, in_q, in_scale, down_q, down_scale)
     back = moved(block, [(target, source) for source, target in ring])
     near = mended(raw, table, gain)
     parts = []

time: 105 us -> 106 us (level)
    pallas_call x1 -> x2, Pallas kernels: 3.81 us -> 4.76 us  [loaded(): pl.pallas_call(functools.partial(loaded_kernel, count), out_shape=tuple((...]
where the time goes in v3:
time: 106 us
  waiting for transfers between devices  38.2 us (36%)
  starting transfers between devices  37.3 us (35%)
  Pallas kernels  28 us (26%)
  other arithmetic  2.42 us (2%)
    pallas_call x9, Pallas kernels, visit(): pl.pallas_call(functools.partial(visit_kernel, count), out_shape=tuple((j...  21.7 us
    ppermute x5, waiting for transfers between devices, circulated(): total = lax.ppermute(summed(step, slice(None), total), 'tok', ring)  17.9 us
    ppermute x24, starting transfers between devices, moved(): return lax.ppermute(value, 'tok', pairs)  16.9 us
    ppermute x24, waiting for transfers between devices, moved(): return lax.ppermute(value, 'tok', pairs)  13.3 us
    ppermute x5, starting transfers between devices, circulated(): total = lax.ppermute(summed(step, slice(None), total), 'tok', ring)  10.6 us
    ppermute x6, starting transfers between devices, circulated(): totals[name] = lax.ppermute(summed(step, rows, totals[name]), 'tok', ring)  9.72 us
    ppermute x6, waiting for transfers between devices, circulated(): totals[name] = lax.ppermute(summed(step, rows, totals[name]), 'tok', ring)  6.93 us
    pallas_call x2, Pallas kernels, loaded(): pl.pallas_call(functools.partial(loaded_kernel, count), out_shape=tuple((...  4.76 us
  transfers between devices with their start and end apart: 35, of which 14 were waited for; matrix products, arithmetic and copies ran while one was open for 1% of the time, Pallas kernels for 26%

profile of v3, /device:TPU:0, one launch (start us, length us, event | category | flops | bytes accessed | tf_op | source)
XLA Modules:
  0.0 106.2 jit_solution(2514281843876634195)
XLA Ops:
  0.0 3.1 %collective-permute-start.5 = (bf16[128,2048]{1,0:T(8,128)(2,1)}, bf16[128,2048]{1,0:T(8,128)(2,1)S(1)}, u32[]{:S(2)}, u32[]{:S(2)}) collective-permute-start(bf16[128,2048]{1,0:T(8,128)(2,1)} %tokens_hbm.1), channel_id=1, source_target_pairs={{0,4},{5,1},{4,8},{9,5},{8,12},{13,9},{12,14},{15,13},{14,10},{11,... | collective-permute-start | bytes 1572872 | tf_op jit(solution)/shard_map/ppermute | solution.py:261
  3.1 1.3 %packed.1 = (bf16[2080,128]{1,0:T(8,128)(2,1)S(1)}, bf16[32,128]{1,0:T(8,128)(2,1)S(1)}) custom-call(bf16[128,2048]{1,0:T(8,128)(2,1)} %tokens_hbm.1, f32[1,2048]{1,0:T(1,128)} %bitcast.4, s32[8,128]{1,0:T(8,128)} %bitcast.6, f32[8,128]{1,0:T(8,128)} %bitcast.7), custom_call_target="tpu_custom_call" | custom-call | tf_op jit(solution)/shard_map/packed/pallas_call | solution.py:121
  4.4 1.6 %collective-permute-start.6 = (bf16[32,128]{1,0:T(8,128)(2,1)S(1)}, bf16[32,128]{1,0:T(8,128)(2,1)S(1)}, u32[]{:S(2)}, u32[]{:S(2)}) collective-permute-start(bf16[32,128]{1,0:T(8,128)(2,1)S(1)} %get-tuple-element.37), channel_id=1, source_target_pairs={{0,4},{5,1},{4,8},{9,5},{8,12},{13,9},{12,14},{15,13},{14,10},{11,... | collective-permute-start | bytes 24584 | tf_op jit(solution)/shard_map/ppermute | solution.py:261
  6.0 2.9 %loaded.2 = (f32[1,2048]{1,0:T(1,128)S(1)}, s32[1,16]{1,0:T(1,128)S(1)}, bf16[1,2,2048,768]{3,2,1,0:T(8,128)(2,1)S(1)}, bf16[1,2,768]{2,1,0:T(2,128)(2,1)S(1)}) custom-call(f32[1,2048]{1,0:T(1,128)} %bitcast.5, s32[1,16]{1,0:T(1,128)} %bitcast.8, bf16[1,2,2048,768]{3,2,1,0:T(8,128)(2,1)} %refs_2_.1, bf16[1,2,768]{2,1,0:T(2,128)(2,1)} %refs_3_.1), custom_call_target="tpu_custom_call" | custom-call | bytes 6298656 | tf_op jit(solution)/shard_map/loaded/pallas_call | solution.py:171
  8.9 1.6 %collective-permute-done.6.table_ref = bf16[32,128]{1,0:T(8,128)(2,1)S(1)} collective-permute-done((bf16[32,128]{1,0:T(8,128)(2,1)S(1)}, bf16[32,128]{1,0:T(8,128)(2,1)S(1)}, u32[]{:S(2)}, u32[]{:S(2)}) %collective-permute-start.6) | collective-permute-done | bytes 8224 | tf_op jit(solution)/shard_map/ppermute | solution.py:261
  10.5 0.2 mended.1.refs_0_
  10.7 0.1 collective-permute-start.22
  10.7 1.9 %loaded.3 = (bf16[1,768,2048]{2,1,0:T(8,128)(2,1)S(1)}, bf16[1,2048]{1,0:T(2,128)(2,1)S(1)}) custom-call(bf16[1,768,2048]{2,1,0:T(8,128)(2,1)} %refs_0_.1, bf16[1,2048]{1,0:T(2,128)(2,1)} %refs_1_.1), custom_call_target="tpu_custom_call" | custom-call | bytes 3149824 | tf_op jit(solution)/shard_map/loaded/pallas_call | solution.py:171
  12.7 2.1 %collective-permute-start.7 = (bf16[2080,128]{1,0:T(8,128)(2,1)S(1)}, bf16[2080,128]{1,0:T(8,128)(2,1)S(1)}, u32[]{:S(2)}, u32[]{:S(2)}) collective-permute-start(bf16[2080,128]{1,0:T(8,128)(2,1)S(1)} %mended.1.refs_0_), channel_id=1, source_target_pairs={{0,4},{5,1},{4,8},{9,5},{8,12},{13,9},{12,14},{15,13},{14,10},{11,... | collective-permute-start | bytes 1597448 | tf_op jit(solution)/shard_map/ppermute | solution.py:261
  14.8 2.7 %visit.17 = (f32[128,2048]{1,0:T(8,128)S(1)}, bf16[128,2048]{1,0:T(8,128)(2,1)S(1)}) custom-call(s32[1,16]{1,0:T(1,128)S(1)} %get-tuple-element.27.owners_ref, bf16[2080,128]{1,0:T(8,128)(2,1)S(1)} %mended.1.refs_0_, bf16[2080,128]{1,0:T(8,128)(2,1)S(1)} %collective-permute-done.22.refs_1_, bf16[1,2,2048,768]{3,2,1,0:T(8,128)(2,1)S(1)} %get-tuple-element.29.refs_2_.refs_1_, ...), custom_call_target="tpu_custom_call" | custom-call | flops 2415919104 | bytes 1572864 | tf_op jit(solution)/shard_map/visit/pallas_call | solution.py:233
  17.5 0.2 collective-permute-start.23
  17.7 4.3 %collective-permute-done.7.refs_0_ = bf16[2080,128]{1,0:T(8,128)(2,1)S(1)} collective-permute-done((bf16[2080,128]{1,0:T(8,128)(2,1)S(1)}, bf16[2080,128]{1,0:T(8,128)(2,1)S(1)}, u32[]{:S(2)}, u32[]{:S(2)}) %collective-permute-start.7) | collective-permute-done | bytes 532512 | tf_op jit(solution)/shard_map/ppermute | solution.py:261
  22.0 2.1 %collective-permute-start.8 = (bf16[2080,128]{1,0:T(8,128)(2,1)S(1)}, bf16[2080,128]{1,0:T(8,128)(2,1)S(1)}, u32[]{:S(2)}, u32[]{:S(2)}) collective-permute-start(bf16[2080,128]{1,0:T(8,128)(2,1)S(1)} %collective-permute-done.7.refs_0_), channel_id=1, source_target_pairs={{0,4},{5,1},{4,8},{9,5},{8,12},{13,9},{12,14},{15,13},{14,10},{11,... | collective-permute-start | bytes 1597448 | tf_op jit(solution)/shard_map/ppermute | solution.py:261
  24.1 0.1 add_convert_fusion.4
  24.2 1.6 %collective-permute-start.24 = (bf16[128,2048]{1,0:T(8,128)(2,1)S(1)}, bf16[128,2048]{1,0:T(8,128)(2,1)S(1)}, u32[]{:S(2)}, u32[]{:S(2)}) collective-permute-start(bf16[128,2048]{1,0:T(8,128)(2,1)S(1)} %add_convert_fusion.4), channel_id=1, source_target_pairs={{0,4},{5,1},{4,8},{9,5},{8,12},{13,9},{12,14},{15,13},{14,10},{11,... | collective-permute-start | bytes 1572872 | tf_op jit(solution)/shard_map/ppermute | solution.py:290
  25.9 2.7 %visit.16 = (f32[128,2048]{1,0:T(8,128)S(1)}, bf16[128,2048]{1,0:T(8,128)(2,1)S(1)}) custom-call(s32[1,16]{1,0:T(1,128)S(1)} %get-tuple-element.27.owners_ref, bf16[2080,128]{1,0:T(8,128)(2,1)S(1)} %collective-permute-done.7.refs_0_, bf16[2080,128]{1,0:T(8,128)(2,1)S(1)} %collective-permute-done.20.refs_1_, ...), custom_call_target="tpu_custom_call" | custom-call | flops 2415919104 | bytes 1572864 | tf_op jit(solution)/shard_map/visit/pallas_call | solution.py:233
  28.6 0.1 collective-permute-start.21
  28.6 2.6 %collective-permute-done.8.refs_0_ = bf16[2080,128]{1,0:T(8,128)(2,1)S(1)} collective-permute-done((bf16[2080,128]{1,0:T(8,128)(2,1)S(1)}, bf16[2080,128]{1,0:T(8,128)(2,1)S(1)}, u32[]{:S(2)}, u32[]{:S(2)}) %collective-permute-start.8) | collective-permute-done | bytes 532512 | tf_op jit(solution)/shard_map/ppermute | solution.py:261
  31.3 2.1 %collective-permute-start.9 = (bf16[2080,128]{1,0:T(8,128)(2,1)S(1)}, bf16[2080,128]{1,0:T(8,128)(2,1)S(1)}, u32[]{:S(2)}, u32[]{:S(2)}) collective-permute-start(bf16[2080,128]{1,0:T(8,128)(2,1)S(1)} %collective-permute-done.8.refs_0_), channel_id=1, source_target_pairs={{0,4},{5,1},{4,8},{9,5},{8,12},{13,9},{12,14},{15,13},{14,10},{11,... | collective-permute-start | bytes 1597448 | tf_op jit(solution)/shard_map/ppermute | solution.py:261
  33.3 3.5 %collective-permute-done.24 = bf16[128,2048]{1,0:T(8,128)(2,1)S(1)} collective-permute-done((bf16[128,2048]{1,0:T(8,128)(2,1)S(1)}, bf16[128,2048]{1,0:T(8,128)(2,1)S(1)}, u32[]{:S(2)}, u32[]{:S(2)}) %collective-permute-start.24) | collective-permute-done | bytes 524320 | tf_op jit(solution)/shard_map/ppermute | solution.py:290
  36.9 0.2 add_convert_fusion.3
  37.1 2.1 %collective-permute-start.25 = (bf16[128,2048]{1,0:T(8,128)(2,1)S(1)}, bf16[128,2048]{1,0:T(8,128)(2,1)S(1)}, u32[]{:S(2)}, u32[]{:S(2)}) collective-permute-start(bf16[128,2048]{1,0:T(8,128)(2,1)S(1)} %add_convert_fusion.3), channel_id=1, source_target_pairs={{0,4},{5,1},{4,8},{9,5},{8,12},{13,9},{12,14},{15,13},{14,10},{11,... | collective-permute-start | bytes 1572872 | tf_op jit(solution)/shard_map/ppermute | solution.py:290
  39.2 2.7 %visit.15 = (f32[128,2048]{1,0:T(8,128)S(1)}, bf16[128,2048]{1,0:T(8,128)(2,1)S(1)}) custom-call(s32[1,16]{1,0:T(1,128)S(1)} %get-tuple-element.27.owners_ref, bf16[2080,128]{1,0:T(8,128)(2,1)S(1)} %collective-permute-done.8.refs_0_, bf16[2080,128]{1,0:T(8,128)(2,1)S(1)} %collective-permute-done.18.refs_1_, ...), custom_call_target="tpu_custom_call" | custom-call | flops 2415919104 | bytes 1572864 | tf_op jit(solution)/shard_map/visit/pallas_call | solution.py:233
  41.9 0.1 collective-permute-start.19
  42.0 0.6 collective-permute-done.9.refs_0_
  42.6 2.1 %collective-permute-start.10 = (bf16[2080,128]{1,0:T(8,128)(2,1)S(1)}, bf16[2080,128]{1,0:T(8,128)(2,1)S(1)}, u32[]{:S(2)}, u32[]{:S(2)}) collective-permute-start(bf16[2080,128]{1,0:T(8,128)(2,1)S(1)} %collective-permute-done.9.refs_0_), channel_id=1, source_target_pairs={{0,4},{5,1},{4,8},{9,5},{8,12},{13,9},{12,14},{15,13},{14,10},{11,... | collective-permute-start | bytes 1597448 | tf_op jit(solution)/shard_map/ppermute | solution.py:261
  44.7 3.5 %collective-permute-done.25 = bf16[128,2048]{1,0:T(8,128)(2,1)S(1)} collective-permute-done((bf16[128,2048]{1,0:T(8,128)(2,1)S(1)}, bf16[128,2048]{1,0:T(8,128)(2,1)S(1)}, u32[]{:S(2)}, u32[]{:S(2)}) %collective-permute-start.25) | collective-permute-done | bytes 524320 | tf_op jit(solution)/shard_map/ppermute | solution.py:290
  48.2 0.2 add_convert_fusion.2
  48.4 2.1 %collective-permute-start.26 = (bf16[128,2048]{1,0:T(8,128)(2,1)S(1)}, bf16[128,2048]{1,0:T(8,128)(2,1)S(1)}, u32[]{:S(2)}, u32[]{:S(2)}) collective-permute-start(bf16[128,2048]{1,0:T(8,128)(2,1)S(1)} %add_convert_fusion.2), channel_id=1, source_target_pairs={{0,4},{5,1},{4,8},{9,5},{8,12},{13,9},{12,14},{15,13},{14,10},{11,... | collective-permute-start | bytes 1572872 | tf_op jit(solution)/shard_map/ppermute | solution.py:290
  50.6 2.7 %visit.14 = (f32[128,2048]{1,0:T(8,128)S(1)}, bf16[128,2048]{1,0:T(8,128)(2,1)S(1)}) custom-call(s32[1,16]{1,0:T(1,128)S(1)} %get-tuple-element.27.owners_ref, bf16[2080,128]{1,0:T(8,128)(2,1)S(1)} %collective-permute-done.9.refs_0_, bf16[2080,128]{1,0:T(8,128)(2,1)S(1)} %collective-permute-done.16.refs_1_, ...), custom_call_target="tpu_custom_call" | custom-call | flops 2415919104 | bytes 1572864 | tf_op jit(solution)/shard_map/visit/pallas_call | solution.py:233
  53.3 0.1 collective-permute-start.17
  53.3 0.6 collective-permute-done.10.refs_0_
  53.9 2.0 %collective-permute-start.2 = (bf16[2080,128]{1,0:T(8,128)(2,1)S(1)}, bf16[2080,128]{1,0:T(8,128)(2,1)S(1)}, u32[]{:S(2)}, u32[]{:S(2)}) collective-permute-start(bf16[2080,128]{1,0:T(8,128)(2,1)S(1)} %get-tuple-element.28.refs_0_), channel_id=1, source_target_pairs={{4,0},{1,5},{8,4},{5,9},{12,8},{9,13},{14,12},{13,15},{10,14},{15,... | collective-permute-start | bytes 1597448 | tf_op jit(solution)/shard_map/ppermute | solution.py:261
  56.0 5.8 %collective-permute-done.26 = bf16[128,2048]{1,0:T(8,128)(2,1)S(1)} collective-permute-done((bf16[128,2048]{1,0:T(8,128)(2,1)S(1)}, bf16[128,2048]{1,0:T(8,128)(2,1)S(1)}, u32[]{:S(2)}, u32[]{:S(2)}) %collective-permute-start.26) | collective-permute-done | bytes 524320 | tf_op jit(solution)/shard_map/ppermute | solution.py:290
  61.8 0.2 add_convert_fusion.1
  62.0 2.6 %collective-permute-start.27 = (bf16[128,2048]{1,0:T(8,128)(2,1)S(1)}, bf16[128,2048]{1,0:T(8,128)(2,1)S(1)}, u32[]{:S(2)}, u32[]{:S(2)}) collective-permute-start(bf16[128,2048]{1,0:T(8,128)(2,1)S(1)} %add_convert_fusion.1), channel_id=1, source_target_pairs={{0,4},{5,1},{4,8},{9,5},{8,12},{13,9},{12,14},{15,13},{14,10},{11,... | collective-permute-start | bytes 1572872 | tf_op jit(solution)/shard_map/ppermute | solution.py:290
  64.6 2.7 %visit.13 = (f32[128,2048]{1,0:T(8,128)S(1)}, bf16[128,2048]{1,0:T(8,128)(2,1)S(1)}) custom-call(s32[1,16]{1,0:T(1,128)S(1)} %get-tuple-element.27.owners_ref, bf16[2080,128]{1,0:T(8,128)(2,1)S(1)} %collective-permute-done.10.refs_0_, bf16[2080,128]{1,0:T(8,128)(2,1)S(1)} %collective-permute-done.14.refs_1_, ...), custom_call_target="tpu_custom_call" | custom-call | flops 2415919104 | bytes 1572864 | tf_op jit(solution)/shard_map/visit/pallas_call | solution.py:233
  67.3 0.1 collective-permute-start.15
  67.3 3.6 %collective-permute-done.11.refs_0_ = bf16[2080,128]{1,0:T(8,128)(2,1)S(1)} collective-permute-done((bf16[2080,128]{1,0:T(8,128)(2,1)S(1)}, bf16[2080,128]{1,0:T(8,128)(2,1)S(1)}, u32[]{:S(2)}, u32[]{:S(2)}) %collective-permute-start.11) | collective-permute-done | bytes 532512 | tf_op jit(solution)/shard_map/ppermute | solution.py:261
  70.9 0.5 collective-permute-start
  71.5 5.1 %collective-permute-done.27 = bf16[128,2048]{1,0:T(8,128)(2,1)S(1)} collective-permute-done((bf16[128,2048]{1,0:T(8,128)(2,1)S(1)}, bf16[128,2048]{1,0:T(8,128)(2,1)S(1)}, u32[]{:S(2)}, u32[]{:S(2)}) %collective-permute-start.27) | collective-permute-done | bytes 524320 | tf_op jit(solution)/shard_map/ppermute | solution.py:290
  76.6 0.2 add_convert_fusion
  76.8 2.1 %collective-permute-start.28 = (bf16[128,2048]{1,0:T(8,128)(2,1)S(1)}, bf16[128,2048]{1,0:T(8,128)(2,1)S(1)}, u32[]{:S(2)}, u32[]{:S(2)}) collective-permute-start(bf16[128,2048]{1,0:T(8,128)(2,1)S(1)} %add_convert_fusion), channel_id=1, source_target_pairs={{0,4},{5,1},{4,8},{9,5},{8,12},{13,9},{12,14},{15,13},{14,10},{11,... | collective-permute-start | bytes 1572872 | tf_op jit(solution)/shard_map/ppermute | solution.py:290
  78.9 1.5 %visit.12 = bf16[128,2048]{1,0:T(8,128)(2,1)S(1)} custom-call(s32[1,16]{1,0:T(1,128)S(1)} %get-tuple-element.27.owners_ref, bf16[2080,128]{1,0:T(8,128)(2,1)S(1)} %collective-permute-done.12.refs_0_, bf16[1,2,2048,768]{3,2,1,0:T(8,128)(2,1)S(1)} %get-tuple-element.29.refs_2_.refs_1_, bf16[1,2,768]{2,1,0:T(2,128)(2,1)S(1)} %get-tuple-element.30.refs_3_.refs_2_, ...), custom_call_target="tpu_custom_call" | custom-call | flops 1207959552 | bytes 786432 | tf_op jit(solution)/shard_map/visit/pallas_call | solution.py:233
  80.4 0.1 collective-permute-start.13
  80.5 2.7 %visit.9 = (f32[128,2048]{1,0:T(8,128)S(1)}, bf16[128,2048]{1,0:T(8,128)(2,1)S(1)}) custom-call(s32[1,16]{1,0:T(1,128)S(1)} %get-tuple-element.27.owners_ref, bf16[2080,128]{1,0:T(8,128)(2,1)S(1)} %get-tuple-element.28.refs_0_, bf16[2080,128]{1,0:T(8,128)(2,1)S(1)} %collective-permute-done.refs_1_, ...), custom_call_target="tpu_custom_call" | custom-call | flops 2415919104 | bytes 1572864 | tf_op jit(solution)/shard_map/visit/pallas_call | solution.py:233
  83.2 0.6 collective-permute-start.1
  83.7 2.7 %visit.10 = (f32[128,2048]{1,0:T(8,128)S(1)}, bf16[128,2048]{1,0:T(8,128)(2,1)S(1)}) custom-call(s32[1,16]{1,0:T(1,128)S(1)} %get-tuple-element.27.owners_ref, bf16[2080,128]{1,0:T(8,128)(2,1)S(1)} %collective-permute-done.2.refs_0_, bf16[2080,128]{1,0:T(8,128)(2,1)S(1)} %collective-permute-done.3.refs_1_, ...), custom_call_target="tpu_custom_call" | custom-call | flops 2415919104 | bytes 1572864 | tf_op jit(solution)/shard_map/visit/pallas_call | solution.py:233
  86.4 0.1 collective-permute-start.4
  86.5 1.5 %visit.11 = f32[128,2048]{1,0:T(8,128)S(1)} custom-call(s32[1,16]{1,0:T(1,128)S(1)} %get-tuple-element.27.owners_ref, bf16[2080,128]{1,0:T(8,128)(2,1)S(1)} %collective-permute-done.11.refs_0_, bf16[1,2,2048,768]{3,2,1,0:T(8,128)(2,1)S(1)} %get-tuple-element.29.refs_2_.refs_1_, bf16[1,2,768]{2,1,0:T(2,128)(2,1)S(1)} %get-tuple-element.30.refs_3_.refs_2_, ...), custom_call_target="tpu_custom_call" | custom-call | flops 1207959552 | bytes 786432 | tf_op jit(solution)/shard_map/visit/pallas_call | solution.py:233
  88.1 0.1 fusion.1
  88.2 1.6 %collective-permute-start.29 = (bf16[56,2048]{1,0:T(8,128)(2,1)S(1)}, bf16[56,2048]{1,0:T(8,128)(2,1)S(1)}, u32[]{:S(2)}, u32[]{:S(2)}) collective-permute-start(bf16[56,2048]{1,0:T(8,128)(2,1)S(1)} %fusion.1), channel_id=1, source_target_pairs={{0,4},{5,1},{4,8},{9,5},{8,12},{13,9},{12,14},{15,13},{14,10},{11,... | collective-permute-start | bytes 688136 | tf_op jit(solution)/shard_map/ppermute | solution.py:295
  89.8 1.6 %collective-permute-start.33 = (bf16[32,2048]{1,0:T(8,128)(2,1)S(1)}, bf16[32,2048]{1,0:T(8,128)(2,1)S(1)}, u32[]{:S(2)}, u32[]{:S(2)}) collective-permute-start(bf16[32,2048]{1,0:T(8,128)(2,1)S(1)} %fusion.5), channel_id=1, source_target_pairs={{0,4},{5,1},{4,8},{9,5},{8,12},{13,9},{12,14},{15,13},{14,10},{11,... | collective-permute-start | bytes 393224 | tf_op jit(solution)/shard_map/ppermute | solution.py:295
  91.5 1.6 %collective-permute-start.31 = (bf16[40,2048]{1,0:T(8,128)(2,1)S(1)}, bf16[40,2048]{1,0:T(8,128)(2,1)S(1)}, u32[]{:S(2)}, u32[]{:S(2)}) collective-permute-start(bf16[40,2048]{1,0:T(8,128)(2,1)S(1)} %fusion.3), channel_id=1, source_target_pairs={{0,4},{5,1},{4,8},{9,5},{8,12},{13,9},{12,14},{15,13},{14,10},{11,... | collective-permute-start | bytes 491528 | tf_op jit(solution)/shard_map/ppermute | solution.py:295
  93.1 2.5 %collective-permute-done.33 = bf16[32,2048]{1,0:T(8,128)(2,1)S(1)} collective-permute-done((bf16[32,2048]{1,0:T(8,128)(2,1)S(1)}, bf16[32,2048]{1,0:T(8,128)(2,1)S(1)}, u32[]{:S(2)}, u32[]{:S(2)}) %collective-permute-start.33) | collective-permute-done | bytes 131104 | tf_op jit(solution)/shard_map/ppermute | solution.py:295
  95.7 1.6 %collective-permute-start.34 = (bf16[32,2048]{1,0:T(8,128)(2,1)S(1)}, bf16[32,2048]{1,0:T(8,128)(2,1)S(1)}, u32[]{:S(2)}, u32[]{:S(2)}) collective-permute-start(bf16[32,2048]{1,0:T(8,128)(2,1)S(1)} %add_convert_fusion.10), channel_id=1, source_target_pairs={{0,4},{5,1},{4,8},{9,5},{8,12},{13,9},{12,14},{15,13},{14,10},{11,... | collective-permute-start | bytes 393224 | tf_op jit(solution)/shard_map/ppermute | solution.py:295
  97.3 0.1 collective-permute-done.31
  97.5 1.6 %collective-permute-start.32 = (bf16[40,2048]{1,0:T(8,128)(2,1)S(1)}, bf16[40,2048]{1,0:T(8,128)(2,1)S(1)}, u32[]{:S(2)}, u32[]{:S(2)}) collective-permute-start(bf16[40,2048]{1,0:T(8,128)(2,1)S(1)} %add_convert_fusion.8), channel_id=1, source_target_pairs={{0,4},{5,1},{4,8},{9,5},{8,12},{13,9},{12,14},{15,13},{14,10},{11,... | collective-permute-start | bytes 491528 | tf_op jit(solution)/shard_map/ppermute | solution.py:295
  99.1 0.1 add_convert_fusion.6
  99.2 1.6 %collective-permute-start.30 = (bf16[56,2048]{1,0:T(8,128)(2,1)S(1)}, bf16[56,2048]{1,0:T(8,128)(2,1)S(1)}, u32[]{:S(2)}, u32[]{:S(2)}) collective-permute-start(bf16[56,2048]{1,0:T(8,128)(2,1)S(1)} %add_convert_fusion.6), channel_id=1, source_target_pairs={{0,4},{5,1},{4,8},{9,5},{8,12},{13,9},{12,14},{15,13},{14,10},{11,... | collective-permute-start | bytes 688136 | tf_op jit(solution)/shard_map/ppermute | solution.py:295
  100.9 1.9 %collective-permute-done.32 = bf16[40,2048]{1,0:T(8,128)(2,1)S(1)} collective-permute-done((bf16[40,2048]{1,0:T(8,128)(2,1)S(1)}, bf16[40,2048]{1,0:T(8,128)(2,1)S(1)}, u32[]{:S(2)}, u32[]{:S(2)}) %collective-permute-start.32) | collective-permute-done | bytes 163872 | tf_op jit(solution)/shard_map/ppermute | solution.py:295
  102.9 2.4 %collective-permute-done.30 = bf16[56,2048]{1,0:T(8,128)(2,1)S(1)} collective-permute-done((bf16[56,2048]{1,0:T(8,128)(2,1)S(1)}, bf16[56,2048]{1,0:T(8,128)(2,1)S(1)}, u32[]{:S(2)}, u32[]{:S(2)}) %collective-permute-start.30) | collective-permute-done | bytes 229408 | tf_op jit(solution)/shard_map/ppermute | solution.py:295
  105.3 0.1 add_convert_fusion.5
  105.4 0.8 pad_maximum_fusion
  (34 shorter events, 0.5 us)
Async XLA Ops:
  0.0 10.5 %collective-permute-start.5 = (bf16[128,2048]{1,0:T(8,128)(2,1)}, bf16[128,2048]{1,0:T(8,128)(2,1)S(1)}, u32[]{:S(2)}, u32[]{:S(2)}) collective-permute-start(bf16[128,2048]{1,0:T(8,128)(2,1)} %tokens_hbm.1), channel_id=1, source_target_pairs={{0,4},{5,1},{4,8},{9,5},{8,12},{13,9},{12,14},{15,13},{14,10},{11,... | collective-permute-start | bytes 1572872 | tf_op jit(solution)/shard_map/ppermute | solution.py:261
  4.4 6.1 %collective-permute-start.6 = (bf16[32,128]{1,0:T(8,128)(2,1)S(1)}, bf16[32,128]{1,0:T(8,128)(2,1)S(1)}, u32[]{:S(2)}, u32[]{:S(2)}) collective-permute-start(bf16[32,128]{1,0:T(8,128)(2,1)S(1)} %get-tuple-element.37), channel_id=1, source_target_pairs={{0,4},{5,1},{4,8},{9,5},{8,12},{13,9},{12,14},{15,13},{14,10},{11,... | collective-permute-start | bytes 24584 | tf_op jit(solution)/shard_map/ppermute | solution.py:261
  10.7 4.1 %collective-permute-start.22 = (bf16[2080,128]{1,0:T(8,128)(2,1)S(1)}, bf16[2080,128]{1,0:T(8,128)(2,1)S(1)}, u32[]{:S(2)}, u32[]{:S(2)}) collective-permute-start(bf16[2080,128]{1,0:T(8,128)(2,1)S(1)} %mended.1.refs_0_), channel_id=1, source_target_pairs={{0,1},{1,0},{2,3},{3,2},{4,5},{5,4},{6,7},{7,6},{8,9},{9,8},{10,11... | collective-permute-start | bytes 1597448 | tf_op jit(solution)/shard_map/ppermute | solution.py:261
  12.7 9.3 %collective-permute-start.7 = (bf16[2080,128]{1,0:T(8,128)(2,1)S(1)}, bf16[2080,128]{1,0:T(8,128)(2,1)S(1)}, u32[]{:S(2)}, u32[]{:S(2)}) collective-permute-start(bf16[2080,128]{1,0:T(8,128)(2,1)S(1)} %mended.1.refs_0_), channel_id=1, source_target_pairs={{0,4},{5,1},{4,8},{9,5},{8,12},{13,9},{12,14},{15,13},{14,10},{11,... | collective-permute-start | bytes 1597448 | tf_op jit(solution)/shard_map/ppermute | solution.py:261
  17.5 6.6 %collective-permute-start.23 = (bf16[128,2048]{1,0:T(8,128)(2,1)S(1)}, bf16[128,2048]{1,0:T(8,128)(2,1)S(1)}, u32[]{:S(2)}, u32[]{:S(2)}) collective-permute-start(bf16[128,2048]{1,0:T(8,128)(2,1)S(1)} %get-tuple-element.48), channel_id=1, source_target_pairs={{0,1},{1,0},{2,3},{3,2},{4,5},{5,4},{6,7},{7,6},{8,9},{9,8},{10,11... | collective-permute-start | bytes 1572872 | tf_op jit(solution)/shard_map/ppermute | solution.py:261
  22.0 3.9 %collective-permute-start.20 = (bf16[2080,128]{1,0:T(8,128)(2,1)S(1)}, bf16[2080,128]{1,0:T(8,128)(2,1)S(1)}, u32[]{:S(2)}, u32[]{:S(2)}) collective-permute-start(bf16[2080,128]{1,0:T(8,128)(2,1)S(1)} %collective-permute-done.7.refs_0_), channel_id=1, source_target_pairs={{0,1},{1,0},{2,3},{3,2},{4,5},{5,4},{6,7},{7,6},{8,9},{9,8},{10,11... | collective-permute-start | bytes 1597448 | tf_op jit(solution)/shard_map/ppermute | solution.py:261
  22.0 9.3 %collective-permute-start.8 = (bf16[2080,128]{1,0:T(8,128)(2,1)S(1)}, bf16[2080,128]{1,0:T(8,128)(2,1)S(1)}, u32[]{:S(2)}, u32[]{:S(2)}) collective-permute-start(bf16[2080,128]{1,0:T(8,128)(2,1)S(1)} %collective-permute-done.7.refs_0_), channel_id=1, source_target_pairs={{0,4},{5,1},{4,8},{9,5},{8,12},{13,9},{12,14},{15,13},{14,10},{11,... | collective-permute-start | bytes 1597448 | tf_op jit(solution)/shard_map/ppermute | solution.py:261
  24.2 12.7 %collective-permute-start.24 = (bf16[128,2048]{1,0:T(8,128)(2,1)S(1)}, bf16[128,2048]{1,0:T(8,128)(2,1)S(1)}, u32[]{:S(2)}, u32[]{:S(2)}) collective-permute-start(bf16[128,2048]{1,0:T(8,128)(2,1)S(1)} %add_convert_fusion.4), channel_id=1, source_target_pairs={{0,4},{5,1},{4,8},{9,5},{8,12},{13,9},{12,14},{15,13},{14,10},{11,... | collective-permute-start | bytes 1572872 | tf_op jit(solution)/shard_map/ppermute | solution.py:290
  28.6 8.3 %collective-permute-start.21 = (bf16[128,2048]{1,0:T(8,128)(2,1)S(1)}, bf16[128,2048]{1,0:T(8,128)(2,1)S(1)}, u32[]{:S(2)}, u32[]{:S(2)}) collective-permute-start(bf16[128,2048]{1,0:T(8,128)(2,1)S(1)} %get-tuple-element.46), channel_id=1, source_target_pairs={{0,1},{1,0},{2,3},{3,2},{4,5},{5,4},{6,7},{7,6},{8,9},{9,8},{10,11... | collective-permute-start | bytes 1572872 | tf_op jit(solution)/shard_map/ppermute | solution.py:261
  31.3 8.0 %collective-permute-start.18 = (bf16[2080,128]{1,0:T(8,128)(2,1)S(1)}, bf16[2080,128]{1,0:T(8,128)(2,1)S(1)}, u32[]{:S(2)}, u32[]{:S(2)}) collective-permute-start(bf16[2080,128]{1,0:T(8,128)(2,1)S(1)} %collective-permute-done.8.refs_0_), channel_id=1, source_target_pairs={{0,1},{1,0},{2,3},{3,2},{4,5},{5,4},{6,7},{7,6},{8,9},{9,8},{10,11... | collective-permute-start | bytes 1597448 | tf_op jit(solution)/shard_map/ppermute | solution.py:261
  31.3 11.3 %collective-permute-start.9 = (bf16[2080,128]{1,0:T(8,128)(2,1)S(1)}, bf16[2080,128]{1,0:T(8,128)(2,1)S(1)}, u32[]{:S(2)}, u32[]{:S(2)}) collective-permute-start(bf16[2080,128]{1,0:T(8,128)(2,1)S(1)} %collective-permute-done.8.refs_0_), channel_id=1, source_target_pairs={{0,4},{5,1},{4,8},{9,5},{8,12},{13,9},{12,14},{15,13},{14,10},{11,... | collective-permute-start | bytes 1597448 | tf_op jit(solution)/shard_map/ppermute | solution.py:261
  37.1 11.1 %collective-permute-start.25 = (bf16[128,2048]{1,0:T(8,128)(2,1)S(1)}, bf16[128,2048]{1,0:T(8,128)(2,1)S(1)}, u32[]{:S(2)}, u32[]{:S(2)}) collective-permute-start(bf16[128,2048]{1,0:T(8,128)(2,1)S(1)} %add_convert_fusion.3), channel_id=1, source_target_pairs={{0,4},{5,1},{4,8},{9,5},{8,12},{13,9},{12,14},{15,13},{14,10},{11,... | collective-permute-start | bytes 1572872 | tf_op jit(solution)/shard_map/ppermute | solution.py:290
  41.9 6.3 %collective-permute-start.19 = (bf16[128,2048]{1,0:T(8,128)(2,1)S(1)}, bf16[128,2048]{1,0:T(8,128)(2,1)S(1)}, u32[]{:S(2)}, u32[]{:S(2)}) collective-permute-start(bf16[128,2048]{1,0:T(8,128)(2,1)S(1)} %get-tuple-element.44), channel_id=1, source_target_pairs={{0,1},{1,0},{2,3},{3,2},{4,5},{5,4},{6,7},{7,6},{8,9},{9,8},{10,11... | collective-permute-start | bytes 1572872 | tf_op jit(solution)/shard_map/ppermute | solution.py:261
  42.6 8.0 %collective-permute-start.16 = (bf16[2080,128]{1,0:T(8,128)(2,1)S(1)}, bf16[2080,128]{1,0:T(8,128)(2,1)S(1)}, u32[]{:S(2)}, u32[]{:S(2)}) collective-permute-start(bf16[2080,128]{1,0:T(8,128)(2,1)S(1)} %collective-permute-done.9.refs_0_), channel_id=1, source_target_pairs={{0,1},{1,0},{2,3},{3,2},{4,5},{5,4},{6,7},{7,6},{8,9},{9,8},{10,11... | collective-permute-start | bytes 1597448 | tf_op jit(solution)/shard_map/ppermute | solution.py:261
  42.6 11.3 %collective-permute-start.10 = (bf16[2080,128]{1,0:T(8,128)(2,1)S(1)}, bf16[2080,128]{1,0:T(8,128)(2,1)S(1)}, u32[]{:S(2)}, u32[]{:S(2)}) collective-permute-start(bf16[2080,128]{1,0:T(8,128)(2,1)S(1)} %collective-permute-done.9.refs_0_), channel_id=1, source_target_pairs={{0,4},{5,1},{4,8},{9,5},{8,12},{13,9},{12,14},{15,13},{14,10},{11,... | collective-permute-start | bytes 1597448 | tf_op jit(solution)/shard_map/ppermute | solution.py:261
  48.4 13.3 %collective-permute-start.26 = (bf16[128,2048]{1,0:T(8,128)(2,1)S(1)}, bf16[128,2048]{1,0:T(8,128)(2,1)S(1)}, u32[]{:S(2)}, u32[]{:S(2)}) collective-permute-start(bf16[128,2048]{1,0:T(8,128)(2,1)S(1)} %add_convert_fusion.2), channel_id=1, source_target_pairs={{0,4},{5,1},{4,8},{9,5},{8,12},{13,9},{12,14},{15,13},{14,10},{11,... | collective-permute-start | bytes 1572872 | tf_op jit(solution)/shard_map/ppermute | solution.py:290
  53.3 8.5 %collective-permute-start.17 = (bf16[128,2048]{1,0:T(8,128)(2,1)S(1)}, bf16[128,2048]{1,0:T(8,128)(2,1)S(1)}, u32[]{:S(2)}, u32[]{:S(2)}) collective-permute-start(bf16[128,2048]{1,0:T(8,128)(2,1)S(1)} %get-tuple-element.42), channel_id=1, source_target_pairs={{0,1},{1,0},{2,3},{3,2},{4,5},{5,4},{6,7},{7,6},{8,9},{9,8},{10,11... | collective-permute-start | bytes 1572872 | tf_op jit(solution)/shard_map/ppermute | solution.py:261
  53.9 10.7 %collective-permute-start.14 = (bf16[2080,128]{1,0:T(8,128)(2,1)S(1)}, bf16[2080,128]{1,0:T(8,128)(2,1)S(1)}, u32[]{:S(2)}, u32[]{:S(2)}) collective-permute-start(bf16[2080,128]{1,0:T(8,128)(2,1)S(1)} %collective-permute-done.10.refs_0_), channel_id=1, source_target_pairs={{0,1},{1,0},{2,3},{3,2},{4,5},{5,4},{6,7},{7,6},{8,9},{9,8},{10,11... | collective-permute-start | bytes 1597448 | tf_op jit(solution)/shard_map/ppermute | solution.py:261
  53.9 17.5 %collective-permute-start.2 = (bf16[2080,128]{1,0:T(8,128)(2,1)S(1)}, bf16[2080,128]{1,0:T(8,128)(2,1)S(1)}, u32[]{:S(2)}, u32[]{:S(2)}) collective-permute-start(bf16[2080,128]{1,0:T(8,128)(2,1)S(1)} %get-tuple-element.28.refs_0_), channel_id=1, source_target_pairs={{4,0},{1,5},{8,4},{5,9},{12,8},{9,13},{14,12},{13,15},{10,14},{15,... | collective-permute-start | bytes 1597448 | tf_op jit(solution)/shard_map/ppermute | solution.py:261
  55.9 15.0 %collective-permute-start.11 = (bf16[2080,128]{1,0:T(8,128)(2,1)S(1)}, bf16[2080,128]{1,0:T(8,128)(2,1)S(1)}, u32[]{:S(2)}, u32[]{:S(2)}) collective-permute-start(bf16[2080,128]{1,0:T(8,128)(2,1)S(1)} %collective-permute-done.10.refs_0_), channel_id=1, source_target_pairs={{0,4},{5,1},{4,8},{9,5},{8,12},{13,9},{12,14},{15,13},{14,10},{11,... | collective-permute-start | bytes 1597448 | tf_op jit(solution)/shard_map/ppermute | solution.py:261
  62.0 14.6 %collective-permute-start.27 = (bf16[128,2048]{1,0:T(8,128)(2,1)S(1)}, bf16[128,2048]{1,0:T(8,128)(2,1)S(1)}, u32[]{:S(2)}, u32[]{:S(2)}) collective-permute-start(bf16[128,2048]{1,0:T(8,128)(2,1)S(1)} %add_convert_fusion.1), channel_id=1, source_target_pairs={{0,4},{5,1},{4,8},{9,5},{8,12},{13,9},{12,14},{15,13},{14,10},{11,... | collective-permute-start | bytes 1572872 | tf_op jit(solution)/shard_map/ppermute | solution.py:290
  67.3 9.3 %collective-permute-start.15 = (bf16[128,2048]{1,0:T(8,128)(2,1)S(1)}, bf16[128,2048]{1,0:T(8,128)(2,1)S(1)}, u32[]{:S(2)}, u32[]{:S(2)}) collective-permute-start(bf16[128,2048]{1,0:T(8,128)(2,1)S(1)} %get-tuple-element.40), channel_id=1, source_target_pairs={{0,1},{1,0},{2,3},{3,2},{4,5},{5,4},{6,7},{7,6},{8,9},{9,8},{10,11... | collective-permute-start | bytes 1572872 | tf_op jit(solution)/shard_map/ppermute | solution.py:261
  70.9 8.0 %collective-permute-start.12 = (bf16[2080,128]{1,0:T(8,128)(2,1)S(1)}, bf16[2080,128]{1,0:T(8,128)(2,1)S(1)}, u32[]{:S(2)}, u32[]{:S(2)}) collective-permute-start(bf16[2080,128]{1,0:T(8,128)(2,1)S(1)} %collective-permute-done.11.refs_0_), channel_id=1, source_target_pairs={{0,1},{1,0},{2,3},{3,2},{4,5},{5,4},{6,7},{7,6},{8,9},{9,8},{10,11... | collective-permute-start | bytes 1597448 | tf_op jit(solution)/shard_map/ppermute | solution.py:261
  70.9 9.6 %collective-permute-start = (bf16[2080,128]{1,0:T(8,128)(2,1)S(1)}, bf16[2080,128]{1,0:T(8,128)(2,1)S(1)}, u32[]{:S(2)}, u32[]{:S(2)}) collective-permute-start(bf16[2080,128]{1,0:T(8,128)(2,1)S(1)} %get-tuple-element.28.refs_0_), channel_id=1, source_target_pairs={{0,1},{1,0},{2,3},{3,2},{4,5},{5,4},{6,7},{7,6},{8,9},{9,8},{10,11... | collective-permute-start | bytes 1597448 | tf_op jit(solution)/shard_map/ppermute | solution.py:261
  71.5 12.3 %collective-permute-start.3 = (bf16[2080,128]{1,0:T(8,128)(2,1)S(1)}, bf16[2080,128]{1,0:T(8,128)(2,1)S(1)}, u32[]{:S(2)}, u32[]{:S(2)}) collective-permute-start(bf16[2080,128]{1,0:T(8,128)(2,1)S(1)} %collective-permute-done.2.refs_0_), channel_id=1, source_target_pairs={{0,1},{1,0},{2,3},{3,2},{4,5},{5,4},{6,7},{7,6},{8,9},{9,8},{10,11... | collective-permute-start | bytes 1597448 | tf_op jit(solution)/shard_map/ppermute | solution.py:261
  76.8 11.3 %collective-permute-start.28 = (bf16[128,2048]{1,0:T(8,128)(2,1)S(1)}, bf16[128,2048]{1,0:T(8,128)(2,1)S(1)}, u32[]{:S(2)}, u32[]{:S(2)}) collective-permute-start(bf16[128,2048]{1,0:T(8,128)(2,1)S(1)} %add_convert_fusion), channel_id=1, source_target_pairs={{0,4},{5,1},{4,8},{9,5},{8,12},{13,9},{12,14},{15,13},{14,10},{11,... | collective-permute-start | bytes 1572872 | tf_op jit(solution)/shard_map/ppermute | solution.py:290
  80.4 7.6 %collective-permute-start.13 = (bf16[128,2048]{1,0:T(8,128)(2,1)S(1)}, bf16[128,2048]{1,0:T(8,128)(2,1)S(1)}, u32[]{:S(2)}, u32[]{:S(2)}) collective-permute-start(bf16[128,2048]{1,0:T(8,128)(2,1)S(1)} %visit.12), channel_id=1, source_target_pairs={{0,1},{1,0},{2,3},{3,2},{4,5},{5,4},{6,7},{7,6},{8,9},{9,8},{10,11... | collective-permute-start | bytes 1572872 | tf_op jit(solution)/shard_map/ppermute | solution.py:261
  83.2 17.6 %collective-permute-start.1 = (bf16[128,2048]{1,0:T(8,128)(2,1)S(1)}, bf16[128,2048]{1,0:T(8,128)(2,1)S(1)}, u32[]{:S(2)}, u32[]{:S(2)}) collective-permute-start(bf16[128,2048]{1,0:T(8,128)(2,1)S(1)} %get-tuple-element.34), channel_id=1, source_target_pairs={{0,1},{1,0},{2,3},{3,2},{4,5},{5,4},{6,7},{7,6},{8,9},{9,8},{10,11... | collective-permute-start | bytes 1572872 | tf_op jit(solution)/shard_map/ppermute | solution.py:261
  86.4 6.7 %collective-permute-start.4 = (bf16[128,2048]{1,0:T(8,128)(2,1)S(1)}, bf16[128,2048]{1,0:T(8,128)(2,1)S(1)}, u32[]{:S(2)}, u32[]{:S(2)}) collective-permute-start(bf16[128,2048]{1,0:T(8,128)(2,1)S(1)} %get-tuple-element.36), channel_id=1, source_target_pairs={{0,1},{1,0},{2,3},{3,2},{4,5},{5,4},{6,7},{7,6},{8,9},{9,8},{10,11... | collective-permute-start | bytes 1572872 | tf_op jit(solution)/shard_map/ppermute | solution.py:261
  88.2 10.9 %collective-permute-start.29 = (bf16[56,2048]{1,0:T(8,128)(2,1)S(1)}, bf16[56,2048]{1,0:T(8,128)(2,1)S(1)}, u32[]{:S(2)}, u32[]{:S(2)}) collective-permute-start(bf16[56,2048]{1,0:T(8,128)(2,1)S(1)} %fusion.1), channel_id=1, source_target_pairs={{0,4},{5,1},{4,8},{9,5},{8,12},{13,9},{12,14},{15,13},{14,10},{11,... | collective-permute-start | bytes 688136 | tf_op jit(solution)/shard_map/ppermute | solution.py:295
  89.8 5.8 %collective-permute-start.33 = (bf16[32,2048]{1,0:T(8,128)(2,1)S(1)}, bf16[32,2048]{1,0:T(8,128)(2,1)S(1)}, u32[]{:S(2)}, u32[]{:S(2)}) collective-permute-start(bf16[32,2048]{1,0:T(8,128)(2,1)S(1)} %fusion.5), channel_id=1, source_target_pairs={{0,4},{5,1},{4,8},{9,5},{8,12},{13,9},{12,14},{15,13},{14,10},{11,... | collective-permute-start | bytes 393224 | tf_op jit(solution)/shard_map/ppermute | solution.py:295
  91.5 5.8 %collective-permute-start.31 = (bf16[40,2048]{1,0:T(8,128)(2,1)S(1)}, bf16[40,2048]{1,0:T(8,128)(2,1)S(1)}, u32[]{:S(2)}, u32[]{:S(2)}) collective-permute-start(bf16[40,2048]{1,0:T(8,128)(2,1)S(1)} %fusion.3), channel_id=1, source_target_pairs={{0,4},{5,1},{4,8},{9,5},{8,12},{13,9},{12,14},{15,13},{14,10},{11,... | collective-permute-start | bytes 491528 | tf_op jit(solution)/shard_map/ppermute | solution.py:295
  95.7 5.1 %collective-permute-start.34 = (bf16[32,2048]{1,0:T(8,128)(2,1)S(1)}, bf16[32,2048]{1,0:T(8,128)(2,1)S(1)}, u32[]{:S(2)}, u32[]{:S(2)}) collective-permute-start(bf16[32,2048]{1,0:T(8,128)(2,1)S(1)} %add_convert_fusion.10), channel_id=1, source_target_pairs={{0,4},{5,1},{4,8},{9,5},{8,12},{13,9},{12,14},{15,13},{14,10},{11,... | collective-permute-start | bytes 393224 | tf_op jit(solution)/shard_map/ppermute | solution.py:295
  97.5 5.4 %collective-permute-start.32 = (bf16[40,2048]{1,0:T(8,128)(2,1)S(1)}, bf16[40,2048]{1,0:T(8,128)(2,1)S(1)}, u32[]{:S(2)}, u32[]{:S(2)}) collective-permute-start(bf16[40,2048]{1,0:T(8,128)(2,1)S(1)} %add_convert_fusion.8), channel_id=1, source_target_pairs={{0,4},{5,1},{4,8},{9,5},{8,12},{13,9},{12,14},{15,13},{14,10},{11,... | collective-permute-start | bytes 491528 | tf_op jit(solution)/shard_map/ppermute | solution.py:295
  99.2 6.1 %collective-permute-start.30 = (bf16[56,2048]{1,0:T(8,128)(2,1)S(1)}, bf16[56,2048]{1,0:T(8,128)(2,1)S(1)}, u32[]{:S(2)}, u32[]{:S(2)}) collective-permute-start(bf16[56,2048]{1,0:T(8,128)(2,1)S(1)} %add_convert_fusion.6), channel_id=1, source_target_pairs={{0,4},{5,1},{4,8},{9,5},{8,12},{13,9},{12,14},{15,13},{14,10},{11,... | collective-permute-start | bytes 688136 | tf_op jit(solution)/shard_map/ppermute | solution.py:295

commit v4 on v3

--- a/solution.py
+++ b/solution.py
@@ -249,6 +249,31 @@
     )(*operands)
 
 
+def finished_kernel(first, part_ref, lent_ref, arrived_ref, *refs):
+    out_hbm, rows_ref, sem = refs[-3:]
+    rows = slice(first, first + arrived_ref.shape[0])
+    total = part_ref[rows, :] + lent_ref[rows, :].astype(jnp.float32)
+    rows_ref[...] = (total + arrived_ref[...].astype(jnp.float32)).astype(jnp.bfloat16)
+    move = pltpu.make_async_copy(rows_ref, out_hbm.at[rows, :], sem)
+    move.start()
+    move.wait()
+
+
+def finished(out, part, lent, arrived, first):
+    held = () if out is None else (out,)
+    return pl.pallas_call(
+        functools.partial(finished_kernel, first),
+        out_shape=jax.ShapeDtypeStruct(part.shape, jnp.bfloat16),
+        in_specs=[pl.BlockSpec(memory_space=pltpu.VMEM)] * 3
+        + [pl.BlockSpec(memory_space=pltpu.HBM)] * len(held),
+        out_specs=pl.BlockSpec(memory_space=pltpu.HBM),
+        scratch_shapes=[pltpu.VMEM(arrived.shape, jnp.bfloat16), pltpu.SemaphoreType.DMA(())],
+        input_output_aliases={3: 0} if held else {},
+        compiler_params=pltpu.CompilerParams(vmem_limit_bytes=SMALL),
+        name="finished",
+    )(part, lent, arrived, *held)
+
+
 def circulated(
     tokens, norm_gain, expert_ids, gate_weights, owner_map, in_q, in_scale, down_q, down_scale
 ):
@@ -293,10 +318,11 @@
     for step in range(chips - 2, chips):
         for name, rows in shares.items():
             totals[name] = lax.ppermute(summed(step, rows, totals[name]), "tok", ring)
-    out = []
+    out = None
+    part, lent = parts[0]
     for name, rows in shares.items():
-        out.append(summed(0, rows, totals[name]))
-    return jnp.concatenate(out)
+        out = finished(out, part, lent, totals[name], rows.start)
+    return out
 
 
 def shares_of(tok_rows):

time: 106 us -> 107 us (level)
  Pallas kernels: 28 us -> 30.3 us
  other arithmetic: 2.42 us -> 1.27 us
  waiting for transfers between devices: 38.2 us -> 37.1 us
    pallas_call x0 -> x3, Pallas kernels: none -> 2.23 us  [finished(): pl.pallas_call(functools.partial(finished_kernel, first), out_shape=jax.S...]
    ppermute x6, waiting for transfers between devices: 6.93 us -> 5.73 us  [circulated(): totals[name] = lax.ppermute(summed(step, rows, totals[name]), 'tok', ring)]
  transfers between devices with their start and end apart: 35 -> 35, of which waited for: 14 -> 12; matrix products, arithmetic and copies ran while one was open for 1% -> 1% of each run, Pallas kernels for 26% -> 28%
where the time goes in v4:
time: 107 us; the launch traced here: 106 us
  starting transfers between devices  37.2 us (35%)
  waiting for transfers between devices  37.1 us (35%)
  Pallas kernels  30.3 us (28%)
  other arithmetic  1.27 us (1%)
    pallas_call x9, Pallas kernels, visit(): pl.pallas_call(functools.partial(visit_kernel, count), out_shape=tuple((j...  21.7 us
    ppermute x5, waiting for transfers between devices, circulated(): total = lax.ppermute(summed(step, slice(None), total), 'tok', ring)  17.9 us
    ppermute x24, starting transfers between devices, moved(): return lax.ppermute(value, 'tok', pairs)  16.9 us
    ppermute x24, waiting for transfers between devices, moved(): return lax.ppermute(value, 'tok', pairs)  13.4 us
    ppermute x5, starting transfers between devices, circulated(): total = lax.ppermute(summed(step, slice(None), total), 'tok', ring)  10.6 us
    ppermute x6, starting transfers between devices, circulated(): totals[name] = lax.ppermute(summed(step, rows, totals[name]), 'tok', ring)  9.66 us
    ppermute x6, waiting for transfers between devices, circulated(): totals[name] = lax.ppermute(summed(step, rows, totals[name]), 'tok', ring)  5.73 us
    pallas_call x2, Pallas kernels, loaded(): pl.pallas_call(functools.partial(loaded_kernel, count), out_shape=tuple((...  4.76 us
  transfers between devices with their start and end apart: 35, of which 12 were waited for; matrix products, arithmetic and copies ran while one was open for 1% of the time, Pallas kernels for 28%

profile of v4, /device:TPU:0, one launch (start us, length us, event | category | flops | bytes accessed | tf_op | source)
XLA Modules:
  0.0 106.3 jit_solution(14730516925831426694)
XLA Ops:
  0.0 3.1 %collective-permute-start.5 = (bf16[128,2048]{1,0:T(8,128)(2,1)}, bf16[128,2048]{1,0:T(8,128)(2,1)S(1)}, u32[]{:S(2)}, u32[]{:S(2)}) collective-permute-start(bf16[128,2048]{1,0:T(8,128)(2,1)} %tokens_hbm.1), channel_id=1, source_target_pairs={{0,4},{5,1},{4,8},{9,5},{8,12},{13,9},{12,14},{15,13},{14,10},{11,... | collective-permute-start | bytes 1572872 | tf_op jit(solution)/shard_map/ppermute | solution.py:286
  3.1 1.3 %packed.1 = (bf16[2080,128]{1,0:T(8,128)(2,1)S(1)}, bf16[32,128]{1,0:T(8,128)(2,1)S(1)}) custom-call(bf16[128,2048]{1,0:T(8,128)(2,1)} %tokens_hbm.1, f32[1,2048]{1,0:T(1,128)} %bitcast.4, s32[8,128]{1,0:T(8,128)} %bitcast.6, f32[8,128]{1,0:T(8,128)} %bitcast.7), custom_call_target="tpu_custom_call" | custom-call | tf_op jit(solution)/shard_map/packed/pallas_call | solution.py:121
  4.4 1.6 %collective-permute-start.6 = (bf16[32,128]{1,0:T(8,128)(2,1)S(1)}, bf16[32,128]{1,0:T(8,128)(2,1)S(1)}, u32[]{:S(2)}, u32[]{:S(2)}) collective-permute-start(bf16[32,128]{1,0:T(8,128)(2,1)S(1)} %get-tuple-element.37), channel_id=1, source_target_pairs={{0,4},{5,1},{4,8},{9,5},{8,12},{13,9},{12,14},{15,13},{14,10},{11,... | collective-permute-start | bytes 24584 | tf_op jit(solution)/shard_map/ppermute | solution.py:286
  6.0 2.9 %loaded.2 = (f32[1,2048]{1,0:T(1,128)S(1)}, s32[1,16]{1,0:T(1,128)S(1)}, bf16[1,2,2048,768]{3,2,1,0:T(8,128)(2,1)S(1)}, bf16[1,2,768]{2,1,0:T(2,128)(2,1)S(1)}) custom-call(f32[1,2048]{1,0:T(1,128)} %bitcast.5, s32[1,16]{1,0:T(1,128)} %bitcast.8, bf16[1,2,2048,768]{3,2,1,0:T(8,128)(2,1)} %refs_2_.1, bf16[1,2,768]{2,1,0:T(2,128)(2,1)} %refs_3_.1), custom_call_target="tpu_custom_call" | custom-call | bytes 6298656 | tf_op jit(solution)/shard_map/loaded/pallas_call | solution.py:171
  8.9 1.6 %collective-permute-done.6.table_ref = bf16[32,128]{1,0:T(8,128)(2,1)S(1)} collective-permute-done((bf16[32,128]{1,0:T(8,128)(2,1)S(1)}, bf16[32,128]{1,0:T(8,128)(2,1)S(1)}, u32[]{:S(2)}, u32[]{:S(2)}) %collective-permute-start.6) | collective-permute-done | bytes 8224 | tf_op jit(solution)/shard_map/ppermute | solution.py:286
  10.5 0.2 mended.1.refs_0_
  10.7 0.1 collective-permute-start.22
  10.7 1.9 %loaded.3 = (bf16[1,768,2048]{2,1,0:T(8,128)(2,1)S(1)}, bf16[1,2048]{1,0:T(2,128)(2,1)S(1)}) custom-call(bf16[1,768,2048]{2,1,0:T(8,128)(2,1)} %refs_0_.1, bf16[1,2048]{1,0:T(2,128)(2,1)} %refs_1_.1), custom_call_target="tpu_custom_call" | custom-call | bytes 3149824 | tf_op jit(solution)/shard_map/loaded/pallas_call | solution.py:171
  12.7 2.1 %collective-permute-start.7 = (bf16[2080,128]{1,0:T(8,128)(2,1)S(1)}, bf16[2080,128]{1,0:T(8,128)(2,1)S(1)}, u32[]{:S(2)}, u32[]{:S(2)}) collective-permute-start(bf16[2080,128]{1,0:T(8,128)(2,1)S(1)} %mended.1.refs_0_), channel_id=1, source_target_pairs={{0,4},{5,1},{4,8},{9,5},{8,12},{13,9},{12,14},{15,13},{14,10},{11,... | collective-permute-start | bytes 1597448 | tf_op jit(solution)/shard_map/ppermute | solution.py:286
  14.8 2.7 %visit.17 = (f32[128,2048]{1,0:T(8,128)S(1)}, bf16[128,2048]{1,0:T(8,128)(2,1)S(1)}) custom-call(s32[1,16]{1,0:T(1,128)S(1)} %get-tuple-element.27.owners_ref, bf16[2080,128]{1,0:T(8,128)(2,1)S(1)} %mended.1.refs_0_, bf16[2080,128]{1,0:T(8,128)(2,1)S(1)} %collective-permute-done.22.refs_1_, bf16[1,2,2048,768]{3,2,1,0:T(8,128)(2,1)S(1)} %get-tuple-element.29.refs_2_.refs_1_, ...), custom_call_target="tpu_custom_call" | custom-call | flops 2415919104 | bytes 1572864 | tf_op jit(solution)/shard_map/visit/pallas_call | solution.py:233
  17.5 0.2 collective-permute-start.23
  17.7 4.3 %collective-permute-done.7.refs_0_ = bf16[2080,128]{1,0:T(8,128)(2,1)S(1)} collective-permute-done((bf16[2080,128]{1,0:T(8,128)(2,1)S(1)}, bf16[2080,128]{1,0:T(8,128)(2,1)S(1)}, u32[]{:S(2)}, u32[]{:S(2)}) %collective-permute-start.7) | collective-permute-done | bytes 532512 | tf_op jit(solution)/shard_map/ppermute | solution.py:286
  22.0 2.1 %collective-permute-start.8 = (bf16[2080,128]{1,0:T(8,128)(2,1)S(1)}, bf16[2080,128]{1,0:T(8,128)(2,1)S(1)}, u32[]{:S(2)}, u32[]{:S(2)}) collective-permute-start(bf16[2080,128]{1,0:T(8,128)(2,1)S(1)} %collective-permute-done.7.refs_0_), channel_id=1, source_target_pairs={{0,4},{5,1},{4,8},{9,5},{8,12},{13,9},{12,14},{15,13},{14,10},{11,... | collective-permute-start | bytes 1597448 | tf_op jit(solution)/shard_map/ppermute | solution.py:286
  24.1 0.1 add_convert_fusion.4
  24.2 1.6 %collective-permute-start.24 = (bf16[128,2048]{1,0:T(8,128)(2,1)S(1)}, bf16[128,2048]{1,0:T(8,128)(2,1)S(1)}, u32[]{:S(2)}, u32[]{:S(2)}) collective-permute-start(bf16[128,2048]{1,0:T(8,128)(2,1)S(1)} %add_convert_fusion.4), channel_id=1, source_target_pairs={{0,4},{5,1},{4,8},{9,5},{8,12},{13,9},{12,14},{15,13},{14,10},{11,... | collective-permute-start | bytes 1572872 | tf_op jit(solution)/shard_map/ppermute | solution.py:315
  25.8 2.7 %visit.16 = (f32[128,2048]{1,0:T(8,128)S(1)}, bf16[128,2048]{1,0:T(8,128)(2,1)S(1)}) custom-call(s32[1,16]{1,0:T(1,128)S(1)} %get-tuple-element.27.owners_ref, bf16[2080,128]{1,0:T(8,128)(2,1)S(1)} %collective-permute-done.7.refs_0_, bf16[2080,128]{1,0:T(8,128)(2,1)S(1)} %collective-permute-done.20.refs_1_, ...), custom_call_target="tpu_custom_call" | custom-call | flops 2415919104 | bytes 1572864 | tf_op jit(solution)/shard_map/visit/pallas_call | solution.py:233
  28.5 0.1 collective-permute-start.21
  28.6 2.7 %collective-permute-done.8.refs_0_ = bf16[2080,128]{1,0:T(8,128)(2,1)S(1)} collective-permute-done((bf16[2080,128]{1,0:T(8,128)(2,1)S(1)}, bf16[2080,128]{1,0:T(8,128)(2,1)S(1)}, u32[]{:S(2)}, u32[]{:S(2)}) %collective-permute-start.8) | collective-permute-done | bytes 532512 | tf_op jit(solution)/shard_map/ppermute | solution.py:286
  31.3 2.1 %collective-permute-start.9 = (bf16[2080,128]{1,0:T(8,128)(2,1)S(1)}, bf16[2080,128]{1,0:T(8,128)(2,1)S(1)}, u32[]{:S(2)}, u32[]{:S(2)}) collective-permute-start(bf16[2080,128]{1,0:T(8,128)(2,1)S(1)} %collective-permute-done.8.refs_0_), channel_id=1, source_target_pairs={{0,4},{5,1},{4,8},{9,5},{8,12},{13,9},{12,14},{15,13},{14,10},{11,... | collective-permute-start | bytes 1597448 | tf_op jit(solution)/shard_map/ppermute | solution.py:286
  33.3 3.5 %collective-permute-done.24 = bf16[128,2048]{1,0:T(8,128)(2,1)S(1)} collective-permute-done((bf16[128,2048]{1,0:T(8,128)(2,1)S(1)}, bf16[128,2048]{1,0:T(8,128)(2,1)S(1)}, u32[]{:S(2)}, u32[]{:S(2)}) %collective-permute-start.24) | collective-permute-done | bytes 524320 | tf_op jit(solution)/shard_map/ppermute | solution.py:315
  36.9 0.2 add_convert_fusion.3
  37.1 2.1 %collective-permute-start.25 = (bf16[128,2048]{1,0:T(8,128)(2,1)S(1)}, bf16[128,2048]{1,0:T(8,128)(2,1)S(1)}, u32[]{:S(2)}, u32[]{:S(2)}) collective-permute-start(bf16[128,2048]{1,0:T(8,128)(2,1)S(1)} %add_convert_fusion.3), channel_id=1, source_target_pairs={{0,4},{5,1},{4,8},{9,5},{8,12},{13,9},{12,14},{15,13},{14,10},{11,... | collective-permute-start | bytes 1572872 | tf_op jit(solution)/shard_map/ppermute | solution.py:315
  39.2 2.7 %visit.15 = (f32[128,2048]{1,0:T(8,128)S(1)}, bf16[128,2048]{1,0:T(8,128)(2,1)S(1)}) custom-call(s32[1,16]{1,0:T(1,128)S(1)} %get-tuple-element.27.owners_ref, bf16[2080,128]{1,0:T(8,128)(2,1)S(1)} %collective-permute-done.8.refs_0_, bf16[2080,128]{1,0:T(8,128)(2,1)S(1)} %collective-permute-done.18.refs_1_, ...), custom_call_target="tpu_custom_call" | custom-call | flops 2415919104 | bytes 1572864 | tf_op jit(solution)/shard_map/visit/pallas_call | solution.py:233
  41.9 0.1 collective-permute-start.19
  42.0 0.6 collective-permute-done.9.refs_0_
  42.6 2.1 %collective-permute-start.10 = (bf16[2080,128]{1,0:T(8,128)(2,1)S(1)}, bf16[2080,128]{1,0:T(8,128)(2,1)S(1)}, u32[]{:S(2)}, u32[]{:S(2)}) collective-permute-start(bf16[2080,128]{1,0:T(8,128)(2,1)S(1)} %collective-permute-done.9.refs_0_), channel_id=1, source_target_pairs={{0,4},{5,1},{4,8},{9,5},{8,12},{13,9},{12,14},{15,13},{14,10},{11,... | collective-permute-start | bytes 1597448 | tf_op jit(solution)/shard_map/ppermute | solution.py:286
  44.7 3.5 %collective-permute-done.25 = bf16[128,2048]{1,0:T(8,128)(2,1)S(1)} collective-permute-done((bf16[128,2048]{1,0:T(8,128)(2,1)S(1)}, bf16[128,2048]{1,0:T(8,128)(2,1)S(1)}, u32[]{:S(2)}, u32[]{:S(2)}) %collective-permute-start.25) | collective-permute-done | bytes 524320 | tf_op jit(solution)/shard_map/ppermute | solution.py:315
  48.2 0.2 add_convert_fusion.2
  48.4 2.1 %collective-permute-start.26 = (bf16[128,2048]{1,0:T(8,128)(2,1)S(1)}, bf16[128,2048]{1,0:T(8,128)(2,1)S(1)}, u32[]{:S(2)}, u32[]{:S(2)}) collective-permute-start(bf16[128,2048]{1,0:T(8,128)(2,1)S(1)} %add_convert_fusion.2), channel_id=1, source_target_pairs={{0,4},{5,1},{4,8},{9,5},{8,12},{13,9},{12,14},{15,13},{14,10},{11,... | collective-permute-start | bytes 1572872 | tf_op jit(solution)/shard_map/ppermute | solution.py:315
  50.5 2.7 %visit.14 = (f32[128,2048]{1,0:T(8,128)S(1)}, bf16[128,2048]{1,0:T(8,128)(2,1)S(1)}) custom-call(s32[1,16]{1,0:T(1,128)S(1)} %get-tuple-element.27.owners_ref, bf16[2080,128]{1,0:T(8,128)(2,1)S(1)} %collective-permute-done.9.refs_0_, bf16[2080,128]{1,0:T(8,128)(2,1)S(1)} %collective-permute-done.16.refs_1_, ...), custom_call_target="tpu_custom_call" | custom-call | flops 2415919104 | bytes 1572864 | tf_op jit(solution)/shard_map/visit/pallas_call | solution.py:233
  53.2 0.1 collective-permute-start.17
  53.3 0.6 collective-permute-done.10.refs_0_
  53.9 2.0 %collective-permute-start.2 = (bf16[2080,128]{1,0:T(8,128)(2,1)S(1)}, bf16[2080,128]{1,0:T(8,128)(2,1)S(1)}, u32[]{:S(2)}, u32[]{:S(2)}) collective-permute-start(bf16[2080,128]{1,0:T(8,128)(2,1)S(1)} %get-tuple-element.28.refs_0_), channel_id=1, source_target_pairs={{4,0},{1,5},{8,4},{5,9},{12,8},{9,13},{14,12},{13,15},{10,14},{15,... | collective-permute-start | bytes 1597448 | tf_op jit(solution)/shard_map/ppermute | solution.py:286
  55.9 0.1 collective-permute-start.11
  56.0 5.8 %collective-permute-done.26 = bf16[128,2048]{1,0:T(8,128)(2,1)S(1)} collective-permute-done((bf16[128,2048]{1,0:T(8,128)(2,1)S(1)}, bf16[128,2048]{1,0:T(8,128)(2,1)S(1)}, u32[]{:S(2)}, u32[]{:S(2)}) %collective-permute-start.26) | collective-permute-done | bytes 524320 | tf_op jit(solution)/shard_map/ppermute | solution.py:315
  61.8 0.2 add_convert_fusion.1
  62.0 2.6 %collective-permute-start.27 = (bf16[128,2048]{1,0:T(8,128)(2,1)S(1)}, bf16[128,2048]{1,0:T(8,128)(2,1)S(1)}, u32[]{:S(2)}, u32[]{:S(2)}) collective-permute-start(bf16[128,2048]{1,0:T(8,128)(2,1)S(1)} %add_convert_fusion.1), channel_id=1, source_target_pairs={{0,4},{5,1},{4,8},{9,5},{8,12},{13,9},{12,14},{15,13},{14,10},{11,... | collective-permute-start | bytes 1572872 | tf_op jit(solution)/shard_map/ppermute | solution.py:315
  64.6 2.7 %visit.13 = (f32[128,2048]{1,0:T(8,128)S(1)}, bf16[128,2048]{1,0:T(8,128)(2,1)S(1)}) custom-call(s32[1,16]{1,0:T(1,128)S(1)} %get-tuple-element.27.owners_ref, bf16[2080,128]{1,0:T(8,128)(2,1)S(1)} %collective-permute-done.10.refs_0_, bf16[2080,128]{1,0:T(8,128)(2,1)S(1)} %collective-permute-done.14.refs_1_, ...), custom_call_target="tpu_custom_call" | custom-call | flops 2415919104 | bytes 1572864 | tf_op jit(solution)/shard_map/visit/pallas_call | solution.py:233
  67.3 0.1 collective-permute-start.15
  67.3 3.6 %collective-permute-done.11.refs_0_ = bf16[2080,128]{1,0:T(8,128)(2,1)S(1)} collective-permute-done((bf16[2080,128]{1,0:T(8,128)(2,1)S(1)}, bf16[2080,128]{1,0:T(8,128)(2,1)S(1)}, u32[]{:S(2)}, u32[]{:S(2)}) %collective-permute-start.11) | collective-permute-done | bytes 532512 | tf_op jit(solution)/shard_map/ppermute | solution.py:286
  70.9 0.5 collective-permute-start
  71.5 5.1 %collective-permute-done.27 = bf16[128,2048]{1,0:T(8,128)(2,1)S(1)} collective-permute-done((bf16[128,2048]{1,0:T(8,128)(2,1)S(1)}, bf16[128,2048]{1,0:T(8,128)(2,1)S(1)}, u32[]{:S(2)}, u32[]{:S(2)}) %collective-permute-start.27) | collective-permute-done | bytes 524320 | tf_op jit(solution)/shard_map/ppermute | solution.py:315
  76.6 0.2 add_convert_fusion
  76.8 2.1 %collective-permute-start.28 = (bf16[128,2048]{1,0:T(8,128)(2,1)S(1)}, bf16[128,2048]{1,0:T(8,128)(2,1)S(1)}, u32[]{:S(2)}, u32[]{:S(2)}) collective-permute-start(bf16[128,2048]{1,0:T(8,128)(2,1)S(1)} %add_convert_fusion), channel_id=1, source_target_pairs={{0,4},{5,1},{4,8},{9,5},{8,12},{13,9},{12,14},{15,13},{14,10},{11,... | collective-permute-start | bytes 1572872 | tf_op jit(solution)/shard_map/ppermute | solution.py:315
  78.9 1.5 %visit.12 = bf16[128,2048]{1,0:T(8,128)(2,1)S(1)} custom-call(s32[1,16]{1,0:T(1,128)S(1)} %get-tuple-element.27.owners_ref, bf16[2080,128]{1,0:T(8,128)(2,1)S(1)} %collective-permute-done.12.refs_0_, bf16[1,2,2048,768]{3,2,1,0:T(8,128)(2,1)S(1)} %get-tuple-element.29.refs_2_.refs_1_, bf16[1,2,768]{2,1,0:T(2,128)(2,1)S(1)} %get-tuple-element.30.refs_3_.refs_2_, ...), custom_call_target="tpu_custom_call" | custom-call | flops 1207959552 | bytes 786432 | tf_op jit(solution)/shard_map/visit/pallas_call | solution.py:233
  80.4 0.1 collective-permute-start.13
  80.5 2.7 %visit.9 = (f32[128,2048]{1,0:T(8,128)S(1)}, bf16[128,2048]{1,0:T(8,128)(2,1)S(1)}) custom-call(s32[1,16]{1,0:T(1,128)S(1)} %get-tuple-element.27.owners_ref, bf16[2080,128]{1,0:T(8,128)(2,1)S(1)} %get-tuple-element.28.refs_0_, bf16[2080,128]{1,0:T(8,128)(2,1)S(1)} %collective-permute-done.refs_1_, ...), custom_call_target="tpu_custom_call" | custom-call | flops 2415919104 | bytes 1572864 | tf_op jit(solution)/shard_map/visit/pallas_call | solution.py:233
  83.2 0.6 collective-permute-start.1
  83.7 2.7 %visit.10 = (f32[128,2048]{1,0:T(8,128)S(1)}, bf16[128,2048]{1,0:T(8,128)(2,1)S(1)}) custom-call(s32[1,16]{1,0:T(1,128)S(1)} %get-tuple-element.27.owners_ref, bf16[2080,128]{1,0:T(8,128)(2,1)S(1)} %collective-permute-done.2.refs_0_, bf16[2080,128]{1,0:T(8,128)(2,1)S(1)} %collective-permute-done.3.refs_1_, ...), custom_call_target="tpu_custom_call" | custom-call | flops 2415919104 | bytes 1572864 | tf_op jit(solution)/shard_map/visit/pallas_call | solution.py:233
  86.4 0.1 collective-permute-start.4
  86.5 1.5 %visit.11 = f32[128,2048]{1,0:T(8,128)S(1)} custom-call(s32[1,16]{1,0:T(1,128)S(1)} %get-tuple-element.27.owners_ref, bf16[2080,128]{1,0:T(8,128)(2,1)S(1)} %collective-permute-done.11.refs_0_, bf16[1,2,2048,768]{3,2,1,0:T(8,128)(2,1)S(1)} %get-tuple-element.29.refs_2_.refs_1_, bf16[1,2,768]{2,1,0:T(2,128)(2,1)S(1)} %get-tuple-element.30.refs_3_.refs_2_, ...), custom_call_target="tpu_custom_call" | custom-call | flops 1207959552 | bytes 786432 | tf_op jit(solution)/shard_map/visit/pallas_call | solution.py:233
  88.0 0.1 fusion.1
  88.1 1.6 %collective-permute-start.33 = (bf16[56,2048]{1,0:T(8,128)(2,1)S(1)}, bf16[56,2048]{1,0:T(8,128)(2,1)S(1)}, u32[]{:S(2)}, u32[]{:S(2)}) collective-permute-start(bf16[56,2048]{1,0:T(8,128)(2,1)S(1)} %fusion.1), channel_id=1, source_target_pairs={{0,4},{5,1},{4,8},{9,5},{8,12},{13,9},{12,14},{15,13},{14,10},{11,... | collective-permute-start | bytes 688136 | tf_op jit(solution)/shard_map/ppermute | solution.py:320
  89.8 1.6 %collective-permute-start.31 = (bf16[40,2048]{1,0:T(8,128)(2,1)S(1)}, bf16[40,2048]{1,0:T(8,128)(2,1)S(1)}, u32[]{:S(2)}, u32[]{:S(2)}) collective-permute-start(bf16[40,2048]{1,0:T(8,128)(2,1)S(1)} %fusion.3), channel_id=1, source_target_pairs={{0,4},{5,1},{4,8},{9,5},{8,12},{13,9},{12,14},{15,13},{14,10},{11,... | collective-permute-start | bytes 491528 | tf_op jit(solution)/shard_map/ppermute | solution.py:320
  91.5 1.6 %collective-permute-start.29 = (bf16[32,2048]{1,0:T(8,128)(2,1)S(1)}, bf16[32,2048]{1,0:T(8,128)(2,1)S(1)}, u32[]{:S(2)}, u32[]{:S(2)}) collective-permute-start(bf16[32,2048]{1,0:T(8,128)(2,1)S(1)} %fusion.5), channel_id=1, source_target_pairs={{0,4},{5,1},{4,8},{9,5},{8,12},{13,9},{12,14},{15,13},{14,10},{11,... | collective-permute-start | bytes 393224 | tf_op jit(solution)/shard_map/ppermute | solution.py:320
  93.1 2.9 %collective-permute-done.31 = bf16[40,2048]{1,0:T(8,128)(2,1)S(1)} collective-permute-done((bf16[40,2048]{1,0:T(8,128)(2,1)S(1)}, bf16[40,2048]{1,0:T(8,128)(2,1)S(1)}, u32[]{:S(2)}, u32[]{:S(2)}) %collective-permute-start.31) | collective-permute-done | bytes 163872 | tf_op jit(solution)/shard_map/ppermute | solution.py:320
  96.0 1.6 %collective-permute-start.32 = (bf16[40,2048]{1,0:T(8,128)(2,1)S(1)}, bf16[40,2048]{1,0:T(8,128)(2,1)S(1)}, u32[]{:S(2)}, u32[]{:S(2)}) collective-permute-start(bf16[40,2048]{1,0:T(8,128)(2,1)S(1)} %add_convert_fusion.6), channel_id=1, source_target_pairs={{0,4},{5,1},{4,8},{9,5},{8,12},{13,9},{12,14},{15,13},{14,10},{11,... | collective-permute-start | bytes 491528 | tf_op jit(solution)/shard_map/ppermute | solution.py:320
  97.6 0.1 add_convert_fusion.5
  97.7 1.6 %collective-permute-start.34 = (bf16[56,2048]{1,0:T(8,128)(2,1)S(1)}, bf16[56,2048]{1,0:T(8,128)(2,1)S(1)}, u32[]{:S(2)}, u32[]{:S(2)}) collective-permute-start(bf16[56,2048]{1,0:T(8,128)(2,1)S(1)} %add_convert_fusion.5), channel_id=1, source_target_pairs={{0,4},{5,1},{4,8},{9,5},{8,12},{13,9},{12,14},{15,13},{14,10},{11,... | collective-permute-start | bytes 688136 | tf_op jit(solution)/shard_map/ppermute | solution.py:320
  99.4 1.6 %collective-permute-start.30 = (bf16[32,2048]{1,0:T(8,128)(2,1)S(1)}, bf16[32,2048]{1,0:T(8,128)(2,1)S(1)}, u32[]{:S(2)}, u32[]{:S(2)}) collective-permute-start(bf16[32,2048]{1,0:T(8,128)(2,1)S(1)} %add_convert_fusion.7), channel_id=1, source_target_pairs={{0,4},{5,1},{4,8},{9,5},{8,12},{13,9},{12,14},{15,13},{14,10},{11,... | collective-permute-start | bytes 393224 | tf_op jit(solution)/shard_map/ppermute | solution.py:320
  101.0 2.8 %collective-permute-done.34.arrived_ref = bf16[56,2048]{1,0:T(8,128)(2,1)S(1)} collective-permute-done((bf16[56,2048]{1,0:T(8,128)(2,1)S(1)}, bf16[56,2048]{1,0:T(8,128)(2,1)S(1)}, u32[]{:S(2)}, u32[]{:S(2)}) %collective-permute-start.34) | collective-permute-done | bytes 229408 | tf_op jit(solution)/shard_map/ppermute | solution.py:320
  103.8 0.8 finished.3.refs_0_
  104.6 0.7 finished.4.refs_0_
  105.4 0.7 finished.5
  (33 shorter events, 0.3 us)
Async XLA Ops:
  0.0 10.5 %collective-permute-start.5 = (bf16[128,2048]{1,0:T(8,128)(2,1)}, bf16[128,2048]{1,0:T(8,128)(2,1)S(1)}, u32[]{:S(2)}, u32[]{:S(2)}) collective-permute-start(bf16[128,2048]{1,0:T(8,128)(2,1)} %tokens_hbm.1), channel_id=1, source_target_pairs={{0,4},{5,1},{4,8},{9,5},{8,12},{13,9},{12,14},{15,13},{14,10},{11,... | collective-permute-start | bytes 1572872 | tf_op jit(solution)/shard_map/ppermute | solution.py:286
  4.4 6.1 %collective-permute-start.6 = (bf16[32,128]{1,0:T(8,128)(2,1)S(1)}, bf16[32,128]{1,0:T(8,128)(2,1)S(1)}, u32[]{:S(2)}, u32[]{:S(2)}) collective-permute-start(bf16[32,128]{1,0:T(8,128)(2,1)S(1)} %get-tuple-element.37), channel_id=1, source_target_pairs={{0,4},{5,1},{4,8},{9,5},{8,12},{13,9},{12,14},{15,13},{14,10},{11,... | collective-permute-start | bytes 24584 | tf_op jit(solution)/shard_map/ppermute | solution.py:286
  10.7 4.1 %collective-permute-start.22 = (bf16[2080,128]{1,0:T(8,128)(2,1)S(1)}, bf16[2080,128]{1,0:T(8,128)(2,1)S(1)}, u32[]{:S(2)}, u32[]{:S(2)}) collective-permute-start(bf16[2080,128]{1,0:T(8,128)(2,1)S(1)} %mended.1.refs_0_), channel_id=1, source_target_pairs={{0,1},{1,0},{2,3},{3,2},{4,5},{5,4},{6,7},{7,6},{8,9},{9,8},{10,11... | collective-permute-start | bytes 1597448 | tf_op jit(solution)/shard_map/ppermute | solution.py:286
  12.7 9.3 %collective-permute-start.7 = (bf16[2080,128]{1,0:T(8,128)(2,1)S(1)}, bf16[2080,128]{1,0:T(8,128)(2,1)S(1)}, u32[]{:S(2)}, u32[]{:S(2)}) collective-permute-start(bf16[2080,128]{1,0:T(8,128)(2,1)S(1)} %mended.1.refs_0_), channel_id=1, source_target_pairs={{0,4},{5,1},{4,8},{9,5},{8,12},{13,9},{12,14},{15,13},{14,10},{11,... | collective-permute-start | bytes 1597448 | tf_op jit(solution)/shard_map/ppermute | solution.py:286
  17.5 6.6 %collective-permute-start.23 = (bf16[128,2048]{1,0:T(8,128)(2,1)S(1)}, bf16[128,2048]{1,0:T(8,128)(2,1)S(1)}, u32[]{:S(2)}, u32[]{:S(2)}) collective-permute-start(bf16[128,2048]{1,0:T(8,128)(2,1)S(1)} %get-tuple-element.48), channel_id=1, source_target_pairs={{0,1},{1,0},{2,3},{3,2},{4,5},{5,4},{6,7},{7,6},{8,9},{9,8},{10,11... | collective-permute-start | bytes 1572872 | tf_op jit(solution)/shard_map/ppermute | solution.py:286
  22.0 3.8 %collective-permute-start.20 = (bf16[2080,128]{1,0:T(8,128)(2,1)S(1)}, bf16[2080,128]{1,0:T(8,128)(2,1)S(1)}, u32[]{:S(2)}, u32[]{:S(2)}) collective-permute-start(bf16[2080,128]{1,0:T(8,128)(2,1)S(1)} %collective-permute-done.7.refs_0_), channel_id=1, source_target_pairs={{0,1},{1,0},{2,3},{3,2},{4,5},{5,4},{6,7},{7,6},{8,9},{9,8},{10,11... | collective-permute-start | bytes 1597448 | tf_op jit(solution)/shard_map/ppermute | solution.py:286
  22.0 9.3 %collective-permute-start.8 = (bf16[2080,128]{1,0:T(8,128)(2,1)S(1)}, bf16[2080,128]{1,0:T(8,128)(2,1)S(1)}, u32[]{:S(2)}, u32[]{:S(2)}) collective-permute-start(bf16[2080,128]{1,0:T(8,128)(2,1)S(1)} %collective-permute-done.7.refs_0_), channel_id=1, source_target_pairs={{0,4},{5,1},{4,8},{9,5},{8,12},{13,9},{12,14},{15,13},{14,10},{11,... | collective-permute-start | bytes 1597448 | tf_op jit(solution)/shard_map/ppermute | solution.py:286
  24.2 12.7 %collective-permute-start.24 = (bf16[128,2048]{1,0:T(8,128)(2,1)S(1)}, bf16[128,2048]{1,0:T(8,128)(2,1)S(1)}, u32[]{:S(2)}, u32[]{:S(2)}) collective-permute-start(bf16[128,2048]{1,0:T(8,128)(2,1)S(1)} %add_convert_fusion.4), channel_id=1, source_target_pairs={{0,4},{5,1},{4,8},{9,5},{8,12},{13,9},{12,14},{15,13},{14,10},{11,... | collective-permute-start | bytes 1572872 | tf_op jit(solution)/shard_map/ppermute | solution.py:315
  28.5 8.4 %collective-permute-start.21 = (bf16[128,2048]{1,0:T(8,128)(2,1)S(1)}, bf16[128,2048]{1,0:T(8,128)(2,1)S(1)}, u32[]{:S(2)}, u32[]{:S(2)}) collective-permute-start(bf16[128,2048]{1,0:T(8,128)(2,1)S(1)} %get-tuple-element.46), channel_id=1, source_target_pairs={{0,1},{1,0},{2,3},{3,2},{4,5},{5,4},{6,7},{7,6},{8,9},{9,8},{10,11... | collective-permute-start | bytes 1572872 | tf_op jit(solution)/shard_map/ppermute | solution.py:286
  31.3 8.0 %collective-permute-start.18 = (bf16[2080,128]{1,0:T(8,128)(2,1)S(1)}, bf16[2080,128]{1,0:T(8,128)(2,1)S(1)}, u32[]{:S(2)}, u32[]{:S(2)}) collective-permute-start(bf16[2080,128]{1,0:T(8,128)(2,1)S(1)} %collective-permute-done.8.refs_0_), channel_id=1, source_target_pairs={{0,1},{1,0},{2,3},{3,2},{4,5},{5,4},{6,7},{7,6},{8,9},{9,8},{10,11... | collective-permute-start | bytes 1597448 | tf_op jit(solution)/shard_map/ppermute | solution.py:286
  31.3 11.3 %collective-permute-start.9 = (bf16[2080,128]{1,0:T(8,128)(2,1)S(1)}, bf16[2080,128]{1,0:T(8,128)(2,1)S(1)}, u32[]{:S(2)}, u32[]{:S(2)}) collective-permute-start(bf16[2080,128]{1,0:T(8,128)(2,1)S(1)} %collective-permute-done.8.refs_0_), channel_id=1, source_target_pairs={{0,4},{5,1},{4,8},{9,5},{8,12},{13,9},{12,14},{15,13},{14,10},{11,... | collective-permute-start | bytes 1597448 | tf_op jit(solution)/shard_map/ppermute | solution.py:286
  37.1 11.1 %collective-permute-start.25 = (bf16[128,2048]{1,0:T(8,128)(2,1)S(1)}, bf16[128,2048]{1,0:T(8,128)(2,1)S(1)}, u32[]{:S(2)}, u32[]{:S(2)}) collective-permute-start(bf16[128,2048]{1,0:T(8,128)(2,1)S(1)} %add_convert_fusion.3), channel_id=1, source_target_pairs={{0,4},{5,1},{4,8},{9,5},{8,12},{13,9},{12,14},{15,13},{14,10},{11,... | collective-permute-start | bytes 1572872 | tf_op jit(solution)/shard_map/ppermute | solution.py:315
  41.9 6.3 %collective-permute-start.19 = (bf16[128,2048]{1,0:T(8,128)(2,1)S(1)}, bf16[128,2048]{1,0:T(8,128)(2,1)S(1)}, u32[]{:S(2)}, u32[]{:S(2)}) collective-permute-start(bf16[128,2048]{1,0:T(8,128)(2,1)S(1)} %get-tuple-element.44), channel_id=1, source_target_pairs={{0,1},{1,0},{2,3},{3,2},{4,5},{5,4},{6,7},{7,6},{8,9},{9,8},{10,11... | collective-permute-start | bytes 1572872 | tf_op jit(solution)/shard_map/ppermute | solution.py:286
  42.6 8.0 %collective-permute-start.16 = (bf16[2080,128]{1,0:T(8,128)(2,1)S(1)}, bf16[2080,128]{1,0:T(8,128)(2,1)S(1)}, u32[]{:S(2)}, u32[]{:S(2)}) collective-permute-start(bf16[2080,128]{1,0:T(8,128)(2,1)S(1)} %collective-permute-done.9.refs_0_), channel_id=1, source_target_pairs={{0,1},{1,0},{2,3},{3,2},{4,5},{5,4},{6,7},{7,6},{8,9},{9,8},{10,11... | collective-permute-start | bytes 1597448 | tf_op jit(solution)/shard_map/ppermute | solution.py:286
  42.6 11.3 %collective-permute-start.10 = (bf16[2080,128]{1,0:T(8,128)(2,1)S(1)}, bf16[2080,128]{1,0:T(8,128)(2,1)S(1)}, u32[]{:S(2)}, u32[]{:S(2)}) collective-permute-start(bf16[2080,128]{1,0:T(8,128)(2,1)S(1)} %collective-permute-done.9.refs_0_), channel_id=1, source_target_pairs={{0,4},{5,1},{4,8},{9,5},{8,12},{13,9},{12,14},{15,13},{14,10},{11,... | collective-permute-start | bytes 1597448 | tf_op jit(solution)/shard_map/ppermute | solution.py:286
  48.4 13.3 %collective-permute-start.26 = (bf16[128,2048]{1,0:T(8,128)(2,1)S(1)}, bf16[128,2048]{1,0:T(8,128)(2,1)S(1)}, u32[]{:S(2)}, u32[]{:S(2)}) collective-permute-start(bf16[128,2048]{1,0:T(8,128)(2,1)S(1)} %add_convert_fusion.2), channel_id=1, source_target_pairs={{0,4},{5,1},{4,8},{9,5},{8,12},{13,9},{12,14},{15,13},{14,10},{11,... | collective-permute-start | bytes 1572872 | tf_op jit(solution)/shard_map/ppermute | solution.py:315
  53.2 8.5 %collective-permute-start.17 = (bf16[128,2048]{1,0:T(8,128)(2,1)S(1)}, bf16[128,2048]{1,0:T(8,128)(2,1)S(1)}, u32[]{:S(2)}, u32[]{:S(2)}) collective-permute-start(bf16[128,2048]{1,0:T(8,128)(2,1)S(1)} %get-tuple-element.42), channel_id=1, source_target_pairs={{0,1},{1,0},{2,3},{3,2},{4,5},{5,4},{6,7},{7,6},{8,9},{9,8},{10,11... | collective-permute-start | bytes 1572872 | tf_op jit(solution)/shard_map/ppermute | solution.py:286
  53.9 10.6 %collective-permute-start.14 = (bf16[2080,128]{1,0:T(8,128)(2,1)S(1)}, bf16[2080,128]{1,0:T(8,128)(2,1)S(1)}, u32[]{:S(2)}, u32[]{:S(2)}) collective-permute-start(bf16[2080,128]{1,0:T(8,128)(2,1)S(1)} %collective-permute-done.10.refs_0_), channel_id=1, source_target_pairs={{0,1},{1,0},{2,3},{3,2},{4,5},{5,4},{6,7},{7,6},{8,9},{9,8},{10,11... | collective-permute-start | bytes 1597448 | tf_op jit(solution)/shard_map/ppermute | solution.py:286
  53.9 17.5 %collective-permute-start.2 = (bf16[2080,128]{1,0:T(8,128)(2,1)S(1)}, bf16[2080,128]{1,0:T(8,128)(2,1)S(1)}, u32[]{:S(2)}, u32[]{:S(2)}) collective-permute-start(bf16[2080,128]{1,0:T(8,128)(2,1)S(1)} %get-tuple-element.28.refs_0_), channel_id=1, source_target_pairs={{4,0},{1,5},{8,4},{5,9},{12,8},{9,13},{14,12},{13,15},{10,14},{15,... | collective-permute-start | bytes 1597448 | tf_op jit(solution)/shard_map/ppermute | solution.py:286
  55.9 15.0 %collective-permute-start.11 = (bf16[2080,128]{1,0:T(8,128)(2,1)S(1)}, bf16[2080,128]{1,0:T(8,128)(2,1)S(1)}, u32[]{:S(2)}, u32[]{:S(2)}) collective-permute-start(bf16[2080,128]{1,0:T(8,128)(2,1)S(1)} %collective-permute-done.10.refs_0_), channel_id=1, source_target_pairs={{0,4},{5,1},{4,8},{9,5},{8,12},{13,9},{12,14},{15,13},{14,10},{11,... | collective-permute-start | bytes 1597448 | tf_op jit(solution)/shard_map/ppermute | solution.py:286
  62.0 14.6 %collective-permute-start.27 = (bf16[128,2048]{1,0:T(8,128)(2,1)S(1)}, bf16[128,2048]{1,0:T(8,128)(2,1)S(1)}, u32[]{:S(2)}, u32[]{:S(2)}) collective-permute-start(bf16[128,2048]{1,0:T(8,128)(2,1)S(1)} %add_convert_fusion.1), channel_id=1, source_target_pairs={{0,4},{5,1},{4,8},{9,5},{8,12},{13,9},{12,14},{15,13},{14,10},{11,... | collective-permute-start | bytes 1572872 | tf_op jit(solution)/shard_map/ppermute | solution.py:315
  67.3 9.3 %collective-permute-start.15 = (bf16[128,2048]{1,0:T(8,128)(2,1)S(1)}, bf16[128,2048]{1,0:T(8,128)(2,1)S(1)}, u32[]{:S(2)}, u32[]{:S(2)}) collective-permute-start(bf16[128,2048]{1,0:T(8,128)(2,1)S(1)} %get-tuple-element.40), channel_id=1, source_target_pairs={{0,1},{1,0},{2,3},{3,2},{4,5},{5,4},{6,7},{7,6},{8,9},{9,8},{10,11... | collective-permute-start | bytes 1572872 | tf_op jit(solution)/shard_map/ppermute | solution.py:286
  70.9 8.0 %collective-permute-start.12 = (bf16[2080,128]{1,0:T(8,128)(2,1)S(1)}, bf16[2080,128]{1,0:T(8,128)(2,1)S(1)}, u32[]{:S(2)}, u32[]{:S(2)}) collective-permute-start(bf16[2080,128]{1,0:T(8,128)(2,1)S(1)} %collective-permute-done.11.refs_0_), channel_id=1, source_target_pairs={{0,1},{1,0},{2,3},{3,2},{4,5},{5,4},{6,7},{7,6},{8,9},{9,8},{10,11... | collective-permute-start | bytes 1597448 | tf_op jit(solution)/shard_map/ppermute | solution.py:286
  70.9 9.5 %collective-permute-start = (bf16[2080,128]{1,0:T(8,128)(2,1)S(1)}, bf16[2080,128]{1,0:T(8,128)(2,1)S(1)}, u32[]{:S(2)}, u32[]{:S(2)}) collective-permute-start(bf16[2080,128]{1,0:T(8,128)(2,1)S(1)} %get-tuple-element.28.refs_0_), channel_id=1, source_target_pairs={{0,1},{1,0},{2,3},{3,2},{4,5},{5,4},{6,7},{7,6},{8,9},{9,8},{10,11... | collective-permute-start | bytes 1597448 | tf_op jit(solution)/shard_map/ppermute | solution.py:286
  71.5 12.3 %collective-permute-start.3 = (bf16[2080,128]{1,0:T(8,128)(2,1)S(1)}, bf16[2080,128]{1,0:T(8,128)(2,1)S(1)}, u32[]{:S(2)}, u32[]{:S(2)}) collective-permute-start(bf16[2080,128]{1,0:T(8,128)(2,1)S(1)} %collective-permute-done.2.refs_0_), channel_id=1, source_target_pairs={{0,1},{1,0},{2,3},{3,2},{4,5},{5,4},{6,7},{7,6},{8,9},{9,8},{10,11... | collective-permute-start | bytes 1597448 | tf_op jit(solution)/shard_map/ppermute | solution.py:286
  76.8 11.3 %collective-permute-start.28 = (bf16[128,2048]{1,0:T(8,128)(2,1)S(1)}, bf16[128,2048]{1,0:T(8,128)(2,1)S(1)}, u32[]{:S(2)}, u32[]{:S(2)}) collective-permute-start(bf16[128,2048]{1,0:T(8,128)(2,1)S(1)} %add_convert_fusion), channel_id=1, source_target_pairs={{0,4},{5,1},{4,8},{9,5},{8,12},{13,9},{12,14},{15,13},{14,10},{11,... | collective-permute-start | bytes 1572872 | tf_op jit(solution)/shard_map/ppermute | solution.py:315
  80.4 7.6 %collective-permute-start.13 = (bf16[128,2048]{1,0:T(8,128)(2,1)S(1)}, bf16[128,2048]{1,0:T(8,128)(2,1)S(1)}, u32[]{:S(2)}, u32[]{:S(2)}) collective-permute-start(bf16[128,2048]{1,0:T(8,128)(2,1)S(1)} %visit.12), channel_id=1, source_target_pairs={{0,1},{1,0},{2,3},{3,2},{4,5},{5,4},{6,7},{7,6},{8,9},{9,8},{10,11... | collective-permute-start | bytes 1572872 | tf_op jit(solution)/shard_map/ppermute | solution.py:286
  83.2 17.8 %collective-permute-start.1 = (bf16[128,2048]{1,0:T(8,128)(2,1)S(1)}, bf16[128,2048]{1,0:T(8,128)(2,1)S(1)}, u32[]{:S(2)}, u32[]{:S(2)}) collective-permute-start(bf16[128,2048]{1,0:T(8,128)(2,1)S(1)} %get-tuple-element.34), channel_id=1, source_target_pairs={{0,1},{1,0},{2,3},{3,2},{4,5},{5,4},{6,7},{7,6},{8,9},{9,8},{10,11... | collective-permute-start | bytes 1572872 | tf_op jit(solution)/shard_map/ppermute | solution.py:286
  86.4 6.7 %collective-permute-start.4 = (bf16[128,2048]{1,0:T(8,128)(2,1)S(1)}, bf16[128,2048]{1,0:T(8,128)(2,1)S(1)}, u32[]{:S(2)}, u32[]{:S(2)}) collective-permute-start(bf16[128,2048]{1,0:T(8,128)(2,1)S(1)} %get-tuple-element.36), channel_id=1, source_target_pairs={{0,1},{1,0},{2,3},{3,2},{4,5},{5,4},{6,7},{7,6},{8,9},{9,8},{10,11... | collective-permute-start | bytes 1572872 | tf_op jit(solution)/shard_map/ppermute | solution.py:286
  88.1 9.5 %collective-permute-start.33 = (bf16[56,2048]{1,0:T(8,128)(2,1)S(1)}, bf16[56,2048]{1,0:T(8,128)(2,1)S(1)}, u32[]{:S(2)}, u32[]{:S(2)}) collective-permute-start(bf16[56,2048]{1,0:T(8,128)(2,1)S(1)} %fusion.1), channel_id=1, source_target_pairs={{0,4},{5,1},{4,8},{9,5},{8,12},{13,9},{12,14},{15,13},{14,10},{11,... | collective-permute-start | bytes 688136 | tf_op jit(solution)/shard_map/ppermute | solution.py:320
  89.8 6.1 %collective-permute-start.31 = (bf16[40,2048]{1,0:T(8,128)(2,1)S(1)}, bf16[40,2048]{1,0:T(8,128)(2,1)S(1)}, u32[]{:S(2)}, u32[]{:S(2)}) collective-permute-start(bf16[40,2048]{1,0:T(8,128)(2,1)S(1)} %fusion.3), channel_id=1, source_target_pairs={{0,4},{5,1},{4,8},{9,5},{8,12},{13,9},{12,14},{15,13},{14,10},{11,... | collective-permute-start | bytes 491528 | tf_op jit(solution)/shard_map/ppermute | solution.py:320
  91.5 7.9 %collective-permute-start.29 = (bf16[32,2048]{1,0:T(8,128)(2,1)S(1)}, bf16[32,2048]{1,0:T(8,128)(2,1)S(1)}, u32[]{:S(2)}, u32[]{:S(2)}) collective-permute-start(bf16[32,2048]{1,0:T(8,128)(2,1)S(1)} %fusion.5), channel_id=1, source_target_pairs={{0,4},{5,1},{4,8},{9,5},{8,12},{13,9},{12,14},{15,13},{14,10},{11,... | collective-permute-start | bytes 393224 | tf_op jit(solution)/shard_map/ppermute | solution.py:320
  96.0 8.6 %collective-permute-start.32 = (bf16[40,2048]{1,0:T(8,128)(2,1)S(1)}, bf16[40,2048]{1,0:T(8,128)(2,1)S(1)}, u32[]{:S(2)}, u32[]{:S(2)}) collective-permute-start(bf16[40,2048]{1,0:T(8,128)(2,1)S(1)} %add_convert_fusion.6), channel_id=1, source_target_pairs={{0,4},{5,1},{4,8},{9,5},{8,12},{13,9},{12,14},{15,13},{14,10},{11,... | collective-permute-start | bytes 491528 | tf_op jit(solution)/shard_map/ppermute | solution.py:320
  97.7 6.1 %collective-permute-start.34 = (bf16[56,2048]{1,0:T(8,128)(2,1)S(1)}, bf16[56,2048]{1,0:T(8,128)(2,1)S(1)}, u32[]{:S(2)}, u32[]{:S(2)}) collective-permute-start(bf16[56,2048]{1,0:T(8,128)(2,1)S(1)} %add_convert_fusion.5), channel_id=1, source_target_pairs={{0,4},{5,1},{4,8},{9,5},{8,12},{13,9},{12,14},{15,13},{14,10},{11,... | collective-permute-start | bytes 688136 | tf_op jit(solution)/shard_map/ppermute | solution.py:320
  99.4 5.9 %collective-permute-start.30 = (bf16[32,2048]{1,0:T(8,128)(2,1)S(1)}, bf16[32,2048]{1,0:T(8,128)(2,1)S(1)}, u32[]{:S(2)}, u32[]{:S(2)}) collective-permute-start(bf16[32,2048]{1,0:T(8,128)(2,1)S(1)} %add_convert_fusion.7), channel_id=1, source_target_pairs={{0,4},{5,1},{4,8},{9,5},{8,12},{13,9},{12,14},{15,13},{14,10},{11,... | collective-permute-start | bytes 393224 | tf_op jit(solution)/shard_map/ppermute | solution.py:320

commit v5 on v4

--- a/solution.py
+++ b/solution.py
@@ -249,6 +249,11 @@
     )(*operands)
 
 
+def added_kernel(rows, part_ref, lent_ref, arrived_ref, out_ref):
+    total = part_ref[rows, :] + lent_ref[rows, :].astype(jnp.float32)
+    out_ref[...] = (total + arrived_ref[...].astype(jnp.float32)).astype(jnp.bfloat16)
+
+
 def finished_kernel(first, part_ref, lent_ref, arrived_ref, *refs):
     out_hbm, rows_ref, sem = refs[-3:]
     rows = slice(first, first + arrived_ref.shape[0])
@@ -310,6 +315,16 @@
         part, lent = (x[rows].astype(jnp.float32) for x in parts[step])
         return (part + lent + arrived.astype(jnp.float32)).astype(jnp.bfloat16)
 
+    def added(step, rows, arrived):
+        return pl.pallas_call(
+            functools.partial(added_kernel, rows),
+            out_shape=jax.ShapeDtypeStruct(arrived.shape, jnp.bfloat16),
+            in_specs=[pl.BlockSpec(memory_space=pltpu.VMEM)] * 3,
+            out_specs=pl.BlockSpec(memory_space=pltpu.VMEM),
+            compiler_params=pltpu.CompilerParams(vmem_limit_bytes=SMALL),
+            name="added",
+        )(*parts[step], arrived)
+
     total = jnp.zeros((), jnp.bfloat16)
     for step in range(1, chips - 2):
         total = lax.ppermute(summed(step, slice(None), total), "tok", ring)
@@ -317,7 +332,8 @@
     totals = {name: total[rows] for name, rows in shares.items()}
     for step in range(chips - 2, chips):
         for name, rows in shares.items():
-            totals[name] = lax.ppermute(summed(step, rows, totals[name]), "tok", ring)
+            add = summed if step < chips - 1 else added
+            totals[name] = lax.ppermute(add(step, rows, totals[name]), "tok", ring)
     out = None
     part, lent = parts[0]
     for name, rows in shares.items():
@@ -326,7 +342,7 @@
 
 
 def shares_of(tok_rows):
-    one, two = tok_rows // 16 * 7, tok_rows // 16 * 12
+    one, two = tok_rows // 16 * 6, tok_rows // 16 * 11
     return {"a": slice(0, one), "b": slice(one, two), "c": slice(two, tok_rows)}
 
 

time: 107 us -> 104 us (0.972)
  waiting for transfers between devices: 37.1 us -> 34.8 us
    ppermute x6, waiting for transfers between devices: 5.73 us -> 3.52 us  [circulated(): totals[name] = lax.ppermute(add(step, rows, totals[name]), 'tok', ring)]
  transfers between devices with their start and end apart: 35 -> 35, of which waited for: 12 -> 16; matrix products, arithmetic and copies ran while one was open for 1% -> 1% of each run, Pallas kernels for 28% -> 28%
where the time goes in v5:
time: 104 us
  starting transfers between devices  37.2 us (36%)
  waiting for transfers between devices  34.8 us (33%)
  Pallas kernels  30.4 us (29%)
  other arithmetic  1.17 us (1%)
    pallas_call x9, Pallas kernels, visit(): pl.pallas_call(functools.partial(visit_kernel, count), out_shape=tuple((j...  21.7 us
    ppermute x5, waiting for transfers between devices, circulated(): total = lax.ppermute(summed(step, slice(None), total), 'tok', ring)  17.9 us
    ppermute x24, starting transfers between devices, moved(): return lax.ppermute(value, 'tok', pairs)  16.9 us
    ppermute x24, waiting for transfers between devices, moved(): return lax.ppermute(value, 'tok', pairs)  13.4 us
    ppermute x5, starting transfers between devices, circulated(): total = lax.ppermute(summed(step, slice(None), total), 'tok', ring)  10.6 us
    ppermute x6, starting transfers between devices, circulated(): totals[name] = lax.ppermute(add(step, rows, totals[name]), 'tok', ring)  9.67 us
    pallas_call x2, Pallas kernels, loaded(): pl.pallas_call(functools.partial(loaded_kernel, count), out_shape=tuple((...  4.76 us
    ppermute x6, waiting for transfers between devices, circulated(): totals[name] = lax.ppermute(add(step, rows, totals[name]), 'tok', ring)  3.52 us
  transfers between devices with their start and end apart: 35, of which 16 were waited for; matrix products, arithmetic and copies ran while one was open for 1% of the time, Pallas kernels for 28%

profile of v5, /device:TPU:0, one launch (start us, length us, event | category | flops | bytes accessed | tf_op | source)
XLA Modules:
  0.0 104.1 jit_solution(3676812059050148447)
XLA Ops:
  0.0 3.1 %collective-permute-start.5 = (bf16[128,2048]{1,0:T(8,128)(2,1)}, bf16[128,2048]{1,0:T(8,128)(2,1)S(1)}, u32[]{:S(2)}, u32[]{:S(2)}) collective-permute-start(bf16[128,2048]{1,0:T(8,128)(2,1)} %tokens_hbm.1), channel_id=1, source_target_pairs={{0,4},{5,1},{4,8},{9,5},{8,12},{13,9},{12,14},{15,13},{14,10},{11,... | collective-permute-start | bytes 1572872 | tf_op jit(solution)/shard_map/ppermute | solution.py:291
  3.1 1.3 %packed.1 = (bf16[2080,128]{1,0:T(8,128)(2,1)S(1)}, bf16[32,128]{1,0:T(8,128)(2,1)S(1)}) custom-call(bf16[128,2048]{1,0:T(8,128)(2,1)} %tokens_hbm.1, f32[1,2048]{1,0:T(1,128)} %bitcast.4, s32[8,128]{1,0:T(8,128)} %bitcast.6, f32[8,128]{1,0:T(8,128)} %bitcast.7), custom_call_target="tpu_custom_call" | custom-call | tf_op jit(solution)/shard_map/packed/pallas_call | solution.py:121
  4.4 1.6 %collective-permute-start.6 = (bf16[32,128]{1,0:T(8,128)(2,1)S(1)}, bf16[32,128]{1,0:T(8,128)(2,1)S(1)}, u32[]{:S(2)}, u32[]{:S(2)}) collective-permute-start(bf16[32,128]{1,0:T(8,128)(2,1)S(1)} %get-tuple-element.37), channel_id=1, source_target_pairs={{0,4},{5,1},{4,8},{9,5},{8,12},{13,9},{12,14},{15,13},{14,10},{11,... | collective-permute-start | bytes 24584 | tf_op jit(solution)/shard_map/ppermute | solution.py:291
  6.0 2.9 %loaded.2 = (f32[1,2048]{1,0:T(1,128)S(1)}, s32[1,16]{1,0:T(1,128)S(1)}, bf16[1,2,2048,768]{3,2,1,0:T(8,128)(2,1)S(1)}, bf16[1,2,768]{2,1,0:T(2,128)(2,1)S(1)}) custom-call(f32[1,2048]{1,0:T(1,128)} %bitcast.5, s32[1,16]{1,0:T(1,128)} %bitcast.8, bf16[1,2,2048,768]{3,2,1,0:T(8,128)(2,1)} %refs_2_.1, bf16[1,2,768]{2,1,0:T(2,128)(2,1)} %refs_3_.1), custom_call_target="tpu_custom_call" | custom-call | bytes 6298656 | tf_op jit(solution)/shard_map/loaded/pallas_call | solution.py:171
  8.9 1.6 %collective-permute-done.6.table_ref = bf16[32,128]{1,0:T(8,128)(2,1)S(1)} collective-permute-done((bf16[32,128]{1,0:T(8,128)(2,1)S(1)}, bf16[32,128]{1,0:T(8,128)(2,1)S(1)}, u32[]{:S(2)}, u32[]{:S(2)}) %collective-permute-start.6) | collective-permute-done | bytes 8224 | tf_op jit(solution)/shard_map/ppermute | solution.py:291
  10.5 0.2 mended.1.refs_0_
  10.7 1.9 %loaded.3 = (bf16[1,768,2048]{2,1,0:T(8,128)(2,1)S(1)}, bf16[1,2048]{1,0:T(2,128)(2,1)S(1)}) custom-call(bf16[1,768,2048]{2,1,0:T(8,128)(2,1)} %refs_0_.1, bf16[1,2048]{1,0:T(2,128)(2,1)} %refs_1_.1), custom_call_target="tpu_custom_call" | custom-call | bytes 3149824 | tf_op jit(solution)/shard_map/loaded/pallas_call | solution.py:171
  12.7 2.1 %collective-permute-start.7 = (bf16[2080,128]{1,0:T(8,128)(2,1)S(1)}, bf16[2080,128]{1,0:T(8,128)(2,1)S(1)}, u32[]{:S(2)}, u32[]{:S(2)}) collective-permute-start(bf16[2080,128]{1,0:T(8,128)(2,1)S(1)} %mended.1.refs_0_), channel_id=1, source_target_pairs={{0,4},{5,1},{4,8},{9,5},{8,12},{13,9},{12,14},{15,13},{14,10},{11,... | collective-permute-start | bytes 1597448 | tf_op jit(solution)/shard_map/ppermute | solution.py:291
  14.8 2.7 %visit.17 = (f32[128,2048]{1,0:T(8,128)S(1)}, bf16[128,2048]{1,0:T(8,128)(2,1)S(1)}) custom-call(s32[1,16]{1,0:T(1,128)S(1)} %get-tuple-element.27.owners_ref, bf16[2080,128]{1,0:T(8,128)(2,1)S(1)} %mended.1.refs_0_, bf16[2080,128]{1,0:T(8,128)(2,1)S(1)} %collective-permute-done.22.refs_1_, bf16[1,2,2048,768]{3,2,1,0:T(8,128)(2,1)S(1)} %get-tuple-element.29.refs_2_.refs_1_, ...), custom_call_target="tpu_custom_call" | custom-call | flops 2415919104 | bytes 1572864 | tf_op jit(solution)/shard_map/visit/pallas_call | solution.py:233
  17.5 0.2 collective-permute-start.23
  17.7 4.3 %collective-permute-done.7.refs_0_ = bf16[2080,128]{1,0:T(8,128)(2,1)S(1)} collective-permute-done((bf16[2080,128]{1,0:T(8,128)(2,1)S(1)}, bf16[2080,128]{1,0:T(8,128)(2,1)S(1)}, u32[]{:S(2)}, u32[]{:S(2)}) %collective-permute-start.7) | collective-permute-done | bytes 532512 | tf_op jit(solution)/shard_map/ppermute | solution.py:291
  22.0 2.1 %collective-permute-start.8 = (bf16[2080,128]{1,0:T(8,128)(2,1)S(1)}, bf16[2080,128]{1,0:T(8,128)(2,1)S(1)}, u32[]{:S(2)}, u32[]{:S(2)}) collective-permute-start(bf16[2080,128]{1,0:T(8,128)(2,1)S(1)} %collective-permute-done.7.refs_0_), channel_id=1, source_target_pairs={{0,4},{5,1},{4,8},{9,5},{8,12},{13,9},{12,14},{15,13},{14,10},{11,... | collective-permute-start | bytes 1597448 | tf_op jit(solution)/shard_map/ppermute | solution.py:291
  24.1 0.1 add_convert_fusion.4
  24.2 1.6 %collective-permute-start.24 = (bf16[128,2048]{1,0:T(8,128)(2,1)S(1)}, bf16[128,2048]{1,0:T(8,128)(2,1)S(1)}, u32[]{:S(2)}, u32[]{:S(2)}) collective-permute-start(bf16[128,2048]{1,0:T(8,128)(2,1)S(1)} %add_convert_fusion.4), channel_id=1, source_target_pairs={{0,4},{5,1},{4,8},{9,5},{8,12},{13,9},{12,14},{15,13},{14,10},{11,... | collective-permute-start | bytes 1572872 | tf_op jit(solution)/shard_map/ppermute | solution.py:330
  25.9 2.7 %visit.16 = (f32[128,2048]{1,0:T(8,128)S(1)}, bf16[128,2048]{1,0:T(8,128)(2,1)S(1)}) custom-call(s32[1,16]{1,0:T(1,128)S(1)} %get-tuple-element.27.owners_ref, bf16[2080,128]{1,0:T(8,128)(2,1)S(1)} %collective-permute-done.7.refs_0_, bf16[2080,128]{1,0:T(8,128)(2,1)S(1)} %collective-permute-done.20.refs_1_, ...), custom_call_target="tpu_custom_call" | custom-call | flops 2415919104 | bytes 1572864 | tf_op jit(solution)/shard_map/visit/pallas_call | solution.py:233
  28.5 0.1 collective-permute-start.21
  28.6 2.7 %collective-permute-done.8.refs_0_ = bf16[2080,128]{1,0:T(8,128)(2,1)S(1)} collective-permute-done((bf16[2080,128]{1,0:T(8,128)(2,1)S(1)}, bf16[2080,128]{1,0:T(8,128)(2,1)S(1)}, u32[]{:S(2)}, u32[]{:S(2)}) %collective-permute-start.8) | collective-permute-done | bytes 532512 | tf_op jit(solution)/shard_map/ppermute | solution.py:291
  31.3 2.1 %collective-permute-start.9 = (bf16[2080,128]{1,0:T(8,128)(2,1)S(1)}, bf16[2080,128]{1,0:T(8,128)(2,1)S(1)}, u32[]{:S(2)}, u32[]{:S(2)}) collective-permute-start(bf16[2080,128]{1,0:T(8,128)(2,1)S(1)} %collective-permute-done.8.refs_0_), channel_id=1, source_target_pairs={{0,4},{5,1},{4,8},{9,5},{8,12},{13,9},{12,14},{15,13},{14,10},{11,... | collective-permute-start | bytes 1597448 | tf_op jit(solution)/shard_map/ppermute | solution.py:291
  33.3 3.5 %collective-permute-done.24 = bf16[128,2048]{1,0:T(8,128)(2,1)S(1)} collective-permute-done((bf16[128,2048]{1,0:T(8,128)(2,1)S(1)}, bf16[128,2048]{1,0:T(8,128)(2,1)S(1)}, u32[]{:S(2)}, u32[]{:S(2)}) %collective-permute-start.24) | collective-permute-done | bytes 524320 | tf_op jit(solution)/shard_map/ppermute | solution.py:330
  36.9 0.2 add_convert_fusion.3
  37.1 2.1 %collective-permute-start.25 = (bf16[128,2048]{1,0:T(8,128)(2,1)S(1)}, bf16[128,2048]{1,0:T(8,128)(2,1)S(1)}, u32[]{:S(2)}, u32[]{:S(2)}) collective-permute-start(bf16[128,2048]{1,0:T(8,128)(2,1)S(1)} %add_convert_fusion.3), channel_id=1, source_target_pairs={{0,4},{5,1},{4,8},{9,5},{8,12},{13,9},{12,14},{15,13},{14,10},{11,... | collective-permute-start | bytes 1572872 | tf_op jit(solution)/shard_map/ppermute | solution.py:330
  39.2 2.7 %visit.15 = (f32[128,2048]{1,0:T(8,128)S(1)}, bf16[128,2048]{1,0:T(8,128)(2,1)S(1)}) custom-call(s32[1,16]{1,0:T(1,128)S(1)} %get-tuple-element.27.owners_ref, bf16[2080,128]{1,0:T(8,128)(2,1)S(1)} %collective-permute-done.8.refs_0_, bf16[2080,128]{1,0:T(8,128)(2,1)S(1)} %collective-permute-done.18.refs_1_, ...), custom_call_target="tpu_custom_call" | custom-call | flops 2415919104 | bytes 1572864 | tf_op jit(solution)/shard_map/visit/pallas_call | solution.py:233
  41.9 0.1 collective-permute-start.19
  42.0 0.6 collective-permute-done.9.refs_0_
  42.6 2.1 %collective-permute-start.10 = (bf16[2080,128]{1,0:T(8,128)(2,1)S(1)}, bf16[2080,128]{1,0:T(8,128)(2,1)S(1)}, u32[]{:S(2)}, u32[]{:S(2)}) collective-permute-start(bf16[2080,128]{1,0:T(8,128)(2,1)S(1)} %collective-permute-done.9.refs_0_), channel_id=1, source_target_pairs={{0,4},{5,1},{4,8},{9,5},{8,12},{13,9},{12,14},{15,13},{14,10},{11,... | collective-permute-start | bytes 1597448 | tf_op jit(solution)/shard_map/ppermute | solution.py:291
  44.7 3.5 %collective-permute-done.25 = bf16[128,2048]{1,0:T(8,128)(2,1)S(1)} collective-permute-done((bf16[128,2048]{1,0:T(8,128)(2,1)S(1)}, bf16[128,2048]{1,0:T(8,128)(2,1)S(1)}, u32[]{:S(2)}, u32[]{:S(2)}) %collective-permute-start.25) | collective-permute-done | bytes 524320 | tf_op jit(solution)/shard_map/ppermute | solution.py:330
  48.2 0.2 add_convert_fusion.2
  48.4 2.1 %collective-permute-start.26 = (bf16[128,2048]{1,0:T(8,128)(2,1)S(1)}, bf16[128,2048]{1,0:T(8,128)(2,1)S(1)}, u32[]{:S(2)}, u32[]{:S(2)}) collective-permute-start(bf16[128,2048]{1,0:T(8,128)(2,1)S(1)} %add_convert_fusion.2), channel_id=1, source_target_pairs={{0,4},{5,1},{4,8},{9,5},{8,12},{13,9},{12,14},{15,13},{14,10},{11,... | collective-permute-start | bytes 1572872 | tf_op jit(solution)/shard_map/ppermute | solution.py:330
  50.6 2.7 %visit.14 = (f32[128,2048]{1,0:T(8,128)S(1)}, bf16[128,2048]{1,0:T(8,128)(2,1)S(1)}) custom-call(s32[1,16]{1,0:T(1,128)S(1)} %get-tuple-element.27.owners_ref, bf16[2080,128]{1,0:T(8,128)(2,1)S(1)} %collective-permute-done.9.refs_0_, bf16[2080,128]{1,0:T(8,128)(2,1)S(1)} %collective-permute-done.16.refs_1_, ...), custom_call_target="tpu_custom_call" | custom-call | flops 2415919104 | bytes 1572864 | tf_op jit(solution)/shard_map/visit/pallas_call | solution.py:233
  53.2 0.1 collective-permute-start.17
  53.3 0.6 collective-permute-done.10.refs_0_
  53.9 2.0 %collective-permute-start.2 = (bf16[2080,128]{1,0:T(8,128)(2,1)S(1)}, bf16[2080,128]{1,0:T(8,128)(2,1)S(1)}, u32[]{:S(2)}, u32[]{:S(2)}) collective-permute-start(bf16[2080,128]{1,0:T(8,128)(2,1)S(1)} %get-tuple-element.28.refs_0_), channel_id=1, source_target_pairs={{4,0},{1,5},{8,4},{5,9},{12,8},{9,13},{14,12},{13,15},{10,14},{15,... | collective-permute-start | bytes 1597448 | tf_op jit(solution)/shard_map/ppermute | solution.py:291
  56.0 5.8 %collective-permute-done.26 = bf16[128,2048]{1,0:T(8,128)(2,1)S(1)} collective-permute-done((bf16[128,2048]{1,0:T(8,128)(2,1)S(1)}, bf16[128,2048]{1,0:T(8,128)(2,1)S(1)}, u32[]{:S(2)}, u32[]{:S(2)}) %collective-permute-start.26) | collective-permute-done | bytes 524320 | tf_op jit(solution)/shard_map/ppermute | solution.py:330
  61.8 0.2 add_convert_fusion.1
  62.0 2.6 %collective-permute-start.27 = (bf16[128,2048]{1,0:T(8,128)(2,1)S(1)}, bf16[128,2048]{1,0:T(8,128)(2,1)S(1)}, u32[]{:S(2)}, u32[]{:S(2)}) collective-permute-start(bf16[128,2048]{1,0:T(8,128)(2,1)S(1)} %add_convert_fusion.1), channel_id=1, source_target_pairs={{0,4},{5,1},{4,8},{9,5},{8,12},{13,9},{12,14},{15,13},{14,10},{11,... | collective-permute-start | bytes 1572872 | tf_op jit(solution)/shard_map/ppermute | solution.py:330
  64.6 2.7 %visit.13 = (f32[128,2048]{1,0:T(8,128)S(1)}, bf16[128,2048]{1,0:T(8,128)(2,1)S(1)}) custom-call(s32[1,16]{1,0:T(1,128)S(1)} %get-tuple-element.27.owners_ref, bf16[2080,128]{1,0:T(8,128)(2,1)S(1)} %collective-permute-done.10.refs_0_, bf16[2080,128]{1,0:T(8,128)(2,1)S(1)} %collective-permute-done.14.refs_1_, ...), custom_call_target="tpu_custom_call" | custom-call | flops 2415919104 | bytes 1572864 | tf_op jit(solution)/shard_map/visit/pallas_call | solution.py:233
  67.3 0.1 collective-permute-start.15
  67.3 3.6 %collective-permute-done.11.refs_0_ = bf16[2080,128]{1,0:T(8,128)(2,1)S(1)} collective-permute-done((bf16[2080,128]{1,0:T(8,128)(2,1)S(1)}, bf16[2080,128]{1,0:T(8,128)(2,1)S(1)}, u32[]{:S(2)}, u32[]{:S(2)}) %collective-permute-start.11) | collective-permute-done | bytes 532512 | tf_op jit(solution)/shard_map/ppermute | solution.py:291
  70.9 0.5 collective-permute-start
  71.5 5.1 %collective-permute-done.27 = bf16[128,2048]{1,0:T(8,128)(2,1)S(1)} collective-permute-done((bf16[128,2048]{1,0:T(8,128)(2,1)S(1)}, bf16[128,2048]{1,0:T(8,128)(2,1)S(1)}, u32[]{:S(2)}, u32[]{:S(2)}) %collective-permute-start.27) | collective-permute-done | bytes 524320 | tf_op jit(solution)/shard_map/ppermute | solution.py:330
  76.6 0.2 add_convert_fusion
  76.8 2.1 %collective-permute-start.28 = (bf16[128,2048]{1,0:T(8,128)(2,1)S(1)}, bf16[128,2048]{1,0:T(8,128)(2,1)S(1)}, u32[]{:S(2)}, u32[]{:S(2)}) collective-permute-start(bf16[128,2048]{1,0:T(8,128)(2,1)S(1)} %add_convert_fusion), channel_id=1, source_target_pairs={{0,4},{5,1},{4,8},{9,5},{8,12},{13,9},{12,14},{15,13},{14,10},{11,... | collective-permute-start | bytes 1572872 | tf_op jit(solution)/shard_map/ppermute | solution.py:330
  78.9 1.5 %visit.12 = bf16[128,2048]{1,0:T(8,128)(2,1)S(1)} custom-call(s32[1,16]{1,0:T(1,128)S(1)} %get-tuple-element.27.owners_ref, bf16[2080,128]{1,0:T(8,128)(2,1)S(1)} %collective-permute-done.12.refs_0_, bf16[1,2,2048,768]{3,2,1,0:T(8,128)(2,1)S(1)} %get-tuple-element.29.refs_2_.refs_1_, bf16[1,2,768]{2,1,0:T(2,128)(2,1)S(1)} %get-tuple-element.30.refs_3_.refs_2_, ...), custom_call_target="tpu_custom_call" | custom-call | flops 1207959552 | bytes 786432 | tf_op jit(solution)/shard_map/visit/pallas_call | solution.py:233
  80.5 2.7 %visit.9 = (f32[128,2048]{1,0:T(8,128)S(1)}, bf16[128,2048]{1,0:T(8,128)(2,1)S(1)}) custom-call(s32[1,16]{1,0:T(1,128)S(1)} %get-tuple-element.27.owners_ref, bf16[2080,128]{1,0:T(8,128)(2,1)S(1)} %get-tuple-element.28.refs_0_, bf16[2080,128]{1,0:T(8,128)(2,1)S(1)} %collective-permute-done.refs_1_, ...), custom_call_target="tpu_custom_call" | custom-call | flops 2415919104 | bytes 1572864 | tf_op jit(solution)/shard_map/visit/pallas_call | solution.py:233
  83.2 0.6 collective-permute-start.1
  83.7 2.7 %visit.10 = (f32[128,2048]{1,0:T(8,128)S(1)}, bf16[128,2048]{1,0:T(8,128)(2,1)S(1)}) custom-call(s32[1,16]{1,0:T(1,128)S(1)} %get-tuple-element.27.owners_ref, bf16[2080,128]{1,0:T(8,128)(2,1)S(1)} %collective-permute-done.2.refs_0_, bf16[2080,128]{1,0:T(8,128)(2,1)S(1)} %collective-permute-done.3.refs_1_, ...), custom_call_target="tpu_custom_call" | custom-call | flops 2415919104 | bytes 1572864 | tf_op jit(solution)/shard_map/visit/pallas_call | solution.py:233
  86.4 0.1 collective-permute-start.4
  86.5 1.5 %visit.11 = f32[128,2048]{1,0:T(8,128)S(1)} custom-call(s32[1,16]{1,0:T(1,128)S(1)} %get-tuple-element.27.owners_ref, bf16[2080,128]{1,0:T(8,128)(2,1)S(1)} %collective-permute-done.11.refs_0_, bf16[1,2,2048,768]{3,2,1,0:T(8,128)(2,1)S(1)} %get-tuple-element.29.refs_2_.refs_1_, bf16[1,2,768]{2,1,0:T(2,128)(2,1)S(1)} %get-tuple-element.30.refs_3_.refs_2_, ...), custom_call_target="tpu_custom_call" | custom-call | flops 1207959552 | bytes 786432 | tf_op jit(solution)/shard_map/visit/pallas_call | solution.py:233
  88.0 0.1 fusion.1
  88.1 1.6 %collective-permute-start.33 = (bf16[48,2048]{1,0:T(8,128)(2,1)S(1)}, bf16[48,2048]{1,0:T(8,128)(2,1)S(1)}, u32[]{:S(2)}, u32[]{:S(2)}) collective-permute-start(bf16[48,2048]{1,0:T(8,128)(2,1)S(1)} %fusion.1), channel_id=1, source_target_pairs={{0,4},{5,1},{4,8},{9,5},{8,12},{13,9},{12,14},{15,13},{14,10},{11,... | collective-permute-start | bytes 589832 | tf_op jit(solution)/shard_map/ppermute | solution.py:336
  89.8 0.1 fusion.3
  89.9 1.6 %collective-permute-start.31 = (bf16[40,2048]{1,0:T(8,128)(2,1)S(1)}, bf16[40,2048]{1,0:T(8,128)(2,1)S(1)}, u32[]{:S(2)}, u32[]{:S(2)}) collective-permute-start(bf16[40,2048]{1,0:T(8,128)(2,1)S(1)} %get-tuple-element.49), channel_id=1, source_target_pairs={{0,4},{5,1},{4,8},{9,5},{8,12},{13,9},{12,14},{15,13},{14,10},{11,... | collective-permute-start | bytes 491528 | tf_op jit(solution)/shard_map/ppermute | solution.py:336
  91.5 1.5 %collective-permute-start.29 = (bf16[40,2048]{1,0:T(8,128)(2,1)S(1)}, bf16[40,2048]{1,0:T(8,128)(2,1)S(1)}, u32[]{:S(2)}, u32[]{:S(2)}) collective-permute-start(bf16[40,2048]{1,0:T(8,128)(2,1)S(1)} %get-tuple-element.50), channel_id=1, source_target_pairs={{0,4},{5,1},{4,8},{9,5},{8,12},{13,9},{12,14},{15,13},{14,10},{11,... | collective-permute-start | bytes 491528 | tf_op jit(solution)/shard_map/ppermute | solution.py:336
  93.0 0.8 collective-permute-done.33.arrived_ref
  93.9 0.1 added.5
  93.9 1.6 %collective-permute-start.34 = (bf16[48,2048]{1,0:T(8,128)(2,1)S(1)}, bf16[48,2048]{1,0:T(8,128)(2,1)S(1)}, u32[]{:S(2)}, u32[]{:S(2)}) collective-permute-start(bf16[48,2048]{1,0:T(8,128)(2,1)S(1)} %added.5), channel_id=1, source_target_pairs={{0,4},{5,1},{4,8},{9,5},{8,12},{13,9},{12,14},{15,13},{14,10},{11,... | collective-permute-start | bytes 589832 | tf_op jit(solution)/shard_map/ppermute | solution.py:336
  95.7 1.6 %collective-permute-start.32 = (bf16[40,2048]{1,0:T(8,128)(2,1)S(1)}, bf16[40,2048]{1,0:T(8,128)(2,1)S(1)}, u32[]{:S(2)}, u32[]{:S(2)}) collective-permute-start(bf16[40,2048]{1,0:T(8,128)(2,1)S(1)} %added.4), channel_id=1, source_target_pairs={{0,4},{5,1},{4,8},{9,5},{8,12},{13,9},{12,14},{15,13},{14,10},{11,... | collective-permute-start | bytes 491528 | tf_op jit(solution)/shard_map/ppermute | solution.py:336
  97.4 1.6 %collective-permute-start.30 = (bf16[40,2048]{1,0:T(8,128)(2,1)S(1)}, bf16[40,2048]{1,0:T(8,128)(2,1)S(1)}, u32[]{:S(2)}, u32[]{:S(2)}) collective-permute-start(bf16[40,2048]{1,0:T(8,128)(2,1)S(1)} %added.3), channel_id=1, source_target_pairs={{0,4},{5,1},{4,8},{9,5},{8,12},{13,9},{12,14},{15,13},{14,10},{11,... | collective-permute-start | bytes 491528 | tf_op jit(solution)/shard_map/ppermute | solution.py:336
  99.1 0.6 collective-permute-done.34.arrived_ref
  99.6 0.8 finished.3.refs_0_
  100.4 1.0 collective-permute-done.32.arrived_ref
  101.4 0.7 finished.4.refs_0_
  102.1 1.0 collective-permute-done.30.arrived_ref
  103.2 0.7 finished.5
  (32 shorter events, 0.5 us)
Async XLA Ops:
  0.0 10.5 %collective-permute-start.5 = (bf16[128,2048]{1,0:T(8,128)(2,1)}, bf16[128,2048]{1,0:T(8,128)(2,1)S(1)}, u32[]{:S(2)}, u32[]{:S(2)}) collective-permute-start(bf16[128,2048]{1,0:T(8,128)(2,1)} %tokens_hbm.1), channel_id=1, source_target_pairs={{0,4},{5,1},{4,8},{9,5},{8,12},{13,9},{12,14},{15,13},{14,10},{11,... | collective-permute-start | bytes 1572872 | tf_op jit(solution)/shard_map/ppermute | solution.py:291
  4.4 6.1 %collective-permute-start.6 = (bf16[32,128]{1,0:T(8,128)(2,1)S(1)}, bf16[32,128]{1,0:T(8,128)(2,1)S(1)}, u32[]{:S(2)}, u32[]{:S(2)}) collective-permute-start(bf16[32,128]{1,0:T(8,128)(2,1)S(1)} %get-tuple-element.37), channel_id=1, source_target_pairs={{0,4},{5,1},{4,8},{9,5},{8,12},{13,9},{12,14},{15,13},{14,10},{11,... | collective-permute-start | bytes 24584 | tf_op jit(solution)/shard_map/ppermute | solution.py:291
  10.7 4.1 %collective-permute-start.22 = (bf16[2080,128]{1,0:T(8,128)(2,1)S(1)}, bf16[2080,128]{1,0:T(8,128)(2,1)S(1)}, u32[]{:S(2)}, u32[]{:S(2)}) collective-permute-start(bf16[2080,128]{1,0:T(8,128)(2,1)S(1)} %mended.1.refs_0_), channel_id=1, source_target_pairs={{0,1},{1,0},{2,3},{3,2},{4,5},{5,4},{6,7},{7,6},{8,9},{9,8},{10,11... | collective-permute-start | bytes 1597448 | tf_op jit(solution)/shard_map/ppermute | solution.py:291
  12.7 9.3 %collective-permute-start.7 = (bf16[2080,128]{1,0:T(8,128)(2,1)S(1)}, bf16[2080,128]{1,0:T(8,128)(2,1)S(1)}, u32[]{:S(2)}, u32[]{:S(2)}) collective-permute-start(bf16[2080,128]{1,0:T(8,128)(2,1)S(1)} %mended.1.refs_0_), channel_id=1, source_target_pairs={{0,4},{5,1},{4,8},{9,5},{8,12},{13,9},{12,14},{15,13},{14,10},{11,... | collective-permute-start | bytes 1597448 | tf_op jit(solution)/shard_map/ppermute | solution.py:291
  17.5 6.6 %collective-permute-start.23 = (bf16[128,2048]{1,0:T(8,128)(2,1)S(1)}, bf16[128,2048]{1,0:T(8,128)(2,1)S(1)}, u32[]{:S(2)}, u32[]{:S(2)}) collective-permute-start(bf16[128,2048]{1,0:T(8,128)(2,1)S(1)} %get-tuple-element.48), channel_id=1, source_target_pairs={{0,1},{1,0},{2,3},{3,2},{4,5},{5,4},{6,7},{7,6},{8,9},{9,8},{10,11... | collective-permute-start | bytes 1572872 | tf_op jit(solution)/shard_map/ppermute | solution.py:291
  22.0 3.9 %collective-permute-start.20 = (bf16[2080,128]{1,0:T(8,128)(2,1)S(1)}, bf16[2080,128]{1,0:T(8,128)(2,1)S(1)}, u32[]{:S(2)}, u32[]{:S(2)}) collective-permute-start(bf16[2080,128]{1,0:T(8,128)(2,1)S(1)} %collective-permute-done.7.refs_0_), channel_id=1, source_target_pairs={{0,1},{1,0},{2,3},{3,2},{4,5},{5,4},{6,7},{7,6},{8,9},{9,8},{10,11... | collective-permute-start | bytes 1597448 | tf_op jit(solution)/shard_map/ppermute | solution.py:291
  22.0 9.3 %collective-permute-start.8 = (bf16[2080,128]{1,0:T(8,128)(2,1)S(1)}, bf16[2080,128]{1,0:T(8,128)(2,1)S(1)}, u32[]{:S(2)}, u32[]{:S(2)}) collective-permute-start(bf16[2080,128]{1,0:T(8,128)(2,1)S(1)} %collective-permute-done.7.refs_0_), channel_id=1, source_target_pairs={{0,4},{5,1},{4,8},{9,5},{8,12},{13,9},{12,14},{15,13},{14,10},{11,... | collective-permute-start | bytes 1597448 | tf_op jit(solution)/shard_map/ppermute | solution.py:291
  24.2 12.7 %collective-permute-start.24 = (bf16[128,2048]{1,0:T(8,128)(2,1)S(1)}, bf16[128,2048]{1,0:T(8,128)(2,1)S(1)}, u32[]{:S(2)}, u32[]{:S(2)}) collective-permute-start(bf16[128,2048]{1,0:T(8,128)(2,1)S(1)} %add_convert_fusion.4), channel_id=1, source_target_pairs={{0,4},{5,1},{4,8},{9,5},{8,12},{13,9},{12,14},{15,13},{14,10},{11,... | collective-permute-start | bytes 1572872 | tf_op jit(solution)/shard_map/ppermute | solution.py:330
  28.5 8.4 %collective-permute-start.21 = (bf16[128,2048]{1,0:T(8,128)(2,1)S(1)}, bf16[128,2048]{1,0:T(8,128)(2,1)S(1)}, u32[]{:S(2)}, u32[]{:S(2)}) collective-permute-start(bf16[128,2048]{1,0:T(8,128)(2,1)S(1)} %get-tuple-element.46), channel_id=1, source_target_pairs={{0,1},{1,0},{2,3},{3,2},{4,5},{5,4},{6,7},{7,6},{8,9},{9,8},{10,11... | collective-permute-start | bytes 1572872 | tf_op jit(solution)/shard_map/ppermute | solution.py:291
  31.3 8.0 %collective-permute-start.18 = (bf16[2080,128]{1,0:T(8,128)(2,1)S(1)}, bf16[2080,128]{1,0:T(8,128)(2,1)S(1)}, u32[]{:S(2)}, u32[]{:S(2)}) collective-permute-start(bf16[2080,128]{1,0:T(8,128)(2,1)S(1)} %collective-permute-done.8.refs_0_), channel_id=1, source_target_pairs={{0,1},{1,0},{2,3},{3,2},{4,5},{5,4},{6,7},{7,6},{8,9},{9,8},{10,11... | collective-permute-start | bytes 1597448 | tf_op jit(solution)/shard_map/ppermute | solution.py:291
  31.3 11.3 %collective-permute-start.9 = (bf16[2080,128]{1,0:T(8,128)(2,1)S(1)}, bf16[2080,128]{1,0:T(8,128)(2,1)S(1)}, u32[]{:S(2)}, u32[]{:S(2)}) collective-permute-start(bf16[2080,128]{1,0:T(8,128)(2,1)S(1)} %collective-permute-done.8.refs_0_), channel_id=1, source_target_pairs={{0,4},{5,1},{4,8},{9,5},{8,12},{13,9},{12,14},{15,13},{14,10},{11,... | collective-permute-start | bytes 1597448 | tf_op jit(solution)/shard_map/ppermute | solution.py:291
  37.1 11.1 %collective-permute-start.25 = (bf16[128,2048]{1,0:T(8,128)(2,1)S(1)}, bf16[128,2048]{1,0:T(8,128)(2,1)S(1)}, u32[]{:S(2)}, u32[]{:S(2)}) collective-permute-start(bf16[128,2048]{1,0:T(8,128)(2,1)S(1)} %add_convert_fusion.3), channel_id=1, source_target_pairs={{0,4},{5,1},{4,8},{9,5},{8,12},{13,9},{12,14},{15,13},{14,10},{11,... | collective-permute-start | bytes 1572872 | tf_op jit(solution)/shard_map/ppermute | solution.py:330
  41.9 6.3 %collective-permute-start.19 = (bf16[128,2048]{1,0:T(8,128)(2,1)S(1)}, bf16[128,2048]{1,0:T(8,128)(2,1)S(1)}, u32[]{:S(2)}, u32[]{:S(2)}) collective-permute-start(bf16[128,2048]{1,0:T(8,128)(2,1)S(1)} %get-tuple-element.44), channel_id=1, source_target_pairs={{0,1},{1,0},{2,3},{3,2},{4,5},{5,4},{6,7},{7,6},{8,9},{9,8},{10,11... | collective-permute-start | bytes 1572872 | tf_op jit(solution)/shard_map/ppermute | solution.py:291
  42.6 8.0 %collective-permute-start.16 = (bf16[2080,128]{1,0:T(8,128)(2,1)S(1)}, bf16[2080,128]{1,0:T(8,128)(2,1)S(1)}, u32[]{:S(2)}, u32[]{:S(2)}) collective-permute-start(bf16[2080,128]{1,0:T(8,128)(2,1)S(1)} %collective-permute-done.9.refs_0_), channel_id=1, source_target_pairs={{0,1},{1,0},{2,3},{3,2},{4,5},{5,4},{6,7},{7,6},{8,9},{9,8},{10,11... | collective-permute-start | bytes 1597448 | tf_op jit(solution)/shard_map/ppermute | solution.py:291
  42.6 11.3 %collective-permute-start.10 = (bf16[2080,128]{1,0:T(8,128)(2,1)S(1)}, bf16[2080,128]{1,0:T(8,128)(2,1)S(1)}, u32[]{:S(2)}, u32[]{:S(2)}) collective-permute-start(bf16[2080,128]{1,0:T(8,128)(2,1)S(1)} %collective-permute-done.9.refs_0_), channel_id=1, source_target_pairs={{0,4},{5,1},{4,8},{9,5},{8,12},{13,9},{12,14},{15,13},{14,10},{11,... | collective-permute-start | bytes 1597448 | tf_op jit(solution)/shard_map/ppermute | solution.py:291
  48.4 13.3 %collective-permute-start.26 = (bf16[128,2048]{1,0:T(8,128)(2,1)S(1)}, bf16[128,2048]{1,0:T(8,128)(2,1)S(1)}, u32[]{:S(2)}, u32[]{:S(2)}) collective-permute-start(bf16[128,2048]{1,0:T(8,128)(2,1)S(1)} %add_convert_fusion.2), channel_id=1, source_target_pairs={{0,4},{5,1},{4,8},{9,5},{8,12},{13,9},{12,14},{15,13},{14,10},{11,... | collective-permute-start | bytes 1572872 | tf_op jit(solution)/shard_map/ppermute | solution.py:330
  53.2 8.5 %collective-permute-start.17 = (bf16[128,2048]{1,0:T(8,128)(2,1)S(1)}, bf16[128,2048]{1,0:T(8,128)(2,1)S(1)}, u32[]{:S(2)}, u32[]{:S(2)}) collective-permute-start(bf16[128,2048]{1,0:T(8,128)(2,1)S(1)} %get-tuple-element.42), channel_id=1, source_target_pairs={{0,1},{1,0},{2,3},{3,2},{4,5},{5,4},{6,7},{7,6},{8,9},{9,8},{10,11... | collective-permute-start | bytes 1572872 | tf_op jit(solution)/shard_map/ppermute | solution.py:291
  53.9 10.7 %collective-permute-start.14 = (bf16[2080,128]{1,0:T(8,128)(2,1)S(1)}, bf16[2080,128]{1,0:T(8,128)(2,1)S(1)}, u32[]{:S(2)}, u32[]{:S(2)}) collective-permute-start(bf16[2080,128]{1,0:T(8,128)(2,1)S(1)} %collective-permute-done.10.refs_0_), channel_id=1, source_target_pairs={{0,1},{1,0},{2,3},{3,2},{4,5},{5,4},{6,7},{7,6},{8,9},{9,8},{10,11... | collective-permute-start | bytes 1597448 | tf_op jit(solution)/shard_map/ppermute | solution.py:291
  53.9 17.5 %collective-permute-start.2 = (bf16[2080,128]{1,0:T(8,128)(2,1)S(1)}, bf16[2080,128]{1,0:T(8,128)(2,1)S(1)}, u32[]{:S(2)}, u32[]{:S(2)}) collective-permute-start(bf16[2080,128]{1,0:T(8,128)(2,1)S(1)} %get-tuple-element.28.refs_0_), channel_id=1, source_target_pairs={{4,0},{1,5},{8,4},{5,9},{12,8},{9,13},{14,12},{13,15},{10,14},{15,... | collective-permute-start | bytes 1597448 | tf_op jit(solution)/shard_map/ppermute | solution.py:291
  55.9 15.0 %collective-permute-start.11 = (bf16[2080,128]{1,0:T(8,128)(2,1)S(1)}, bf16[2080,128]{1,0:T(8,128)(2,1)S(1)}, u32[]{:S(2)}, u32[]{:S(2)}) collective-permute-start(bf16[2080,128]{1,0:T(8,128)(2,1)S(1)} %collective-permute-done.10.refs_0_), channel_id=1, source_target_pairs={{0,4},{5,1},{4,8},{9,5},{8,12},{13,9},{12,14},{15,13},{14,10},{11,... | collective-permute-start | bytes 1597448 | tf_op jit(solution)/shard_map/ppermute | solution.py:291
  62.0 14.6 %collective-permute-start.27 = (bf16[128,2048]{1,0:T(8,128)(2,1)S(1)}, bf16[128,2048]{1,0:T(8,128)(2,1)S(1)}, u32[]{:S(2)}, u32[]{:S(2)}) collective-permute-start(bf16[128,2048]{1,0:T(8,128)(2,1)S(1)} %add_convert_fusion.1), channel_id=1, source_target_pairs={{0,4},{5,1},{4,8},{9,5},{8,12},{13,9},{12,14},{15,13},{14,10},{11,... | collective-permute-start | bytes 1572872 | tf_op jit(solution)/shard_map/ppermute | solution.py:330
  67.3 9.3 %collective-permute-start.15 = (bf16[128,2048]{1,0:T(8,128)(2,1)S(1)}, bf16[128,2048]{1,0:T(8,128)(2,1)S(1)}, u32[]{:S(2)}, u32[]{:S(2)}) collective-permute-start(bf16[128,2048]{1,0:T(8,128)(2,1)S(1)} %get-tuple-element.40), channel_id=1, source_target_pairs={{0,1},{1,0},{2,3},{3,2},{4,5},{5,4},{6,7},{7,6},{8,9},{9,8},{10,11... | collective-permute-start | bytes 1572872 | tf_op jit(solution)/shard_map/ppermute | solution.py:291
  70.9 8.0 %collective-permute-start.12 = (bf16[2080,128]{1,0:T(8,128)(2,1)S(1)}, bf16[2080,128]{1,0:T(8,128)(2,1)S(1)}, u32[]{:S(2)}, u32[]{:S(2)}) collective-permute-start(bf16[2080,128]{1,0:T(8,128)(2,1)S(1)} %collective-permute-done.11.refs_0_), channel_id=1, source_target_pairs={{0,1},{1,0},{2,3},{3,2},{4,5},{5,4},{6,7},{7,6},{8,9},{9,8},{10,11... | collective-permute-start | bytes 1597448 | tf_op jit(solution)/shard_map/ppermute | solution.py:291
  70.9 9.6 %collective-permute-start = (bf16[2080,128]{1,0:T(8,128)(2,1)S(1)}, bf16[2080,128]{1,0:T(8,128)(2,1)S(1)}, u32[]{:S(2)}, u32[]{:S(2)}) collective-permute-start(bf16[2080,128]{1,0:T(8,128)(2,1)S(1)} %get-tuple-element.28.refs_0_), channel_id=1, source_target_pairs={{0,1},{1,0},{2,3},{3,2},{4,5},{5,4},{6,7},{7,6},{8,9},{9,8},{10,11... | collective-permute-start | bytes 1597448 | tf_op jit(solution)/shard_map/ppermute | solution.py:291
  71.5 12.3 %collective-permute-start.3 = (bf16[2080,128]{1,0:T(8,128)(2,1)S(1)}, bf16[2080,128]{1,0:T(8,128)(2,1)S(1)}, u32[]{:S(2)}, u32[]{:S(2)}) collective-permute-start(bf16[2080,128]{1,0:T(8,128)(2,1)S(1)} %collective-permute-done.2.refs_0_), channel_id=1, source_target_pairs={{0,1},{1,0},{2,3},{3,2},{4,5},{5,4},{6,7},{7,6},{8,9},{9,8},{10,11... | collective-permute-start | bytes 1597448 | tf_op jit(solution)/shard_map/ppermute | solution.py:291
  76.8 11.3 %collective-permute-start.28 = (bf16[128,2048]{1,0:T(8,128)(2,1)S(1)}, bf16[128,2048]{1,0:T(8,128)(2,1)S(1)}, u32[]{:S(2)}, u32[]{:S(2)}) collective-permute-start(bf16[128,2048]{1,0:T(8,128)(2,1)S(1)} %add_convert_fusion), channel_id=1, source_target_pairs={{0,4},{5,1},{4,8},{9,5},{8,12},{13,9},{12,14},{15,13},{14,10},{11,... | collective-permute-start | bytes 1572872 | tf_op jit(solution)/shard_map/ppermute | solution.py:330
  80.4 7.6 %collective-permute-start.13 = (bf16[128,2048]{1,0:T(8,128)(2,1)S(1)}, bf16[128,2048]{1,0:T(8,128)(2,1)S(1)}, u32[]{:S(2)}, u32[]{:S(2)}) collective-permute-start(bf16[128,2048]{1,0:T(8,128)(2,1)S(1)} %visit.12), channel_id=1, source_target_pairs={{0,1},{1,0},{2,3},{3,2},{4,5},{5,4},{6,7},{7,6},{8,9},{9,8},{10,11... | collective-permute-start | bytes 1572872 | tf_op jit(solution)/shard_map/ppermute | solution.py:291
  83.2 15.9 %collective-permute-start.1 = (bf16[128,2048]{1,0:T(8,128)(2,1)S(1)}, bf16[128,2048]{1,0:T(8,128)(2,1)S(1)}, u32[]{:S(2)}, u32[]{:S(2)}) collective-permute-start(bf16[128,2048]{1,0:T(8,128)(2,1)S(1)} %get-tuple-element.34), channel_id=1, source_target_pairs={{0,1},{1,0},{2,3},{3,2},{4,5},{5,4},{6,7},{7,6},{8,9},{9,8},{10,11... | collective-permute-start | bytes 1572872 | tf_op jit(solution)/shard_map/ppermute | solution.py:291
  86.4 6.6 %collective-permute-start.4 = (bf16[128,2048]{1,0:T(8,128)(2,1)S(1)}, bf16[128,2048]{1,0:T(8,128)(2,1)S(1)}, u32[]{:S(2)}, u32[]{:S(2)}) collective-permute-start(bf16[128,2048]{1,0:T(8,128)(2,1)S(1)} %get-tuple-element.36), channel_id=1, source_target_pairs={{0,1},{1,0},{2,3},{3,2},{4,5},{5,4},{6,7},{7,6},{8,9},{9,8},{10,11... | collective-permute-start | bytes 1572872 | tf_op jit(solution)/shard_map/ppermute | solution.py:291
  88.1 5.7 %collective-permute-start.33 = (bf16[48,2048]{1,0:T(8,128)(2,1)S(1)}, bf16[48,2048]{1,0:T(8,128)(2,1)S(1)}, u32[]{:S(2)}, u32[]{:S(2)}) collective-permute-start(bf16[48,2048]{1,0:T(8,128)(2,1)S(1)} %fusion.1), channel_id=1, source_target_pairs={{0,4},{5,1},{4,8},{9,5},{8,12},{13,9},{12,14},{15,13},{14,10},{11,... | collective-permute-start | bytes 589832 | tf_op jit(solution)/shard_map/ppermute | solution.py:336
  89.9 5.7 %collective-permute-start.31 = (bf16[40,2048]{1,0:T(8,128)(2,1)S(1)}, bf16[40,2048]{1,0:T(8,128)(2,1)S(1)}, u32[]{:S(2)}, u32[]{:S(2)}) collective-permute-start(bf16[40,2048]{1,0:T(8,128)(2,1)S(1)} %get-tuple-element.49), channel_id=1, source_target_pairs={{0,4},{5,1},{4,8},{9,5},{8,12},{13,9},{12,14},{15,13},{14,10},{11,... | collective-permute-start | bytes 491528 | tf_op jit(solution)/shard_map/ppermute | solution.py:336
  91.5 5.8 %collective-permute-start.29 = (bf16[40,2048]{1,0:T(8,128)(2,1)S(1)}, bf16[40,2048]{1,0:T(8,128)(2,1)S(1)}, u32[]{:S(2)}, u32[]{:S(2)}) collective-permute-start(bf16[40,2048]{1,0:T(8,128)(2,1)S(1)} %get-tuple-element.50), channel_id=1, source_target_pairs={{0,4},{5,1},{4,8},{9,5},{8,12},{13,9},{12,14},{15,13},{14,10},{11,... | collective-permute-start | bytes 491528 | tf_op jit(solution)/shard_map/ppermute | solution.py:336
  93.9 5.7 %collective-permute-start.34 = (bf16[48,2048]{1,0:T(8,128)(2,1)S(1)}, bf16[48,2048]{1,0:T(8,128)(2,1)S(1)}, u32[]{:S(2)}, u32[]{:S(2)}) collective-permute-start(bf16[48,2048]{1,0:T(8,128)(2,1)S(1)} %added.5), channel_id=1, source_target_pairs={{0,4},{5,1},{4,8},{9,5},{8,12},{13,9},{12,14},{15,13},{14,10},{11,... | collective-permute-start | bytes 589832 | tf_op jit(solution)/shard_map/ppermute | solution.py:336
  95.7 5.7 %collective-permute-start.32 = (bf16[40,2048]{1,0:T(8,128)(2,1)S(1)}, bf16[40,2048]{1,0:T(8,128)(2,1)S(1)}, u32[]{:S(2)}, u32[]{:S(2)}) collective-permute-start(bf16[40,2048]{1,0:T(8,128)(2,1)S(1)} %added.4), channel_id=1, source_target_pairs={{0,4},{5,1},{4,8},{9,5},{8,12},{13,9},{12,14},{15,13},{14,10},{11,... | collective-permute-start | bytes 491528 | tf_op jit(solution)/shard_map/ppermute | solution.py:336
  97.4 5.7 %collective-permute-start.30 = (bf16[40,2048]{1,0:T(8,128)(2,1)S(1)}, bf16[40,2048]{1,0:T(8,128)(2,1)S(1)}, u32[]{:S(2)}, u32[]{:S(2)}) collective-permute-start(bf16[40,2048]{1,0:T(8,128)(2,1)S(1)} %added.3), channel_id=1, source_target_pairs={{0,4},{5,1},{4,8},{9,5},{8,12},{13,9},{12,14},{15,13},{14,10},{11,... | collective-permute-start | bytes 491528 | tf_op jit(solution)/shard_map/ppermute | solution.py:336
